TPU v7x, 32 devices: a whole 2x2x4 slice. The times are simulated.
32 devices in a mesh: sec: 4 (over x, core), lat: 2 (over y), col: 4 (over z).
Axes of the slice: x: 2, y: 2, z: 4, core: 2. Of those that a mesh axis runs over, the one named last changes fastest.
Arguments:
- state: float32 [1, 4, 28, 192, 384], P(None, 'sec', None, 'lat', 'col'), may hold values from -6 to 6
- forcing: float32 [1, 4, 28, 192, 384], P(None, 'sec', None, 'lat', 'col'), may hold values from -4 to 4
- crm_moisture: bfloat16 [1, 32, 28, 8, 4, 2304], P(None, None, None, ('sec', 'lat'), 'col'), may hold values from -6 to 6
- cloud_order: int32 [4, 2, 9216], P('col', 'lat'), may hold values from 0 to 9215, each once within a row
- wave_table: int32 [128], replicated, may hold values from 0 to 127, each once
Outputs:
- state_out: float32 [1, 4, 28, 192, 384], P(None, 'sec', None, 'lat', 'col')
- spectral: float32 [4, 1, 28, 128, 2, 128], P('sec', None, 'col', 'lat')
Inputs may be any that keep to these rules, and one draw needn't show every extreme that they name: `cloud_order`: every row lists each of the 9216 columns of a band block once. `wave_table`: each wavenumber stands in exactly one slot.
All inputs are finite; a program needn't handle non-finite values.
Results may differ from a plain program's by a relative error of at most 0.0003.
Values sent between devices are 32-bit elements; how exact they have to be, the bound alone decides.
A program may use at most 128 MiB of HBM per device.

v0:
```python
import math

import jax
import jax.numpy as jnp
from jax import lax
from jax.sharding import PartitionSpec as P

NLON = 384
NLAT = 192
MMAX = 128
NSUB = 4


COURANT_SCALE = 0.4
CONDENSE = 0.5


def transport(values, courant, mixing):
    forward = jnp.roll(values, -1, axis=0)
    behind = jnp.roll(values, 1, axis=0)
    return -0.5 * courant * (forward - behind) + mixing * (forward - 2.0 * values + behind)


def cloud_model(vertical_state_stack, forcing, vapour_mass_fraction):
    wind_u = vertical_state_stack[0]
    wind_v = vertical_state_stack[1]
    atmospheric_warmth = vertical_state_stack[2]
    humidity = vertical_state_stack[3]
    courant = COURANT_SCALE * jnp.tanh(wind_u)
    mixing = 0.2 + 0.5 * jnp.abs(courant)
    convective_warming_rate = jnp.broadcast_to(atmospheric_warmth, vapour_mass_fraction.shape)
    crm_water = humidity + vapour_mass_fraction
    start_water = crm_water
    ground_precipitation = jnp.zeros_like(atmospheric_warmth)
    for substep in range(NSUB):
        heat_move = transport(convective_warming_rate, courant, mixing)
        water_move = transport(crm_water, courant, mixing)
        condensed = CONDENSE * jnp.maximum(crm_water - convective_warming_rate, 0.0)
        convective_warming_rate = (
            convective_warming_rate + heat_move + condensed + forcing[2] / NSUB
        )
        crm_water = crm_water + water_move - condensed + forcing[3] / NSUB
        ground_precipitation = ground_precipitation + jnp.mean(condensed, axis=0)
    ground_precipitation = ground_precipitation / NSUB
    zonal_velocity_rate = -ground_precipitation * wind_u + forcing[0]
    meridional_velocity_rate = -ground_precipitation * wind_v + forcing[1]
    warming_rate_change = jnp.mean(convective_warming_rate, axis=0) - atmospheric_warmth
    vapour_rate_change = jnp.mean(crm_water - start_water, axis=0)
    return jnp.stack(
        (zonal_velocity_rate, meridional_velocity_rate, warming_rate_change, vapour_rate_change)
    )


def trig_table(longitudes, wave_numbers):
    phase = (longitudes[:, None] * wave_numbers[None, :] % NLON).astype(jnp.float32) * (
        2.0 * math.pi / NLON
    )
    return jnp.stack((jnp.cos(phase), jnp.sin(phase)), axis=1) / math.sqrt(NLON)


def legendre_table(orders):
    colatitude = (jnp.arange(NLAT, dtype=jnp.int32).astype(jnp.float32) + 0.5) * (math.pi / NLAT)
    cosine = jnp.cos(colatitude)[None, :]
    sine_lat = jnp.sin(colatitude)
    order_col = orders.astype(jnp.float32)[:, None]
    log_diag = 0.5 * (
        lax.lgamma(order_col + 1.5) - lax.lgamma(jnp.float32(1.5)) - lax.lgamma(order_col + 1.0)
    )
    log_diag = log_diag + order_col * jnp.log(sine_lat)[None, :] - 0.5 * math.log(2.0)
    diagonal = jnp.exp(log_diag)
    empty = jnp.zeros_like(diagonal)

    def march_forward(carried, degree):
        previous, current = carried
        deg_float = degree.astype(jnp.float32)
        active = deg_float > order_col
        numerator = jnp.where(active, 4.0 * deg_float * deg_float - 1.0, 1.0)
        bottom = jnp.where(active, deg_float * deg_float - order_col * order_col, 1.0)
        lower_deg = deg_float - 1.0
        retreat = jnp.sqrt(
            jnp.maximum(lower_deg * lower_deg - order_col * order_col, 0.0)
            / (4.0 * lower_deg * lower_deg - 1.0)
        )
        grown = jnp.sqrt(numerator / bottom) * (cosine * current - retreat * previous)
        fresh_row = jnp.where(active, grown, jnp.where(deg_float == order_col, diagonal, 0.0))
        return ((current, fresh_row), fresh_row)

    _, legendre_rows = lax.scan(
        march_forward, (empty, empty), jnp.arange(MMAX, dtype=jnp.int32), unroll=8
    )
    weights = sine_lat / math.sqrt(NLAT)
    return legendre_rows * weights[None, None, :]


def shards(state, forcing, crm_moisture, cloud_order, wave_table):
    members, _, levels, band_rows, lon_block = state.shape
    sections = lax.axis_size("sec")
    lat_bands = lax.axis_size("lat")
    block_cols = band_rows * lon_block
    targets = sections * lat_bands
    per_target = block_cols // targets
    run_cols = lat_bands * per_target
    slot_list = cloud_order[0, 0]
    flat_state = state[:, 0].reshape(members, levels, block_cols)
    flat_force = forcing[:, 0].reshape(members, levels, block_cols)
    stacked = jnp.stack((flat_state, flat_force))
    use_matrix = block_cols <= 2048
    if use_matrix:
        column_ids = jnp.arange(block_cols, dtype=jnp.int32)
        selector = (slot_list[:, None] == column_ids[None, :]).astype(jnp.float32)
        selector = selector.reshape(targets, per_target, block_cols)
        by_target = jnp.einsum(
            "xelc,tpc->txelp", stacked, selector, precision=lax.Precision.HIGHEST
        )
    else:
        slot_table = slot_list.reshape(targets, per_target)
        by_target = jnp.take(stacked, slot_table, axis=3).transpose(3, 0, 1, 2, 4)
    send_width = 2 * members * levels * per_target
    outgoing = by_target.reshape(targets, 1, send_width)
    arrived = lax.all_to_all(outgoing, ("sec", "lat"), split_axis=0, concat_axis=1, tiled=True)
    arrived = arrived.reshape(sections, lat_bands, 2, members, levels, per_target)
    arrived = arrived.transpose(2, 3, 0, 4, 1, 5).reshape(2, members, sections, levels, run_cols)
    vapour_mass_fraction = crm_moisture[:, :, :, 0, 0, :].astype(jnp.float32)
    tendency = jax.vmap(cloud_model)(arrived[0], arrived[1], vapour_mass_fraction)
    back_width = members * levels * per_target
    parted = tendency.reshape(members, sections, levels, lat_bands, per_target).transpose(
        1, 3, 0, 2, 4
    )
    homeward = parted.reshape(targets, 1, back_width)
    returned = lax.all_to_all(homeward, ("sec", "lat"), split_axis=0, concat_axis=1, tiled=True)
    returned = returned.reshape(targets, members, levels, per_target)
    if use_matrix:
        column_tend = jnp.einsum(
            "telp,tpc->elc", returned, selector, precision=lax.Precision.HIGHEST
        )
    else:
        in_slot_order = returned.transpose(1, 2, 0, 3).reshape(members, levels, block_cols)
        inverse = (
            jnp.zeros((block_cols,), jnp.int32)
            .at[slot_list]
            .set(jnp.arange(block_cols, dtype=jnp.int32))
        )
        column_tend = jnp.take(in_slot_order, inverse, axis=2)
    new_state = state + column_tend.reshape(members, 1, levels, band_rows, lon_block)
    fields_now = new_state[:, 0]
    regrouped = lax.all_to_all(fields_now, "col", split_axis=1, concat_axis=3, tiled=True)
    trig_rows = trig_table(jnp.arange(NLON, dtype=jnp.int32), wave_table)
    spectra = jnp.einsum("elay,ycs->leacs", regrouped, trig_rows, precision=lax.Precision.HIGHEST)
    owner_count = MMAX // lat_bands
    owned_waves = lax.dynamic_slice_in_dim(
        wave_table, lax.axis_index("lat") * owner_count, owner_count
    )
    weighted = legendre_table(owned_waves)
    coeffs = jnp.einsum(
        "leacs,nsa->lescn",
        lax.all_to_all(spectra, "lat", split_axis=4, concat_axis=2, tiled=True),
        weighted,
        precision=lax.Precision.HIGHEST,
    )
    return (new_state, coeffs.transpose(1, 0, 2, 3, 4)[None])


def solution(mesh):
    placed = (
        P(None, "sec", None, "lat", "col"),
        P(None, "sec", None, "lat", "col"),
        P(None, None, None, ("sec", "lat"), "col", None),
        P("col", "lat", None),
        P(),
    )
    return jax.shard_map(
        shards,
        mesh=mesh,
        in_specs=placed,
        out_specs=(P(None, "sec", None, "lat", "col"), P("sec", None, "col", "lat", None, None)),
        check_vma=False,
    )
```

profile of v0, /device:TPU:0, one launch (start us, length us, event | category | flops | bytes accessed | tf_op | source)
XLA Modules:
  0.0 617.8 jit_solution(15308398719967561475)
XLA Ops:
  0.6 4.0 copy.116
  4.6 4.0 copy.117
  8.7 13.0 %maximum_bitcast_fusion = f32[2,28,9216]{1,0,2:T(2,128)} fusion(f32[1,1,28,9216]{2,0,3,1:T(1,128)} %bitcast.285, f32[1,1,28,9216]{2,0,3,1:T(1,128)} %bitcast.284), kind=kLoop, calls=%fused_computation.84 | loop fusion | flops 516096 | bytes 4128768 | tf_op jit(solution)/shard_map/stack | solution.py:106
  21.7 66.6 %gather_fusion = f32[9216,2,28]{2,1,0:T(2,128)} fusion(f32[2,28,9216]{1,0,2:T(2,128)} %maximum_bitcast_fusion, s32[9216]{0:T(1024)S(1)} %broadcast_clamp_fusion), kind=kCustom, calls=%fused_computation | custom fusion | bytes 4165632 | tf_op jit(solution)/shard_map/jit(_take)/gather | solution.py:117
  88.3 8.0 %copy.118 = f32[8,1152,2,28]{1,0,2,3:T(8,128)S(1)} copy(f32[8,1152,2,28]{3,2,1,0:T(2,128)} %bitcast.286) | data formatting | bytes 4128768 | tf_op jit(solution)/shard_map/jit(_take)/gather | solution.py:117
  97.9 2.1 copy.96
  100.1 30.3 %all_to_all.48 = f32[8,1,64512]{2,1,0:T(1,128)S(1)} all-to-all(f32[8,1,64512]{2,1,0:T(1,128)S(1)} %copy.96), channel_id=1, replica_groups=mesh['sec'=4,'lat'=2,'col'=4] {'sec','lat'}, dimensions={0} | all-to-all | bytes 4128768 | tf_op jit(solution)/shard_map/all_to_all | solution.py:120
  130.4 6.9 %reduce.8 = f32[8,64512]{1,0:T(8,128)} reduce(f32[8,1,64512]{2,1,0:T(1,128)S(1)} %all_to_all.48, f32[]{:T(128)} %constant.239), dimensions={1}, to_apply=%all_to_all.16.reduce_sub_computation | reduce | bytes 4128772 | tf_op jit(solution)/shard_map/all_to_all | solution.py:120
  137.3 2.0 reshape.4359
  141.3 1.8 broadcast_multiply_fusion.3
  143.9 1.8 copy.98
  145.7 2.2 squeeze.70
  148.9 1.8 copy_bitcast_fusion.3
  151.4 8.7 %fusion.44 = (f32[1,32,28,2304]{3,1,2,0:T(8,128)}, f32[1,32,28,2304]{3,1,2,0:T(8,128)S(1)}) fusion(f32[1,1,28,2304]{3,1,2,0:T(1,128)S(1)} %get-tuple-element.412, f32[1,31,28,2304]{3,1,2,0:T(8,128)S(1)} %slice.206, bf16[1,32,28,1,1,2304]{5,1,4,3,2,0:T(8,128)(2,1)S(1)} %copy-done.2, f32[28,2304]{1,0:T(8,128)S(1)} %get-tuple-element.418, ...), kind=kLoop, calls=%fused_computation.94 | loop fusion | flops 33030144 | bytes 30449664 | tf_op jit(solution)/shard_map/vmap()/add | solution.py:40
  160.0 6.5 %fusion.107 = (f32[1,31,28,2304]{3,1,2,0:T(8,128)}, f32[1,31,28,2304]{3,1,2,0:T(8,128)}) fusion(f32[1,32,28,2304]{3,1,2,0:T(8,128)S(1)} %get-tuple-element.407), kind=kLoop, calls=%fused_computation.237 | loop fusion | bytes 31997952 | tf_op jit(solution)/shard_map/vmap(jit(_roll_static))/slice | solution.py:19
  166.9 15.7 %fusion.51 = (f32[28,2304]{1,0:T(8,128)}, f32[28,2304]{1,0:T(8,128)}, f32[1,32,28,2304]{3,1,2,0:T(8,128)S(1)}) fusion(f32[28,2304]{1,0:T(8,128)S(1)} %get-tuple-element.418, bf16[1,32,28,1,1,2304]{5,1,4,3,2,0:T(8,128)(2,1)S(1)} %copy-done.2, f32[28,2304]{1,0:T(8,128)S(1)} %get-tuple-element.423, f32[28,2304]{1,0:T(8,128)S(1)} %copy-done.8, ...), kind=kLoop, calls=%fused_computation.125 | loop fusion | flops 67995648 | bytes 39481344 | tf_op jit(solution)/shard_map/vmap()/reduce_sum | solution.py:43
  182.6 8.4 %fusion.105 = (f32[1,31,28,2304]{3,1,2,0:T(8,128)}, f32[1,31,28,2304]{3,1,2,0:T(8,128)}) fusion(f32[1,32,28,2304]{3,1,2,0:T(8,128)S(1)} %get-tuple-element.336), kind=kLoop, calls=%fused_computation.235 | loop fusion | bytes 31997952 | tf_op jit(solution)/shard_map/vmap(jit(_roll_static))/slice | solution.py:19
  190.9 2.2 copy-done
  193.2 1.2 fusion.106
  194.3 6.4 %fusion.103 = (f32[1,31,28,2304]{3,1,2,0:T(8,128)}, f32[1,31,28,2304]{3,1,2,0:T(8,128)}) fusion(f32[1,32,28,2304]{3,1,2,0:T(8,128)S(1)} %bitcast.282), kind=kLoop, calls=%fused_computation.233 | loop fusion | bytes 31997952 | tf_op jit(solution)/shard_map/vmap(jit(_roll_static))/slice | solution.py:19
  200.7 1.2 fusion.104
  201.9 31.2 %fusion.52 = (f32[28,2304]{1,0:T(8,128)}, f32[1,32,28,2304]{3,1,2,0:T(8,128)}, f32[1,32,28,2304]{3,1,2,0:T(8,128)}) fusion(f32[28,2304]{1,0:T(8,128)S(1)} %get-tuple-element.419, f32[1,32,28,2304]{3,1,2,0:T(8,128)} %copy-done, f32[28,2304]{1,0:T(8,128)S(1)} %get-tuple-element.418, bf16[1,32,28,1,1,2304]{5,1,4,3,2,0:T(8,128)(2,1)S(1)} %copy-done.2, ...), kind=kLoop, calls=%fused_computation.126 | loop fusion | flops 96961536 | bytes 72253440 | tf_op jit(solution)/shard_map/vmap()/reduce_sum | solution.py:43
  233.0 12.5 %fusion.97 = (f32[1,31,28,2304]{3,1,2,0:T(8,128)}, f32[1,31,28,2304]{3,1,2,0:T(8,128)}) fusion(f32[1,32,28,2304]{3,1,2,0:T(8,128)} %get-tuple-element.338), kind=kLoop, calls=%fused_computation.227 | loop fusion | bytes 31997952 | tf_op jit(solution)/shard_map/vmap(jit(_roll_static))/slice | solution.py:19
  245.5 3.4 fusion.98
  248.9 6.4 %fusion.101 = (f32[1,31,28,2304]{3,1,2,0:T(8,128)}, f32[1,31,28,2304]{3,1,2,0:T(8,128)}) fusion(f32[1,32,28,2304]{3,1,2,0:T(8,128)S(1)} %bitcast.280), kind=kLoop, calls=%fused_computation.231 | loop fusion | bytes 31997952 | tf_op jit(solution)/shard_map/vmap(jit(_roll_static))/slice | solution.py:19
  255.3 1.1 fusion.102
  256.4 18.1 %subtract_add_fusion = (f32[1,32,28,2304]{3,1,2,0:T(8,128)S(1)}, f32[1,32,28,2304]{3,1,2,0:T(8,128)S(1)}) fusion(f32[1,32,28,2304]{3,1,2,0:T(8,128)} %get-tuple-element.338, f32[1,31,28,2304]{3,1,2,0:T(8,128)} %get-tuple-element.383, f32[1,1,28,2304]{3,1,2,0:T(1,128)} %get-tuple-element.385, f32[1,1,28,2304]{3,1,2,0:T(1,128)} %get-tuple-element.384, ...), kind=kLoop, calls=%fused_computation.114 | loop fusion | flops 55738368 | bytes 67092480 | tf_op jit(solution)/shard_map/vmap()/add | solution.py:42
  274.5 6.4 %fusion.95 = (f32[1,31,28,2304]{3,1,2,0:T(8,128)}, f32[1,31,28,2304]{3,1,2,0:T(8,128)}) fusion(f32[1,32,28,2304]{3,1,2,0:T(8,128)S(1)} %get-tuple-element.376), kind=kLoop, calls=%fused_computation.225 | loop fusion | bytes 31997952 | tf_op jit(solution)/shard_map/vmap(jit(_roll_static))/slice | solution.py:19
  282.0 6.4 %fusion.99 = (f32[1,31,28,2304]{3,1,2,0:T(8,128)}, f32[1,31,28,2304]{3,1,2,0:T(8,128)}) fusion(f32[1,32,28,2304]{3,1,2,0:T(8,128)S(1)} %get-tuple-element.377), kind=kLoop, calls=%fused_computation.229 | loop fusion | bytes 31997952 | tf_op jit(solution)/shard_map/vmap(jit(_roll_static))/slice | solution.py:19
  288.4 1.2 fusion.100
  289.6 20.4 %add_reduce_fusion = (f32[28,2304]{1,0:T(8,128)}, f32[28,2304]{1,0:T(8,128)}, f32[28,2304]{1,0:T(8,128)}) fusion(f32[1,32,28,2304]{3,1,2,0:T(8,128)S(1)} %get-tuple-element.377, f32[1,31,28,2304]{3,1,2,0:T(8,128)} %get-tuple-element.387, f32[1,1,28,2304]{3,1,2,0:T(1,128)} %get-tuple-element.389, f32[1,1,28,2304]{3,1,2,0:T(1,128)} %get-tuple-element.388, ...), kind=kLoop, calls=%fused_computation.111 | loop fusion | flops 67931136 | bytes 55738368 | tf_op jit(solution)/shard_map/vmap()/reduce_sum | solution.py:47
  311.0 1.3 multiply_negate_fusion
  312.3 4.1 fusion.64
  317.3 2.0 reshape.4406
  319.3 3.6 all-to-all-start.1
  322.9 34.2 %scatter_custom_fusion = s32[9216]{0:T(1024)S(1)} fusion(s32[9216]{0:T(1024)S(1)} %bitcast.309, s32[9216]{0:T(1024)S(1)} %iota.45, s32[]{:T(128)} %constant.186.clone.1), kind=kCustom, calls=%fused_computation.179 | custom fusion | bytes 36868 | tf_op jit(solution)/shard_map/scatter | solution.py:141
  357.4 3.4 copy.105
  360.8 33.4 %gather_fusion.1 = f32[9216,28]{1,0:T(8,128)} fusion(f32[28,9216]{0,1:T(8,128)} %bitcast.283, s32[9216]{0:T(1024)S(1)} %fusion.73), kind=kCustom, calls=%fused_computation.1 | custom fusion | bytes 2101248 | tf_op jit(solution)/shard_map/jit(_take)/gather | solution.py:143
  394.2 3.2 copy.106
  397.4 1.3 select_add_fusion
  398.7 5.1 all-to-all-start.2
  405.4 31.7 %all-to-all-done.2 = f32[1,28,96,96]{3,2,0,1:T(8,128)S(1)} async-done(((f32[1,28,96,96]{3,2,0,1:T(8,128)}), f32[1,28,96,96]{3,2,0,1:T(8,128)S(1)}, u32[]{:S(2)}, u32[]{:S(2)}) %all-to-all-start.2) | async-done | bytes 1032224 | tf_op jit(solution)/shard_map/all_to_all | solution.py:146
  438.7 1.3 convolution_bitcast_fusion
  440.0 1.4 copy.109
  441.4 3.6 all-to-all-start.3
  444.9 153.6 %while.19 = (s32[]{:T(128)}, f32[64,192]{1,0:T(8,128)S(1)}, f32[64,192]{1,0:T(8,128)S(1)}, f32[16,8,64,192]{3,2,1,0:T(8,128)}, s32[16,8]{0,1:T(8,128)S(1)}, /*in...) while((s32[]{:T(128)}, f32[64,192]{1,0:T(8,128)S(1)}, ...), condition=%wide.region_8.9_spmd.clone.clone, body=%wide.region_7.8_spmd.clone.clone.sunk | while | flops 926866 | bytes 3029748 | solution.py:88
  598.6 8.6 %copy.107 = f32[128,64,192]{0,2,1:T(8,128)} copy(f32[128,64,192]{2,1,0:T(8,128)} %bitcast.288) | data formatting | bytes 12582912 | tf_op jit(solution)/shard_map/reshape | solution.py:88
  608.6 7.7 %fusion.56 = f32[1,1,7,64,2,128]{5,2,4,3,1,0:T(8,128)S(1)} fusion(f32[7,192,2,64]{1,0,2,3:T(8,128)S(1)} %reshape.4408, f32[128,64,192]{0,2,1:T(8,128)} %copy.107, f32[192]{0:T(256)S(1)} %fusion.76), kind=kOutput, calls=%fused_computation.134 | convolution fusion | flops 265814016 | bytes 7439104 | tf_op jit(solution)/shard_map/leacs,nsa->lescn/dot_general | solution.py:154
  (347 shorter events, 87.4 us)
Async XLA Ops:
  0.6 8.1 %copy-start.11 = (s32[1,1,9216]{2,1,0:T(1,128)S(1)}, s32[1,1,9216]{2,1,0:T(1,128)}, u32[]{:S(2)}) copy-start(s32[1,1,9216]{2,1,0:T(1,128)} %param.10) | copy-start | bytes 110596
  141.3 2.6 copy-start.5
  143.9 58.0 %copy-start.3 = (f32[28,2304]{1,0:T(8,128)}, f32[28,2304]{1,0:T(8,128)S(1)}, u32[]{:S(2)}) copy-start(f32[28,2304]{1,0:T(8,128)S(1)} %get-tuple-element.423) | copy-start | bytes 774148
  143.9 7.5 %copy-start.8 = (f32[28,2304]{1,0:T(8,128)S(1)}, f32[28,2304]{1,0:T(8,128)}, u32[]{:S(2)}) copy-start(f32[28,2304]{1,0:T(8,128)} %broadcast_multiply_fusion.2) | copy-start | bytes 774148
  147.9 1.0 copy-start.9
  147.9 3.5 copy-start.2
  151.3 15.5 %copy-start.1 = (f32[1,31,28,2304]{3,1,2,0:T(8,128)}, f32[1,31,28,2304]{3,1,2,0:T(8,128)S(1)}, u32[]{:S(2)}) copy-start(f32[1,31,28,2304]{3,1,2,0:T(8,128)S(1)} %slice.206) | copy-start | bytes 23998468
  182.5 10.6 %copy-start = (f32[1,32,28,2304]{3,1,2,0:T(8,128)}, f32[1,32,28,2304]{3,1,2,0:T(8,128)S(1)}, u32[]{:S(2)}) copy-start(f32[1,32,28,2304]{3,1,2,0:T(8,128)S(1)} %get-tuple-element.336) | copy-start | bytes 24772612
  182.5 11.8 %slice-start.2 = ((s8[8257536]{0:T(1024)(128)(4,1)}), s8[4194304]{0:T(1024)(128)(4,1)S(1)}, s32[]{:S(2)}) async-start(s8[8257536]{0:T(1024)(128)(4,1)} %bitcast.281), calls=%async_computation.6 | async-start | bytes 8388608
  182.5 11.8 %slice-start.3 = ((s8[8257536]{0:T(1024)(128)(4,1)}), s8[4063232]{0:T(1024)(128)(4,1)S(1)}, s32[]{:S(2)}) async-start(s8[8257536]{0:T(1024)(128)(4,1)} %bitcast.281), calls=%async_computation.7 | async-start | bytes 8126464
  233.0 15.9 %slice-start = ((s8[8257536]{0:T(1024)(128)(4,1)}), s8[4194304]{0:T(1024)(128)(4,1)S(1)}, s32[]{:S(2)}) async-start(s8[8257536]{0:T(1024)(128)(4,1)} %bitcast.279), calls=%async_computation.4 | async-start | bytes 8388608
  233.0 15.9 %slice-start.1 = ((s8[8257536]{0:T(1024)(128)(4,1)}), s8[4063232]{0:T(1024)(128)(4,1)S(1)}, s32[]{:S(2)}) async-start(s8[8257536]{0:T(1024)(128)(4,1)} %bitcast.279), calls=%async_computation.5 | async-start | bytes 8126464
  282.0 7.6 %copy-start.4 = (f32[28,2304]{1,0:T(8,128)S(1)}, f32[28,2304]{1,0:T(8,128)}, u32[]{:S(2)}) copy-start(f32[28,2304]{1,0:T(8,128)} %copy-done.3) | copy-start | bytes 774148
  289.6 22.7 %copy-start.6 = (f32[1,4,28,2304]{3,1,2,0:T(4,128)S(1)}, f32[1,4,28,2304]{3,1,2,0:T(4,128)}, u32[]{:S(2)}) copy-start(f32[1,4,28,2304]{3,1,2,0:T(4,128)} %copy-done.5) | copy-start | bytes 3096580
  310.0 7.0 %copy-start.10 = (f32[28,2304]{1,0:T(8,128)S(1)}, f32[28,2304]{1,0:T(8,128)}, u32[]{:S(2)}) copy-start(f32[28,2304]{1,0:T(8,128)} %get-tuple-element.275) | copy-start | bytes 774148
  310.0 12.9 %copy-start.12 = (s32[1,1,9216]{2,1,0:T(1,128)S(1)}, s32[1,1,9216]{2,1,0:T(1,128)}, u32[]{:S(2)}) copy-start(s32[1,1,9216]{2,1,0:T(1,128)} %param.10) | copy-start | bytes 110596
  319.3 38.0 %all-to-all-start.1 = ((f32[8,1,32256]{2,1,0:T(1,128)}), f32[8,1,32256]{2,1,0:T(1,128)S(1)}, u32[]{:S(2)}, u32[]{:S(2)}) async-start(f32[8,1,32256]{2,1,0:T(1,128)} %reshape.4406), calls=%async_computation.1 | async-start | bytes 2064384 | tf_op jit(solution)/shard_map/all_to_all | solution.py:130
  360.8 36.6 %copy-start.7 = (f32[1,1,28,96,96]{4,3,2,1,0:T(8,128)S(1)}, f32[1,1,28,96,96]{4,3,2,1,0:T(8,128)}, u32[]{:S(2)}) copy-start(f32[1,1,28,96,96]{4,3,2,1,0:T(8,128)} %param.7) | copy-start | bytes 3096580
  394.2 9.8 %copy-start.13 = (s32[128]{0:T(128)S(1)}, s32[128]{0:T(128)}, u32[]{:S(2)}) copy-start(s32[128]{0:T(128)} %param.11) | copy-start | bytes 1540
  398.7 38.4 %all-to-all-start.2 = ((f32[1,28,96,96]{3,2,0,1:T(8,128)}), f32[1,28,96,96]{3,2,0,1:T(8,128)S(1)}, u32[]{:S(2)}, u32[]{:S(2)}) async-start(f32[1,28,96,96]{3,2,0,1:T(8,128)} %bitcast.25), calls=%async_computation.2 | async-start | bytes 2752512 | tf_op jit(solution)/shard_map/all_to_all | solution.py:146
  441.4 165.8 %all-to-all-start.3 = ((f32[7,1,96,2,128]{2,3,1,0,4:T(2,128)}), f32[7,1,96,2,128]{2,3,1,0,4:T(2,128)S(1)}, u32[]{:S(2)}, u32[]{:S(2)}) async-start(f32[7,1,96,2,128]{2,3,1,0,4:T(2,128)} %copy.109), calls=%async_computation.3 | async-start | bytes 1835008 | tf_op jit(solution)/shard_map/all_to_all | solution.py:156
where the time goes:
time: 625 us; the launch traced here: 618 us
  local copies, waits for them, and re-layouts  276 us (44%)
  other arithmetic  175 us (28%)
  loops' own time  81.3 us (13%)
  waiting for transfers between devices  31.7 us (5%)
  blocking collectives  30.3 us (5%)
  starting transfers between devices  12.2 us (2%)
  matrix products  9.01 us (1%)
    another operation x1, loops' own time, legendre_table(): lax.scan(march_forward, (empty, empty), jnp.arange(MMAX, dtype=jnp.int32)...  81.3 us
    gather x2, local copies, waits for them, and re-layouts, shards(): by_target = jnp.take(stacked, slot_table, axis=3).transpose(3, 0, 1, 2, 4)  74.6 us
    slice x15, local copies, waits for them, and re-layouts, transport(): forward = jnp.roll(values, -1, axis=0)  62.9 us
    reduce_sum x2, other arithmetic, cloud_model(): ground_precipitation = ground_precipitation + jnp.mean(condensed, axis=0)  46.8 us
    gather x2, local copies, waits for them, and re-layouts, shards(): column_tend = jnp.take(in_slot_order, inverse, axis=2)  36.6 us
    scatter x1, local copies, waits for them, and re-layouts, shards(): inverse = jnp.zeros((block_cols,), jnp.int32).at[slot_list].set(jnp.arang...  34.2 us
    all_to_all x1, waiting for transfers between devices, shards(): lax.all_to_all(fields_now, 'col', split_axis=1, concat_axis=3, tiled=True)  31.7 us
    all_to_all x1, blocking collectives, shards(): lax.all_to_all(outgoing, ('sec', 'lat'), split_axis=0, concat_axis=1, til...  30.3 us
  transfers between devices with their start and end apart: 3, of which 1 were waited for; matrix products, arithmetic and copies ran while one was open for 19% of the time, Pallas kernels for 0%

commit v1 on v0

v1 whole, which is shorter than its diff:
```python
import math

import jax
import jax.numpy as jnp
from jax import lax
from jax.experimental import pallas as pl
from jax.experimental.pallas import tpu as pltpu
from jax.sharding import PartitionSpec as P

NLON = 384
NLAT = 192
MMAX = 128
NSUB = 4
LANES = 128
ROWS = 8

COURANT_SCALE = 0.4
CONDENSE = 0.5


def lane_slice(t):
    return pl.ds(pl.multiple_of(t * LANES, LANES), LANES)


def permute_kernel(x_ref, order_ref, out_ref):
    rows, cols = x_ref.shape
    tiles = cols // LANES

    def one(t, carry):
        order = jnp.broadcast_to(order_ref[:, lane_slice(t)], (ROWS, LANES))
        source = order >> 7
        lane = order & (LANES - 1)
        total = [jnp.zeros((ROWS, LANES), jnp.float32) for _ in range(rows // ROWS)]
        for s in range(tiles):
            hit = source == s
            for r in range(rows // ROWS):
                block = x_ref[r * ROWS : (r + 1) * ROWS, s * LANES : (s + 1) * LANES]
                moved = jnp.take_along_axis(block, lane, axis=1)
                total[r] = jnp.where(hit, moved, total[r])
        for r in range(rows // ROWS):
            out_ref[r * ROWS : (r + 1) * ROWS, lane_slice(t)] = total[r]
        return carry

    lax.fori_loop(0, tiles, one, 0)


def permute(values, order):
    return pl.pallas_call(
        permute_kernel,
        out_shape=jax.ShapeDtypeStruct(values.shape, jnp.float32),
        in_specs=[pl.BlockSpec(memory_space=pltpu.VMEM)] * 2,
        out_specs=pl.BlockSpec(memory_space=pltpu.VMEM),
        name="permute",
    )(values, order)


def cloud_kernel(wind_ref, gap_ref, push_ref, anomaly_ref, rain_ref):
    count, levels, width = anomaly_ref.shape
    scale = CONDENSE / count

    for c0 in range(0, width, LANES):
        c1 = min(c0 + LANES, width)
        for base in range(0, levels, 2 * ROWS):
            top = min(base + 2 * ROWS, levels)
            for r0 in range(base, top, ROWS):
                r1 = min(r0 + ROWS, top)
                courant = COURANT_SCALE * jnp.tanh(wind_ref[r0:r1, c0:c1])
                mixing = 0.2 + 0.5 * jnp.abs(courant)
                ahead = mixing - 0.5 * courant
                back = mixing + 0.5 * courant
                keep = 1.0 - 2.0 * mixing
                push = push_ref[r0:r1, c0:c1]
                start = gap_ref[r0:r1, c0:c1]
                gap = [
                    start
                    + anomaly_ref[n, base:top, c0:c1].astype(jnp.float32)[r0 - base : r1 - base]
                    for n in range(count)
                ]
                rain = [jnp.zeros_like(start) for _ in range(2)]
                for substep in range(NSUB):
                    fresh = []
                    for n in range(count):
                        wet = jnp.maximum(gap[n], 0.0)
                        rain[n % 2] = rain[n % 2] + wet
                        if substep < NSUB - 1:
                            fresh.append(
                                (ahead * gap[(n + 1) % count] + back * gap[n - 1])
                                + (keep * gap[n] + (push - wet))
                            )
                    gap = fresh
                rain_ref[r0:r1, c0:c1] = scale * (rain[0] + rain[1])


def cloud_model(wind, gap, push, anomaly):
    count, levels, width = anomaly.shape
    block = LANES if width % LANES == 0 else width
    flat = pl.BlockSpec((levels, block), lambda i: (0, i))
    return pl.pallas_call(
        cloud_kernel,
        grid=(width // block,),
        out_shape=jax.ShapeDtypeStruct((levels, width), jnp.float32),
        in_specs=[flat, flat, flat, pl.BlockSpec((count, levels, block), lambda i: (0, 0, i))],
        out_specs=flat,
        name="cloud",
    )(wind, gap, push, anomaly)


def legendre_kernel(grow_ref, retreat_ref, order_ref, zero_ref, cosine_ref, diag_ref, fourier_ref, out_ref, *tables):
    slots = order_ref.shape[0]
    halves = len(tables)
    order = order_ref[...]
    grow = grow_ref[...]
    retreat = retreat_ref[...]
    cosine = [cosine_ref[:, h * LANES : (h + 1) * LANES] for h in range(halves)]
    for h in range(halves):
        tables[h][: 2 * slots, :] = jnp.zeros((2 * slots, LANES), jnp.float32)

    def march(n, carry):
        index = zero_ref[...] + n
        grow_n = jnp.take_along_axis(grow, index, axis=1)
        retreat_n = jnp.take_along_axis(retreat, index, axis=1)
        first = order == n
        for h in range(halves):
            previous = tables[h][pl.ds(pl.multiple_of(n * slots, ROWS), slots), :]
            current = tables[h][pl.ds(pl.multiple_of((n + 1) * slots, ROWS), slots), :]
            grown = grow_n * (cosine[h] * current - retreat_n * previous)
            fresh = jnp.where(first, diag_ref[:, h * LANES : (h + 1) * LANES], grown)
            tables[h][pl.ds(pl.multiple_of((n + 2) * slots, ROWS), slots), :] = fresh
        return carry

    lax.fori_loop(0, MMAX, march, 0)

    def contract(s, carry):
        total = None
        for h in range(halves):
            weighted = tables[h][pl.ds(2 * slots + s, MMAX, stride=slots), :]
            term = lax.dot_general(
                fourier_ref[s, :, h * LANES : (h + 1) * LANES],
                weighted,
                (((1,), (1,)), ((), ())),
                precision=lax.Precision.HIGHEST,
                preferred_element_type=jnp.float32,
            )
            total = term if total is None else total + term
        out_ref[s] = total
        return carry

    lax.fori_loop(0, slots, contract, 0)


def legendre(orders, fourier):
    slots, terms, lats = fourier.shape
    wide = -(-lats // LANES) * LANES
    colatitude = (jnp.arange(lats, dtype=jnp.int32).astype(jnp.float32) + 0.5) * (math.pi / lats)
    sine_lat = jnp.sin(colatitude)
    order_col = orders.astype(jnp.float32)[:, None]
    log_diag = 0.5 * (
        lax.lgamma(order_col + 1.5) - lax.lgamma(jnp.float32(1.5)) - lax.lgamma(order_col + 1.0)
    )
    log_diag = log_diag + order_col * jnp.log(sine_lat)[None, :] - 0.5 * math.log(2.0)
    diagonal = jnp.exp(log_diag) * (sine_lat / math.sqrt(lats))[None, :]
    degree = jnp.arange(MMAX, dtype=jnp.int32).astype(jnp.float32)[None, :]
    active = degree > order_col
    numerator = jnp.where(active, 4.0 * degree * degree - 1.0, 0.0)
    bottom = jnp.where(active, degree * degree - order_col * order_col, 1.0)
    lower = degree - 1.0
    retreat = jnp.sqrt(
        jnp.maximum(lower * lower - order_col * order_col, 0.0) / (4.0 * lower * lower - 1.0)
    )
    grow = jnp.sqrt(numerator / bottom)
    pad = ((0, 0), (0, wide - lats))
    return pl.pallas_call(
        legendre_kernel,
        out_shape=jax.ShapeDtypeStruct((slots, terms, MMAX), jnp.float32),
        in_specs=[pl.BlockSpec(memory_space=pltpu.VMEM)] * 7,
        out_specs=pl.BlockSpec(memory_space=pltpu.VMEM),
        scratch_shapes=[pltpu.VMEM(((MMAX + 2) * slots, LANES), jnp.float32)] * (wide // LANES),
        name="legendre",
    )(
        grow,
        retreat,
        jnp.broadcast_to(orders[:, None], (slots, LANES)),
        jnp.zeros((slots, LANES), jnp.int32),
        jnp.pad(jnp.cos(colatitude)[None, :], pad),
        jnp.pad(diagonal, pad),
        jnp.pad(fourier, ((0, 0),) + pad),
    )


def trig_table(longitudes, wave_numbers):
    phase = (longitudes[:, None] * wave_numbers[None, :] % NLON).astype(jnp.float32) * (
        2.0 * math.pi / NLON
    )
    return jnp.stack((jnp.cos(phase), jnp.sin(phase)), axis=1) / math.sqrt(NLON)


def inverse_order(order):
    cols = order.shape[0]
    tiles = cols // LANES
    slots = jnp.arange(cols, dtype=jnp.int32)
    high = (order[None, :] // LANES) == jnp.arange(tiles, dtype=jnp.int32)[:, None]
    low = (order[:, None] % LANES) == jnp.arange(LANES, dtype=jnp.int32)[None, :]
    digits = jnp.stack((slots // LANES, slots % LANES)).astype(jnp.bfloat16)
    left = jnp.where(high[None], digits[:, None, :], jnp.bfloat16(0)).reshape(2 * tiles, cols)
    found = jnp.dot(left, low.astype(jnp.bfloat16), preferred_element_type=jnp.float32)
    found = found.reshape(2, cols).astype(jnp.int32)
    return found[0] * LANES + found[1]


def shards(state, forcing, crm_moisture, cloud_order, wave_table):
    members, _, levels, band_rows, lon_block = state.shape
    sections = lax.axis_size("sec")
    lat_bands = lax.axis_size("lat")
    block_cols = band_rows * lon_block
    targets = sections * lat_bands
    per_target = block_cols // targets
    run_cols = lat_bands * per_target
    padded = -(-levels // ROWS) * ROWS
    field = lax.axis_index("sec")
    slot_list = cloud_order[0, 0]
    own, force = state[0, 0], forcing[0, 0]

    mate = lax.ppermute(jnp.where(field == 2, force, own), "sec", [(2, 3), (3, 2)])
    part = jnp.where(
        field == 3, (force - mate) / NSUB, jnp.where(field == 2, mate - own, own)
    )
    flat = jnp.pad(part.reshape(levels, block_cols), ((0, padded - levels), (0, 0)))
    in_slots = permute(flat, slot_list[None, :])[:levels]
    outgoing = in_slots.reshape(levels, targets, per_target).transpose(1, 0, 2)
    arrived = lax.all_to_all(outgoing, ("sec", "lat"), split_axis=0, concat_axis=0, tiled=True)
    arrived = arrived.reshape(sections, lat_bands, levels, per_target).transpose(0, 2, 1, 3)
    arrived = arrived.reshape(sections, levels, run_cols)
    rain = cloud_model(arrived[0], arrived[2], arrived[3], crm_moisture[0, :, :, 0, 0, :])
    homeward = rain.reshape(levels, lat_bands, per_target).transpose(1, 0, 2)
    homeward = jnp.broadcast_to(homeward[None], (sections, lat_bands, levels, per_target))
    homeward = homeward.reshape(targets, levels, per_target)
    returned = lax.all_to_all(homeward, ("sec", "lat"), split_axis=0, concat_axis=0, tiled=True)
    returned = returned.transpose(1, 0, 2).reshape(levels, block_cols)
    returned = jnp.pad(returned, ((0, padded - levels), (0, 0)))
    rainfall = permute(returned, inverse_order(slot_list)[None, :])[:levels]
    rainfall = rainfall.reshape(levels, band_rows, lon_block)
    share = jnp.where(
        field < 2, own * (-1.0 / NSUB), jnp.where(field == 2, jnp.float32(1), jnp.float32(-1))
    )
    fresh = own + (share * rainfall + force)

    regrouped = lax.all_to_all(fresh, "col", split_axis=0, concat_axis=2, tiled=True)
    trig_rows = trig_table(jnp.arange(NLON, dtype=jnp.int32), wave_table)
    spectra = jnp.einsum("lay,ycs->slca", regrouped, trig_rows, precision=lax.Precision.HIGHEST)
    owner_count = MMAX // lat_bands
    owned_waves = lax.dynamic_slice_in_dim(
        wave_table, lax.axis_index("lat") * owner_count, owner_count
    )
    gathered = lax.all_to_all(spectra, "lat", split_axis=0, concat_axis=3, tiled=True)
    own_levels = gathered.shape[1]
    coeffs = legendre(owned_waves, gathered.reshape(owner_count, own_levels * 2, NLAT))
    coeffs = coeffs.reshape(owner_count, own_levels, 2, MMAX).transpose(1, 0, 2, 3)
    return (fresh[None, None], coeffs[None, None])


def solution(mesh):
    placed = (
        P(None, "sec", None, "lat", "col"),
        P(None, "sec", None, "lat", "col"),
        P(None, None, None, ("sec", "lat"), "col", None),
        P("col", "lat", None),
        P(),
    )
    return jax.shard_map(
        shards,
        mesh=mesh,
        in_specs=placed,
        out_specs=(P(None, "sec", None, "lat", "col"), P("sec", None, "col", "lat", None, None)),
        check_vma=False,
    )
```

time: 625 us -> 275 us (0.44)
  local copies, waits for them, and re-layouts: 276 us -> 48.7 us
  other arithmetic: 175 us -> 17.8 us
  Pallas kernels: 0 us -> 118 us
  loops' own time: 81.3 us -> 0 us
  blocking collectives: 30.3 us -> 0 us
  waiting for transfers between devices: 31.7 us -> 58.2 us
  starting transfers between devices: 12.2 us -> 20.9 us
    pallas_call x0 -> x4, Pallas kernels: none -> 118 us  [the longest x2 59 us: permute(): pl.pallas_call(permute_kernel, out_shape=jax.ShapeDtypeStruct(values.shap...]
    gather x4 -> x0, local copies, waits for them, and re-layouts: 111 us -> none  [the longest x2 74.6 us: shards(): by_target = jnp.take(stacked, slot_table, axis=3).transpose(3, 0, 1, 2, 4)]
    another operation x1 -> x0, loops' own time: 81.3 us -> none  [legendre_table(): lax.scan(march_forward, (empty, empty), jnp.arange(MMAX, dtype=jnp.int32)...]
    slice x34 -> x0, local copies, waits for them, and re-layouts: 75.4 us -> none  [the longest x15 62.9 us: transport(): forward = jnp.roll(values, -1, axis=0)]
    reduce_sum x3 -> x0, other arithmetic: 67.2 us -> none  [the longest x2 46.8 us: cloud_model(): ground_precipitation = ground_precipitation + jnp.mean(condensed, axis=0)]
    scatter x1 -> x0, local copies, waits for them, and re-layouts: 34.2 us -> none  [shards(): inverse = jnp.zeros((block_cols,), jnp.int32).at[slot_list].set(jnp.arang...]
    sqrt x48 -> x1, other arithmetic: 31 us -> 0.72 us  [legendre(): jnp.sqrt(jnp.maximum(lower * lower - order_col * order_col, 0.0) / (4.0 *...]
    all_to_all x1 -> x0, blocking collectives: 30.3 us -> none  [shards(): lax.all_to_all(outgoing, ('sec', 'lat'), split_axis=0, concat_axis=1, til...]
  transfers between devices with their start and end apart: 3 -> 5, of which waited for: 1 -> 4; matrix products, arithmetic and copies ran while one was open for 19% -> 10% of each run, Pallas kernels for 0% -> 0%
where the time goes in v1:
time: 275 us; the launch traced here: 274 us
  Pallas kernels  118 us (43%)
  waiting for transfers between devices  58.2 us (21%)
  local copies, waits for them, and re-layouts  48.7 us (18%)
  starting transfers between devices  20.9 us (8%)
  other arithmetic  17.8 us (6%)
  matrix products  9.21 us (3%)
    pallas_call x2, Pallas kernels, permute(): pl.pallas_call(permute_kernel, out_shape=jax.ShapeDtypeStruct(values.shap...  59 us
    pallas_call x1, Pallas kernels, legendre(): pl.pallas_call(legendre_kernel, out_shape=jax.ShapeDtypeStruct((slots, te...  43.9 us
    all_to_all x1, waiting for transfers between devices, shards(): lax.all_to_all(fresh, 'col', split_axis=0, concat_axis=2, tiled=True)  26.2 us
    all_to_all x1, waiting for transfers between devices, shards(): lax.all_to_all(outgoing, ('sec', 'lat'), split_axis=0, concat_axis=0, til...  16.1 us
    pallas_call x1, Pallas kernels, cloud_model(): pl.pallas_call(cloud_kernel, grid=(width // block,), out_shape=jax.ShapeD...  15.3 us
    unnamed x22, local copies, waits for them, and re-layouts  12.2 us
    all_to_all x1, waiting for transfers between devices, shards(): lax.all_to_all(spectra, 'lat', split_axis=0, concat_axis=3, tiled=True)  9.02 us
    all_to_all x1, waiting for transfers between devices, shards(): lax.all_to_all(homeward, ('sec', 'lat'), split_axis=0, concat_axis=0, til...  6.81 us
  transfers between devices with their start and end apart: 5, of which 4 were waited for; matrix products, arithmetic and copies ran while one was open for 10% of the time, Pallas kernels for 0%

profile of v1, /device:TPU:0, one launch (start us, length us, event | category | flops | bytes accessed | tf_op | source)
XLA Modules:
  0.0 273.9 jit_solution(11726903530138641278)
XLA Ops:
  0.6 3.0 %bitcast_select_fusion = f32[28,96,96]{2,1,0:T(8,128)} fusion(f32[1,1,28,96,96]{4,3,2,1,0:T(8,128)} %param.5, f32[1,1,28,96,96]{4,3,2,1,0:T(8,128)} %param.6, pred[]{:T(512)S(6)} %eq.44), kind=kLoop, calls=%fused_computation.10 | loop fusion | flops 258048 | bytes 3096577 | tf_op jit(solution)/shard_map/jit(_where)/select_n | solution.py:223
  3.6 1.8 collective-permute-start
  6.4 6.8 %copy.55 = bf16[1,32,28,1,1,2304]{5,2,1,4,3,0:T(8,128)(2,1)} copy(bf16[1,32,28,1,1,2304]{5,1,4,3,2,0:T(8,128)(2,1)} %param.7) | data formatting | bytes 8257536 | tf_op args[2]
  13.3 2.8 %fusion.2 = f32[28,96,96]{2,1,0:T(8,128)} fusion(f32[28,96,96]{2,1,0:T(8,128)} %collective-permute-done, f32[1,1,28,96,96]{4,3,2,1,0:T(8,128)S(1)} %copy-done, f32[1,1,28,96,96]{4,3,2,1,0:T(8,128)S(1)} %copy-done.1, pred[]{:T(512)S(6)} %eq.44, pred[]{:T(512)S(6)} %eq.45), kind=kLoop, calls=%fused_computation.7 | loop fusion | flops 1290240 | bytes 4128770 | tf_op jit(solution)/shard_map/jit(_where)/select_n | solution.py:224
  16.1 3.2 %reshape.476 = f32[28,9216]{1,0:T(8,128)} reshape(f32[28,96,96]{2,1,0:T(8,128)} %fusion.2) | data formatting | bytes 2064384 | tf_op jit(solution)/shard_map/reshape | solution.py:227
  19.3 2.4 pad.19.x_ref
  21.7 29.5 %permute.2 = f32[32,9216]{1,0:T(8,128)} custom-call(f32[32,9216]{1,0:T(8,128)} %pad.19.x_ref, s32[1,9216]{1,0:T(1,128)} %bitcast.106), custom_call_target="tpu_custom_call" | custom-call | tf_op jit(solution)/shard_map/permute/pallas_call | solution.py:48
  51.2 1.5 copy.46
  52.8 1.2 copy.57
  54.0 5.5 %all-to-all-start = ((f32[8,28,1152]{2,1,0:T(8,128)}), f32[8,28,1152]{2,1,0:T(8,128)}, u32[]{:S(2)}, u32[]{:S(2)}) async-start(f32[8,28,1152]{2,1,0:T(8,128)} %bitcast.91), calls=%async_computation | async-start | bytes 2359296 | tf_op jit(solution)/shard_map/all_to_all | solution.py:230
  59.5 16.1 %all-to-all-done = f32[8,28,1152]{2,1,0:T(8,128)} async-done(((f32[8,28,1152]{2,1,0:T(8,128)}), f32[8,28,1152]{2,1,0:T(8,128)}, u32[]{:S(2)}, u32[]{:S(2)}) %all-to-all-start) | async-done | bytes 1032224 | tf_op jit(solution)/shard_map/all_to_all | solution.py:230
  75.6 2.1 copy.58
  77.9 0.7 copy.47
  78.7 0.7 copy.48
  79.5 0.7 copy.49
  80.3 15.3 %cloud.1 = f32[28,2304]{1,0:T(8,128)} custom-call(f32[28,2304]{1,0:T(8,128)} %bitcast.99, f32[28,2304]{1,0:T(8,128)} %bitcast.100, f32[28,2304]{1,0:T(8,128)} %bitcast.101, bf16[32,28,2304]{2,1,0:T(8,128)(2,1)} %bitcast.85), custom_call_target="tpu_custom_call" | custom-call | tf_op jit(solution)/shard_map/cloud/pallas_call | solution.py:98
  95.6 1.8 reshape.479
  97.4 1.0 copy.33
  98.4 1.1 broadcast_in_dim.74
  99.5 4.3 %all-to-all-start.1 = ((f32[8,28,1152]{2,1,0:T(8,128)}), f32[8,28,1152]{2,1,0:T(8,128)}, u32[]{:S(2)}, u32[]{:S(2)}) async-start(f32[8,28,1152]{2,1,0:T(8,128)} %bitcast.90), calls=%async_computation.1 | async-start | bytes 2359296 | tf_op jit(solution)/shard_map/all_to_all | solution.py:237
  103.8 2.0 broadcast_select_fusion
  105.7 6.5 %fusion.7 = s32[144,128]{1,0:T(8,128)S(1)} fusion(bf16[144,9216]{1,0:T(8,128)(2,1)} %bitcast.97, s32[9216]{0:T(1024)S(1)} %copy-done.3), kind=kOutput, calls=%fused_computation.20 | convolution fusion | flops 340936704 | bytes 2764800 | tf_op jit(solution)/shard_map/dot_general | solution.py:205
  112.9 6.8 %all-to-all-done.1 = f32[8,28,1152]{2,1,0:T(8,128)} async-done(((f32[8,28,1152]{2,1,0:T(8,128)}), f32[8,28,1152]{2,1,0:T(8,128)}, u32[]{:S(2)}, u32[]{:S(2)}) %all-to-all-start.1) | async-done | bytes 1032224 | tf_op jit(solution)/shard_map/all_to_all | solution.py:237
  119.7 1.9 copy.34
  121.9 1.1 pad.20.x_ref
  123.0 29.5 %permute.3 = f32[32,9216]{1,0:T(8,128)} custom-call(f32[32,9216]{1,0:T(8,128)} %pad.20.x_ref, s32[1,9216]{1,0:T(1,128)} %bitcast.108), custom_call_target="tpu_custom_call" | custom-call | tf_op jit(solution)/shard_map/permute/pallas_call | solution.py:48
  152.5 2.9 %reshape.483 = f32[28,96,96]{2,1,0:T(8,128)} reshape(f32[28,9216]{1,0:T(8,128)} %bitcast.86) | data formatting | bytes 2064384 | tf_op jit(solution)/shard_map/reshape | solution.py:241
  155.4 2.8 %bitcast_add_fusion = f32[28,96,96]{2,1,0:T(8,128)} fusion(f32[1,1,28,96,96]{4,3,2,1,0:T(8,128)S(1)} %copy-done, f32[28,96,96]{2,1,0:T(8,128)} %reshape.483, f32[1,1,28,96,96]{4,3,2,1,0:T(8,128)S(1)} %copy-done.1, f32[]{:T(128)S(6)} %select_n.123, pred[]{:T(512)S(6)} %lt.24), kind=kLoop, calls=%fused_computation.9 | loop fusion | flops 1290240 | bytes 4128773 | tf_op jit(solution)/shard_map/add | solution.py:245
  158.2 5.0 %all-to-all-start.2 = ((f32[28,96,96]{2,1,0:T(8,128)}), f32[28,96,96]{2,1,0:T(8,128)}, u32[]{:S(2)}, u32[]{:S(2)}) async-start(f32[28,96,96]{2,1,0:T(8,128)} %bitcast_add_fusion), calls=%async_computation.2 | async-start | bytes 2752512 | tf_op jit(solution)/shard_map/all_to_all | solution.py:247
  163.5 0.6 pad.22.diag_ref
  164.8 0.7 divide_sqrt_fusion
  165.6 1.6 fusion.18
  167.1 2.9 %reshape.482 = f32[1,1,28,96,96]{4,3,2,1,0:T(8,128)} reshape(f32[28,9216]{1,0:T(8,128)} %bitcast.87) | data formatting | bytes 2064384 | tf_op jit(solution)/shard_map/reshape | solution.py:241
  170.0 26.2 %all-to-all-done.2 = f32[28,96,96]{2,1,0:T(8,128)} async-done(((f32[28,96,96]{2,1,0:T(8,128)}), f32[28,96,96]{2,1,0:T(8,128)}, u32[]{:S(2)}, u32[]{:S(2)}) %all-to-all-start.2) | async-done | bytes 1032224 | tf_op jit(solution)/shard_map/all_to_all | solution.py:247
  196.2 3.3 %copy.56 = f32[4,7,96,96]{3,0,2,1:T(4,128)} copy(f32[4,7,96,96]{3,2,1,0:T(8,128)} %bitcast.15) | data formatting | bytes 2064384 | tf_op jit(solution)/shard_map/all_to_all | solution.py:247
  199.6 2.9 %reshape.487 = f32[7,96,384,1]{2,1,0,3:T(8,128)} reshape(f32[7,96,4,96]{3,2,1,0:T(4,128)} %bitcast.88) | data formatting | bytes 2064384 | tf_op jit(solution)/shard_map/all_to_all | solution.py:247
  202.4 2.7 convolution_bitcast_fusion
  205.1 1.4 copy.36
  206.5 4.4 %all-to-all-start.3 = ((f32[128,7,2,96]{3,2,1,0:T(2,128)}), f32[128,7,2,96]{3,2,1,0:T(2,128)}, u32[]{:S(2)}, u32[]{:S(2)}) async-start(f32[128,7,2,96]{3,2,1,0:T(2,128)} %copy.36), calls=%async_computation.3 | async-start | bytes 1835008 | tf_op jit(solution)/shard_map/all_to_all | solution.py:254
  210.9 2.8 %add_add_fusion = f32[1,1,28,96,96]{4,3,2,1,0:T(8,128)} fusion(f32[1,1,28,96,96]{4,3,2,1,0:T(8,128)S(1)} %copy-done, f32[1,1,28,96,96]{4,3,2,1,0:T(8,128)S(1)} %copy-done.1, f32[1,1,28,96,96]{4,3,2,1,0:T(8,128)} %reshape.482, f32[]{:T(128)S(6)} %select_n.123, pred[]{:T(512)S(6)} %lt.24), kind=kLoop, calls=%fused_computation.17 | loop fusion | flops 1290240 | bytes 4128773 | tf_op jit(solution)/shard_map/add | solution.py:245
  213.7 9.0 %all-to-all-done.3 = f32[128,7,2,96]{3,2,1,0:T(2,128)} async-done(((f32[128,7,2,96]{3,2,1,0:T(2,128)}), f32[128,7,2,96]{3,2,1,0:T(2,128)}, u32[]{:S(2)}, u32[]{:S(2)}) %all-to-all-start.3) | async-done | bytes 688160 | tf_op jit(solution)/shard_map/all_to_all | solution.py:254
  222.7 1.3 copy.37
  224.0 0.7 copy.44
  225.3 1.1 pad.23.fourier_ref
  226.4 0.7 broadcast_in_dim.81.order_ref
  227.7 43.9 %legendre.1 = f32[64,14,128]{2,1,0:T(8,128)} custom-call(f32[64,128]{1,0:T(8,128)} %get-tuple-element.18.grow_ref, f32[64,128]{1,0:T(8,128)} %get-tuple-element.17.retreat_ref, s32[64,128]{1,0:T(8,128)} %broadcast_in_dim.81.order_ref, s32[64,128]{1,0:T(8,128)} %broadcast_in_dim.82.zero_ref, f32[1,256]{1,0:T(1,128)} %pad.21.cosine_ref, ...), custom_call_target="tpu_custom_call" | custom-call | tf_op jit(solution)/shard_map/legendre/pallas_call | solution.py:172
  271.6 1.2 copy.40
  272.8 1.1 copy.41
  (35 shorter events, 4.7 us)
Async XLA Ops:
  0.6 4.8 %copy-start.2 = (s32[1,1,9216]{2,1,0:T(1,128)S(1)}, s32[1,1,9216]{2,1,0:T(1,128)}, u32[]{:S(2)}) copy-start(s32[1,1,9216]{2,1,0:T(1,128)} %param.8) | copy-start | bytes 110596
  3.6 9.6 %collective-permute-start = (f32[28,96,96]{2,1,0:T(8,128)}, f32[28,96,96]{2,1,0:T(8,128)}, u32[]{:S(2)}, u32[]{:S(2)}) collective-permute-start(f32[28,96,96]{2,1,0:T(8,128)} %bitcast_select_fusion), channel_id=1, source_target_pairs={{16,24},{24,16},{17,25},{25,17},{18,26},{26,18},{19,27},{27,19},{2... | collective-permute-start | bytes 3096584 | tf_op jit(solution)/shard_map/ppermute | solution.py:223
  6.4 6.9 %copy-start = (f32[1,1,28,96,96]{4,3,2,1,0:T(8,128)S(1)}, f32[1,1,28,96,96]{4,3,2,1,0:T(8,128)}, u32[]{:S(2)}) copy-start(f32[1,1,28,96,96]{4,3,2,1,0:T(8,128)} %param.5) | copy-start | bytes 3096580
  6.4 6.9 %copy-start.1 = (f32[1,1,28,96,96]{4,3,2,1,0:T(8,128)S(1)}, f32[1,1,28,96,96]{4,3,2,1,0:T(8,128)}, u32[]{:S(2)}) copy-start(f32[1,1,28,96,96]{4,3,2,1,0:T(8,128)} %param.6) | copy-start | bytes 3096580
  54.0 21.7 %all-to-all-start = ((f32[8,28,1152]{2,1,0:T(8,128)}), f32[8,28,1152]{2,1,0:T(8,128)}, u32[]{:S(2)}, u32[]{:S(2)}) async-start(f32[8,28,1152]{2,1,0:T(8,128)} %bitcast.91), calls=%async_computation | async-start | bytes 2359296 | tf_op jit(solution)/shard_map/all_to_all | solution.py:230
  99.5 20.2 %all-to-all-start.1 = ((f32[8,28,1152]{2,1,0:T(8,128)}), f32[8,28,1152]{2,1,0:T(8,128)}, u32[]{:S(2)}, u32[]{:S(2)}) async-start(f32[8,28,1152]{2,1,0:T(8,128)} %bitcast.90), calls=%async_computation.1 | async-start | bytes 2359296 | tf_op jit(solution)/shard_map/all_to_all | solution.py:237
  103.8 2.0 copy-start.3
  158.2 5.0 %copy-start.4 = (s32[128]{0:T(128)S(1)}, s32[128]{0:T(128)}, u32[]{:S(2)}) copy-start(s32[128]{0:T(128)} %param.9) | copy-start | bytes 1540
  158.2 38.1 %all-to-all-start.2 = ((f32[28,96,96]{2,1,0:T(8,128)}), f32[28,96,96]{2,1,0:T(8,128)}, u32[]{:S(2)}, u32[]{:S(2)}) async-start(f32[28,96,96]{2,1,0:T(8,128)} %bitcast_add_fusion), calls=%async_computation.2 | async-start | bytes 2752512 | tf_op jit(solution)/shard_map/all_to_all | solution.py:247
  206.5 16.2 %all-to-all-start.3 = ((f32[128,7,2,96]{3,2,1,0:T(2,128)}), f32[128,7,2,96]{3,2,1,0:T(2,128)}, u32[]{:S(2)}, u32[]{:S(2)}) async-start(f32[128,7,2,96]{3,2,1,0:T(2,128)} %copy.36), calls=%async_computation.3 | async-start | bytes 1835008 | tf_op jit(solution)/shard_map/all_to_all | solution.py:254

commit v2 on v1

--- a/solution.py
+++ b/solution.py
@@ -18,30 +18,43 @@
 CONDENSE = 0.5
 
 
-def lane_slice(t):
-    return pl.ds(pl.multiple_of(t * LANES, LANES), LANES)
-
-
-def permute_kernel(x_ref, order_ref, out_ref):
+def permute_kernel(x_ref, order_ref, out_ref, parts):
     rows, cols = x_ref.shape
     tiles = cols // LANES
+    width = 2 * LANES if tiles % 2 == 0 else LANES
+    batch = tiles // 3 if tiles % 3 == 0 else tiles
+
+    for s in range(tiles):
+        block = x_ref[:, s * LANES : (s + 1) * LANES]
+        coarse = block.astype(jnp.bfloat16)
+        parts[s * rows : (s + 1) * rows, :LANES] = coarse
+        parts[s * rows : (s + 1) * rows, LANES:] = (block - coarse.astype(jnp.float32)).astype(
+            jnp.bfloat16
+        )
+    wanted = lax.broadcasted_iota(jnp.int32, (2 * LANES, width), 0) & (LANES - 1)
 
     def one(t, carry):
-        order = jnp.broadcast_to(order_ref[:, lane_slice(t)], (ROWS, LANES))
-        source = order >> 7
-        lane = order & (LANES - 1)
-        total = [jnp.zeros((ROWS, LANES), jnp.float32) for _ in range(rows // ROWS)]
-        for s in range(tiles):
-            hit = source == s
-            for r in range(rows // ROWS):
-                block = x_ref[r * ROWS : (r + 1) * ROWS, s * LANES : (s + 1) * LANES]
-                moved = jnp.take_along_axis(block, lane, axis=1)
-                total[r] = jnp.where(hit, moved, total[r])
+        at = pl.ds(pl.multiple_of(t * width, width), width)
+        order = order_ref[:, at]
+        source = jnp.broadcast_to(order >> 7, (ROWS, width))
+        chosen = jnp.where(wanted == (order & (LANES - 1)), 1.0, 0.0).astype(jnp.bfloat16)
+        total = [jnp.zeros((ROWS, width), jnp.float32) for _ in range(rows // ROWS)]
+        for first in range(0, tiles, batch):
+            moved = jnp.dot(
+                parts[first * rows : (first + batch) * rows, :],
+                chosen,
+                preferred_element_type=jnp.float32,
+            )
+            for s in range(batch):
+                hit = source == first + s
+                for r in range(rows // ROWS):
+                    begin = s * rows + r * ROWS
+                    total[r] = jnp.where(hit, moved[begin : begin + ROWS], total[r])
         for r in range(rows // ROWS):
-            out_ref[r * ROWS : (r + 1) * ROWS, lane_slice(t)] = total[r]
+            out_ref[r * ROWS : (r + 1) * ROWS, at] = total[r]
         return carry
 
-    lax.fori_loop(0, tiles, one, 0)
+    lax.fori_loop(0, cols // width, one, 0)
 
 
 def permute(values, order):
@@ -50,6 +63,9 @@
         out_shape=jax.ShapeDtypeStruct(values.shape, jnp.float32),
         in_specs=[pl.BlockSpec(memory_space=pltpu.VMEM)] * 2,
         out_specs=pl.BlockSpec(memory_space=pltpu.VMEM),
+        scratch_shapes=[
+            pltpu.VMEM((values.shape[0] * values.shape[1] // LANES, 2 * LANES), jnp.bfloat16)
+        ],
         name="permute",
     )(values, order)
 
@@ -105,7 +121,7 @@
     )(wind, gap, push, anomaly)
 
 
-def legendre_kernel(grow_ref, retreat_ref, order_ref, zero_ref, cosine_ref, diag_ref, fourier_ref, out_ref, *tables):
+def march_kernel(grow_ref, retreat_ref, order_ref, zero_ref, cosine_ref, diag_ref, *tables):
     slots = order_ref.shape[0]
     halves = len(tables)
     order = order_ref[...]
@@ -130,26 +146,38 @@
 
     lax.fori_loop(0, MMAX, march, 0)
 
-    def contract(s, carry):
-        total = None
-        for h in range(halves):
-            weighted = tables[h][pl.ds(2 * slots + s, MMAX, stride=slots), :]
-            term = lax.dot_general(
-                fourier_ref[s, :, h * LANES : (h + 1) * LANES],
-                weighted,
-                (((1,), (1,)), ((), ())),
-                precision=lax.Precision.HIGHEST,
-                preferred_element_type=jnp.float32,
+
+def contract_kernel(fourier_ref, *refs):
+    *tables, out_ref = refs
+    slots, terms, _ = fourier_ref.shape
+    group = 4 if slots % 4 == 0 else 1
+
+    def split(values):
+        coarse = values.astype(jnp.bfloat16)
+        return coarse, (values - coarse.astype(jnp.float32)).astype(jnp.bfloat16)
+
+    def product(left, right):
+        return lax.dot_general(
+            left, right, (((1,), (1,)), ((), ())), preferred_element_type=jnp.float32
+        )
+
+    def contract(g, carry):
+        for j in range(group):
+            s = g * group + j
+            weighted = jnp.concatenate(
+                [table[pl.ds(2 * slots + s, MMAX, stride=slots), :] for table in tables], axis=1
             )
-            total = term if total is None else total + term
-        out_ref[s] = total
+            coarse, fine = split(weighted)
+            head, rest = split(fourier_ref[s])
+            main = product(jnp.concatenate([head, rest], axis=0), coarse)
+            out_ref[s] = main[:terms] + main[terms:] + product(head, fine)
         return carry
 
-    lax.fori_loop(0, slots, contract, 0)
-
-
-def legendre(orders, fourier):
-    slots, terms, lats = fourier.shape
+    lax.fori_loop(0, slots // group, contract, 0)
+
+
+def legendre_tables(orders, lats):
+    slots = orders.shape[0]
     wide = -(-lats // LANES) * LANES
     colatitude = (jnp.arange(lats, dtype=jnp.int32).astype(jnp.float32) + 0.5) * (math.pi / lats)
     sine_lat = jnp.sin(colatitude)
@@ -169,13 +197,16 @@
     )
     grow = jnp.sqrt(numerator / bottom)
     pad = ((0, 0), (0, wide - lats))
+    table = jax.ShapeDtypeStruct(((MMAX + 2) * slots, LANES), jnp.float32)
     return pl.pallas_call(
-        legendre_kernel,
-        out_shape=jax.ShapeDtypeStruct((slots, terms, MMAX), jnp.float32),
-        in_specs=[pl.BlockSpec(memory_space=pltpu.VMEM)] * 7,
-        out_specs=pl.BlockSpec(memory_space=pltpu.VMEM),
-        scratch_shapes=[pltpu.VMEM(((MMAX + 2) * slots, LANES), jnp.float32)] * (wide // LANES),
-        name="legendre",
+        march_kernel,
+        out_shape=[table] * (wide // LANES),
+        in_specs=[pl.BlockSpec(memory_space=pltpu.VMEM)] * 6,
+        out_specs=[pl.BlockSpec(memory_space=pltpu.VMEM)] * (wide // LANES),
+        cost_estimate=pl.CostEstimate(
+            flops=6 * MMAX * slots * wide, bytes_accessed=16 * MMAX * slots * wide, transcendentals=0
+        ),
+        name="march",
     )(
         grow,
         retreat,
@@ -183,8 +214,22 @@
         jnp.zeros((slots, LANES), jnp.int32),
         jnp.pad(jnp.cos(colatitude)[None, :], pad),
         jnp.pad(diagonal, pad),
-        jnp.pad(fourier, ((0, 0),) + pad),
-    )
+    )
+
+
+def contract_tables(fourier, tables):
+    slots, terms, lats = fourier.shape
+    wide = len(tables) * LANES
+    padded = -(-terms // 16) * 16
+    fourier = jnp.pad(fourier, ((0, 0), (0, padded - terms), (0, wide - lats)))
+    found = pl.pallas_call(
+        contract_kernel,
+        out_shape=jax.ShapeDtypeStruct((slots, padded, MMAX), jnp.float32),
+        in_specs=[pl.BlockSpec(memory_space=pltpu.VMEM)] * (1 + len(tables)),
+        out_specs=pl.BlockSpec(memory_space=pltpu.VMEM),
+        name="contract",
+    )(fourier, *tables)
+    return found[:, :terms]
 
 
 def trig_table(longitudes, wave_numbers):
@@ -227,6 +272,7 @@
     flat = jnp.pad(part.reshape(levels, block_cols), ((0, padded - levels), (0, 0)))
     in_slots = permute(flat, slot_list[None, :])[:levels]
     outgoing = in_slots.reshape(levels, targets, per_target).transpose(1, 0, 2)
+    crm_moisture, outgoing = lax.optimization_barrier((crm_moisture, outgoing))
     arrived = lax.all_to_all(outgoing, ("sec", "lat"), split_axis=0, concat_axis=0, tiled=True)
     arrived = arrived.reshape(sections, lat_bands, levels, per_target).transpose(0, 2, 1, 3)
     arrived = arrived.reshape(sections, levels, run_cols)
@@ -248,12 +294,15 @@
     trig_rows = trig_table(jnp.arange(NLON, dtype=jnp.int32), wave_table)
     spectra = jnp.einsum("lay,ycs->slca", regrouped, trig_rows, precision=lax.Precision.HIGHEST)
     owner_count = MMAX // lat_bands
+    wave_table, _ = lax.optimization_barrier((wave_table, rainfall))
     owned_waves = lax.dynamic_slice_in_dim(
         wave_table, lax.axis_index("lat") * owner_count, owner_count
     )
     gathered = lax.all_to_all(spectra, "lat", split_axis=0, concat_axis=3, tiled=True)
     own_levels = gathered.shape[1]
-    coeffs = legendre(owned_waves, gathered.reshape(owner_count, own_levels * 2, NLAT))
+    coeffs = contract_tables(
+        gathered.reshape(owner_count, own_levels * 2, NLAT), legendre_tables(owned_waves, NLAT)
+    )
     coeffs = coeffs.reshape(owner_count, own_levels, 2, MMAX).transpose(1, 0, 2, 3)
     return (fresh[None, None], coeffs[None, None])
 

time: 275 us -> 221 us (0.80)
  Pallas kernels: 118 us -> 88.6 us
  waiting for transfers between devices: 58.2 us -> 31.1 us
    all_to_all x1, waiting for transfers between devices: 26.2 us -> 6.32 us  [shards(): lax.all_to_all(fresh, 'col', split_axis=0, concat_axis=2, tiled=True)]
    pallas_call x2, Pallas kernels: 59 us -> 42.6 us  [permute(): pl.pallas_call(permute_kernel, out_shape=jax.ShapeDtypeStruct(values.shap...]
    pallas_call x1 -> x2, Pallas kernels: 43.9 us -> 30.7 us  [the longest x1 18.7 us: legendre_tables(): pl.pallas_call(march_kernel, out_shape=[table] * (wide // LANES), in_spec...]
    unnamed x22 -> x21, local copies, waits for them, and re-layouts: 12.2 us -> 5.47 us
    all_to_all x1, waiting for transfers between devices: 16.1 us -> 9.34 us  [shards(): lax.all_to_all(outgoing, ('sec', 'lat'), split_axis=0, concat_axis=0, til...]
    optimization_barrier x0 -> x1, local copies, waits for them, and re-layouts: none -> 6.6 us  [shards(): crm_moisture, outgoing = lax.optimization_barrier((crm_moisture, outgoing))]
  transfers between devices with their start and end apart: 5 -> 5, of which waited for: 4 -> 4; matrix products, arithmetic and copies ran while one was open for 10% -> 13% of each run, Pallas kernels for 0% -> 8%
where the time goes in v2:
time: 221 us; the launch traced here: 220 us
  Pallas kernels  88.6 us (40%)
  local copies, waits for them, and re-layouts  48.6 us (22%)
  waiting for transfers between devices  31.1 us (14%)
  starting transfers between devices  23.5 us (11%)
  other arithmetic  17.9 us (8%)
  matrix products  9.22 us (4%)
    pallas_call x2, Pallas kernels, permute(): pl.pallas_call(permute_kernel, out_shape=jax.ShapeDtypeStruct(values.shap...  42.6 us
    pallas_call x1, Pallas kernels, legendre_tables(): pl.pallas_call(march_kernel, out_shape=[table] * (wide // LANES), in_spec...  18.7 us
    pallas_call x1, Pallas kernels, cloud_model(): pl.pallas_call(cloud_kernel, grid=(width // block,), out_shape=jax.ShapeD...  15.4 us
    pallas_call x1, Pallas kernels, contract_tables(): pl.pallas_call(contract_kernel, out_shape=jax.ShapeDtypeStruct((slots, pa...  12 us
    all_to_all x1, waiting for transfers between devices, shards(): lax.all_to_all(outgoing, ('sec', 'lat'), split_axis=0, concat_axis=0, til...  9.34 us
    all_to_all x1, waiting for transfers between devices, shards(): lax.all_to_all(spectra, 'lat', split_axis=0, concat_axis=3, tiled=True)  8.8 us
    all_to_all x1, starting transfers between devices, shards(): lax.all_to_all(outgoing, ('sec', 'lat'), split_axis=0, concat_axis=0, til...  7.68 us
    all_to_all x1, waiting for transfers between devices, shards(): lax.all_to_all(homeward, ('sec', 'lat'), split_axis=0, concat_axis=0, til...  6.63 us
  transfers between devices with their start and end apart: 5, of which 4 were waited for; matrix products, arithmetic and copies ran while one was open for 13% of the time, Pallas kernels for 8%

profile of v2, /device:TPU:0, one launch (start us, length us, event | category | flops | bytes accessed | tf_op | source)
XLA Modules:
  0.0 219.8 jit_solution(16984336459161654282)
XLA Ops:
  0.7 3.1 %bitcast_select_fusion = f32[28,96,96]{2,1,0:T(8,128)} fusion(f32[1,1,28,96,96]{4,3,2,1,0:T(8,128)} %param.5, f32[1,1,28,96,96]{4,3,2,1,0:T(8,128)} %param.6, pred[]{:T(512)S(6)} %eq.44), kind=kLoop, calls=%fused_computation.10 | loop fusion | flops 258048 | bytes 3096577 | tf_op jit(solution)/shard_map/jit(_where)/select_n | solution.py:268
  3.8 1.7 collective-permute-start
  6.7 2.8 %fusion.2 = f32[28,96,96]{2,1,0:T(8,128)} fusion(f32[28,96,96]{2,1,0:T(8,128)} %collective-permute-done, f32[1,1,28,96,96]{4,3,2,1,0:T(8,128)S(1)} %copy-done, f32[1,1,28,96,96]{4,3,2,1,0:T(8,128)S(1)} %copy-done.1, pred[]{:T(512)S(6)} %eq.44, pred[]{:T(512)S(6)} %eq.45), kind=kLoop, calls=%fused_computation.7 | loop fusion | flops 1290240 | bytes 4128770 | tf_op jit(solution)/shard_map/jit(_where)/select_n | solution.py:269
  9.5 3.2 %reshape.476 = f32[28,9216]{1,0:T(8,128)} reshape(f32[28,96,96]{2,1,0:T(8,128)} %fusion.2) | data formatting | bytes 2064384 | tf_op jit(solution)/shard_map/reshape | solution.py:272
  12.7 2.4 %pad.19.x_ref = f32[32,9216]{1,0:T(8,128)} pad(f32[28,9216]{1,0:T(8,128)} %reshape.476, f32[]{:T(128)} %constant.138.clone.1), padding=0_4x0_0 | pad | bytes 2211844 | tf_op jit(solution)/shard_map/jit(_pad)/pad | solution.py:272
  15.0 21.3 %permute.2 = f32[32,9216]{1,0:T(8,128)} custom-call(f32[32,9216]{1,0:T(8,128)} %pad.19.x_ref, s32[1,9216]{1,0:T(1,128)} %bitcast.108), custom_call_target="tpu_custom_call" | custom-call | tf_op jit(solution)/shard_map/permute/pallas_call | solution.py:61
  36.4 1.5 copy.46
  37.9 1.2 copy.57
  39.1 7.7 %all-to-all-start = ((f32[8,28,1152]{2,1,0:T(8,128)}), f32[8,28,1152]{2,1,0:T(8,128)}, u32[]{:S(2)}, u32[]{:S(2)}) async-start(f32[8,28,1152]{2,1,0:T(8,128)} %bitcast.92), calls=%async_computation | async-start | bytes 2359296 | tf_op jit(solution)/shard_map/all_to_all | solution.py:276
  46.9 6.6 %copy.55 = bf16[1,32,28,1,1,2304]{5,2,1,4,3,0:T(8,128)(2,1)} copy(bf16[1,32,28,1,1,2304]{5,1,4,3,2,0:T(8,128)(2,1)} %param.7) | data formatting | bytes 8257536 | tf_op jit(solution)/shard_map/optimization_barrier | solution.py:275
  53.5 9.3 %all-to-all-done = f32[8,28,1152]{2,1,0:T(8,128)} async-done(((f32[8,28,1152]{2,1,0:T(8,128)}), f32[8,28,1152]{2,1,0:T(8,128)}, u32[]{:S(2)}, u32[]{:S(2)}) %all-to-all-start) | async-done | bytes 1032224 | tf_op jit(solution)/shard_map/all_to_all | solution.py:276
  62.8 2.1 copy.58
  65.1 0.7 copy.49
  65.9 0.7 copy.48
  66.8 0.7 copy.47
  67.5 15.4 %cloud.1 = f32[28,2304]{1,0:T(8,128)} custom-call(f32[28,2304]{1,0:T(8,128)} %bitcast.103, f32[28,2304]{1,0:T(8,128)} %bitcast.102, f32[28,2304]{1,0:T(8,128)} %bitcast.101, bf16[32,28,2304]{2,1,0:T(8,128)(2,1)} %bitcast.86), custom_call_target="tpu_custom_call" | custom-call | tf_op jit(solution)/shard_map/cloud/pallas_call | solution.py:114
  82.8 1.8 reshape.479
  84.6 1.0 copy.33
  85.6 1.1 broadcast_in_dim.74
  86.7 4.4 %all-to-all-start.1 = ((f32[8,28,1152]{2,1,0:T(8,128)}), f32[8,28,1152]{2,1,0:T(8,128)}, u32[]{:S(2)}, u32[]{:S(2)}) async-start(f32[8,28,1152]{2,1,0:T(8,128)} %bitcast.91), calls=%async_computation.1 | async-start | bytes 2359296 | tf_op jit(solution)/shard_map/all_to_all | solution.py:283
  91.2 2.0 broadcast_select_fusion
  93.1 6.5 %fusion.7 = s32[144,128]{1,0:T(8,128)S(1)} fusion(bf16[144,9216]{1,0:T(8,128)(2,1)} %bitcast.98, s32[9216]{0:T(1024)S(1)} %copy-done.3), kind=kOutput, calls=%fused_computation.20 | convolution fusion | flops 340936704 | bytes 2764800 | tf_op jit(solution)/shard_map/dot_general | solution.py:250
  100.3 6.6 %all-to-all-done.1 = f32[8,28,1152]{2,1,0:T(8,128)} async-done(((f32[8,28,1152]{2,1,0:T(8,128)}), f32[8,28,1152]{2,1,0:T(8,128)}, u32[]{:S(2)}, u32[]{:S(2)}) %all-to-all-start.1) | async-done | bytes 1032224 | tf_op jit(solution)/shard_map/all_to_all | solution.py:283
  106.9 1.9 copy.34
  109.1 1.1 pad.20.x_ref
  110.2 21.3 %permute.3 = f32[32,9216]{1,0:T(8,128)} custom-call(f32[32,9216]{1,0:T(8,128)} %pad.20.x_ref, s32[1,9216]{1,0:T(1,128)} %bitcast.110), custom_call_target="tpu_custom_call" | custom-call | tf_op jit(solution)/shard_map/permute/pallas_call | solution.py:61
  131.5 2.9 %reshape.483 = f32[28,96,96]{2,1,0:T(8,128)} reshape(f32[28,9216]{1,0:T(8,128)} %bitcast.87) | data formatting | bytes 2064384 | tf_op jit(solution)/shard_map/reshape | solution.py:287
  134.4 2.8 %bitcast_add_fusion = f32[28,96,96]{2,1,0:T(8,128)} fusion(f32[1,1,28,96,96]{4,3,2,1,0:T(8,128)S(1)} %copy-done, f32[28,96,96]{2,1,0:T(8,128)} %reshape.483, f32[1,1,28,96,96]{4,3,2,1,0:T(8,128)S(1)} %copy-done.1, f32[]{:T(128)S(6)} %select_n.123, pred[]{:T(512)S(6)} %lt.24), kind=kLoop, calls=%fused_computation.9 | loop fusion | flops 1290240 | bytes 4128773 | tf_op jit(solution)/shard_map/add | solution.py:291
  137.2 5.0 %all-to-all-start.2 = ((f32[28,96,96]{2,1,0:T(8,128)}), f32[28,96,96]{2,1,0:T(8,128)}, u32[]{:S(2)}, u32[]{:S(2)}) async-start(f32[28,96,96]{2,1,0:T(8,128)} %bitcast_add_fusion), calls=%async_computation.2 | async-start | bytes 2752512 | tf_op jit(solution)/shard_map/all_to_all | solution.py:293
  142.9 1.5 fusion.18
  144.5 2.9 %reshape.482 = f32[1,1,28,96,96]{4,3,2,1,0:T(8,128)} reshape(f32[28,9216]{1,0:T(8,128)} %bitcast.88) | data formatting | bytes 2064384 | tf_op jit(solution)/shard_map/reshape | solution.py:287
  148.3 0.7 divide_sqrt_fusion
  149.0 0.7 broadcast_in_dim.82.order_ref
  150.3 18.7 %march.1 = (f32[8320,128]{1,0:T(8,128)}, f32[8320,128]{1,0:T(8,128)}) custom-call(f32[64,128]{1,0:T(8,128)} %get-tuple-element.26.grow_ref, f32[64,128]{1,0:T(8,128)} %get-tuple-element.25.retreat_ref, s32[64,128]{1,0:T(8,128)} %broadcast_in_dim.82.order_ref, s32[64,128]{1,0:T(8,128)} %broadcast_in_dim.83.zero_ref, f32[1,256]{1,0:T(1,128)} %pad.22.cosine_ref, ...), custom_call_target="tpu_custom_call" | custom-call | flops 12582912 | bytes 33554432 | tf_op jit(solution)/shard_map/march/pallas_call | solution.py:201
  168.9 6.3 %all-to-all-done.2 = f32[28,96,96]{2,1,0:T(8,128)} async-done(((f32[28,96,96]{2,1,0:T(8,128)}), f32[28,96,96]{2,1,0:T(8,128)}, u32[]{:S(2)}, u32[]{:S(2)}) %all-to-all-start.2) | async-done | bytes 1032224 | tf_op jit(solution)/shard_map/all_to_all | solution.py:293
  175.2 3.3 %copy.56 = f32[4,7,96,96]{3,0,2,1:T(4,128)} copy(f32[4,7,96,96]{3,2,1,0:T(8,128)} %bitcast.15) | data formatting | bytes 2064384 | tf_op jit(solution)/shard_map/all_to_all | solution.py:293
  178.5 2.9 %reshape.487 = f32[7,96,384,1]{2,1,0,3:T(8,128)} reshape(f32[7,96,4,96]{3,2,1,0:T(4,128)} %bitcast.89) | data formatting | bytes 2064384 | tf_op jit(solution)/shard_map/all_to_all | solution.py:293
  181.4 2.7 %convolution_bitcast_fusion = f32[128,7,2,96]{0,3,1,2:T(8,128)S(1)} fusion(f32[7,96,384,1]{2,1,0,3:T(8,128)} %reshape.487, f32[384,1,128]{2,0,1:T(8,128)} %get-tuple-element.28, f32[384,1,128]{2,0,1:T(8,128)} %get-tuple-element.27), kind=kOutput, calls=%fused_computation.18 | convolution fusion | flops 792920064 | bytes 2113536 | tf_op jit(solution)/shard_map/lay,ycs->slca/dot_general | solution.py:295
  184.1 1.4 copy.36
  185.5 4.6 %all-to-all-start.3 = ((f32[128,7,2,96]{3,2,1,0:T(2,128)}), f32[128,7,2,96]{3,2,1,0:T(2,128)}, u32[]{:S(2)}, u32[]{:S(2)}) async-start(f32[128,7,2,96]{3,2,1,0:T(2,128)} %copy.36), calls=%async_computation.3 | async-start | bytes 1835008 | tf_op jit(solution)/shard_map/all_to_all | solution.py:301
  190.2 2.8 %add_add_fusion = f32[1,1,28,96,96]{4,3,2,1,0:T(8,128)} fusion(f32[1,1,28,96,96]{4,3,2,1,0:T(8,128)S(1)} %copy-done, f32[1,1,28,96,96]{4,3,2,1,0:T(8,128)S(1)} %copy-done.1, f32[1,1,28,96,96]{4,3,2,1,0:T(8,128)} %reshape.482, f32[]{:T(128)S(6)} %select_n.123, pred[]{:T(512)S(6)} %lt.24), kind=kLoop, calls=%fused_computation.17 | loop fusion | flops 1290240 | bytes 4128773 | tf_op jit(solution)/shard_map/add | solution.py:291
  193.0 8.8 %all-to-all-done.3 = f32[128,7,2,96]{3,2,1,0:T(2,128)} async-done(((f32[128,7,2,96]{3,2,1,0:T(2,128)}), f32[128,7,2,96]{3,2,1,0:T(2,128)}, u32[]{:S(2)}, u32[]{:S(2)}) %all-to-all-start.3) | async-done | bytes 688160 | tf_op jit(solution)/shard_map/all_to_all | solution.py:301
  201.8 1.3 copy.37
  203.1 0.7 copy.44
  204.4 1.1 pad.21.fourier_ref
  205.5 12.0 %contract.1 = f32[64,16,128]{2,1,0:T(8,128)} custom-call(f32[64,16,256]{2,1,0:T(8,128)} %pad.21.fourier_ref, f32[8320,128]{1,0:T(8,128)} %get-tuple-element.10.refs_0_, f32[8320,128]{1,0:T(8,128)} %get-tuple-element.11.refs_1_), custom_call_target="tpu_custom_call" | custom-call | tf_op jit(solution)/shard_map/contract/pallas_call | solution.py:225
  217.5 1.2 copy.40
  218.7 1.1 copy.41
  (36 shorter events, 5.3 us)
Async XLA Ops:
  0.6 4.9 %copy-start.2 = (s32[1,1,9216]{2,1,0:T(1,128)S(1)}, s32[1,1,9216]{2,1,0:T(1,128)}, u32[]{:S(2)}) copy-start(s32[1,1,9216]{2,1,0:T(1,128)} %param.8) | copy-start | bytes 110596
  0.6 6.0 %copy-start = (f32[1,1,28,96,96]{4,3,2,1,0:T(8,128)S(1)}, f32[1,1,28,96,96]{4,3,2,1,0:T(8,128)}, u32[]{:S(2)}) copy-start(f32[1,1,28,96,96]{4,3,2,1,0:T(8,128)} %param.5) | copy-start | bytes 3096580
  0.7 6.0 %copy-start.1 = (f32[1,1,28,96,96]{4,3,2,1,0:T(8,128)S(1)}, f32[1,1,28,96,96]{4,3,2,1,0:T(8,128)}, u32[]{:S(2)}) copy-start(f32[1,1,28,96,96]{4,3,2,1,0:T(8,128)} %param.6) | copy-start | bytes 3096580
  3.8 2.8 %collective-permute-start = (f32[28,96,96]{2,1,0:T(8,128)}, f32[28,96,96]{2,1,0:T(8,128)}, u32[]{:S(2)}, u32[]{:S(2)}) collective-permute-start(f32[28,96,96]{2,1,0:T(8,128)} %bitcast_select_fusion), channel_id=1, source_target_pairs={{16,24},{24,16},{17,25},{25,17},{18,26},{26,18},{19,27},{27,19},{2... | collective-permute-start | bytes 3096584 | tf_op jit(solution)/shard_map/ppermute | solution.py:268
  39.1 23.7 %all-to-all-start = ((f32[8,28,1152]{2,1,0:T(8,128)}), f32[8,28,1152]{2,1,0:T(8,128)}, u32[]{:S(2)}, u32[]{:S(2)}) async-start(f32[8,28,1152]{2,1,0:T(8,128)} %bitcast.92), calls=%async_computation | async-start | bytes 2359296 | tf_op jit(solution)/shard_map/all_to_all | solution.py:276
  86.7 20.2 %all-to-all-start.1 = ((f32[8,28,1152]{2,1,0:T(8,128)}), f32[8,28,1152]{2,1,0:T(8,128)}, u32[]{:S(2)}, u32[]{:S(2)}) async-start(f32[8,28,1152]{2,1,0:T(8,128)} %bitcast.91), calls=%async_computation.1 | async-start | bytes 2359296 | tf_op jit(solution)/shard_map/all_to_all | solution.py:283
  91.2 2.0 copy-start.3
  137.2 5.7 %copy-start.4 = (s32[128]{0:T(128)S(1)}, s32[128]{0:T(128)}, u32[]{:S(2)}) copy-start(s32[128]{0:T(128)} %param.9) | copy-start | bytes 1540
  137.2 38.0 %all-to-all-start.2 = ((f32[28,96,96]{2,1,0:T(8,128)}), f32[28,96,96]{2,1,0:T(8,128)}, u32[]{:S(2)}, u32[]{:S(2)}) async-start(f32[28,96,96]{2,1,0:T(8,128)} %bitcast_add_fusion), calls=%async_computation.2 | async-start | bytes 2752512 | tf_op jit(solution)/shard_map/all_to_all | solution.py:293
  185.5 16.3 %all-to-all-start.3 = ((f32[128,7,2,96]{3,2,1,0:T(2,128)}), f32[128,7,2,96]{3,2,1,0:T(2,128)}, u32[]{:S(2)}, u32[]{:S(2)}) async-start(f32[128,7,2,96]{3,2,1,0:T(2,128)} %copy.36), calls=%async_computation.3 | async-start | bytes 1835008 | tf_op jit(solution)/shard_map/all_to_all | solution.py:301

commit v3 on v2

--- a/solution.py
+++ b/solution.py
@@ -18,53 +18,84 @@
 CONDENSE = 0.5
 
 
-def permute_kernel(x_ref, order_ref, out_ref, parts):
-    rows, cols = x_ref.shape
+def permute_kernel(x_ref, order_ref, out_ref, parts, held):
+    levels = x_ref.shape[-2]
+    rows = held.shape[0]
+    cols = order_ref.shape[1]
     tiles = cols // LANES
-    width = 2 * LANES if tiles % 2 == 0 else LANES
-    batch = tiles // 3 if tiles % 3 == 0 else tiles
+    gathered = held.shape[1] // LANES
+    multiplied = tiles - gathered
+    halves = 2 if tiles % 2 == 0 else 1
+    width = halves * LANES
+    fill = jnp.zeros((rows - levels, LANES), jnp.float32)
+    groups = range(rows // ROWS)
 
     for s in range(tiles):
-        block = x_ref[:, s * LANES : (s + 1) * LANES]
-        coarse = block.astype(jnp.bfloat16)
-        parts[s * rows : (s + 1) * rows, :LANES] = coarse
-        parts[s * rows : (s + 1) * rows, LANES:] = (block - coarse.astype(jnp.float32)).astype(
-            jnp.bfloat16
-        )
+        if x_ref.ndim == 2:
+            block = x_ref[:, s * LANES : (s + 1) * LANES]
+        else:
+            per = x_ref.shape[2] // LANES
+            block = x_ref[s // per, :, s % per * LANES : (s % per + 1) * LANES]
+        if rows > levels:
+            block = jnp.concatenate([block, fill], axis=0)
+        if s < multiplied:
+            coarse = block.astype(jnp.bfloat16)
+            parts[s * rows : (s + 1) * rows, :LANES] = coarse
+            parts[s * rows : (s + 1) * rows, LANES:] = (
+                block - coarse.astype(jnp.float32)
+            ).astype(jnp.bfloat16)
+        else:
+            held[:, (s - multiplied) * LANES : (s - multiplied + 1) * LANES] = block
     wanted = lax.broadcasted_iota(jnp.int32, (2 * LANES, width), 0) & (LANES - 1)
 
     def one(t, carry):
-        at = pl.ds(pl.multiple_of(t * width, width), width)
-        order = order_ref[:, at]
-        source = jnp.broadcast_to(order >> 7, (ROWS, width))
-        chosen = jnp.where(wanted == (order & (LANES - 1)), 1.0, 0.0).astype(jnp.bfloat16)
-        total = [jnp.zeros((ROWS, width), jnp.float32) for _ in range(rows // ROWS)]
-        for first in range(0, tiles, batch):
-            moved = jnp.dot(
-                parts[first * rows : (first + batch) * rows, :],
-                chosen,
-                preferred_element_type=jnp.float32,
-            )
-            for s in range(batch):
-                hit = source == first + s
-                for r in range(rows // ROWS):
+        order = order_ref[:, pl.ds(pl.multiple_of(t * width, width), width)]
+        lane = order & (LANES - 1)
+        chosen = jnp.where(wanted == lane, 1.0, 0.0).astype(jnp.bfloat16)
+        moved = jnp.dot(parts[...], chosen, preferred_element_type=jnp.float32)
+        for h in range(halves):
+            mine = slice(h * LANES, (h + 1) * LANES)
+            source = jnp.broadcast_to(order[:, mine] >> 7, (ROWS, LANES))
+            lanes = jnp.broadcast_to(lane[:, mine], (ROWS, LANES))
+            total = [jnp.zeros((ROWS, LANES), jnp.float32) for _ in groups]
+            for s in range(gathered):
+                hit = source == multiplied + s
+                for r in groups:
+                    block = held[r * ROWS : (r + 1) * ROWS, s * LANES : (s + 1) * LANES]
+                    total[r] = jnp.where(hit, jnp.take_along_axis(block, lanes, axis=1), total[r])
+            for s in range(multiplied):
+                hit = source == s
+                for r in groups:
                     begin = s * rows + r * ROWS
-                    total[r] = jnp.where(hit, moved[begin : begin + ROWS], total[r])
-        for r in range(rows // ROWS):
-            out_ref[r * ROWS : (r + 1) * ROWS, at] = total[r]
+                    total[r] = jnp.where(hit, moved[begin : begin + ROWS, mine], total[r])
+            tile = t * halves + h
+            for r in groups:
+                end = min((r + 1) * ROWS, levels)
+                value = total[r][: end - r * ROWS]
+                if out_ref.ndim == 2:
+                    at = pl.ds(pl.multiple_of(tile * LANES, LANES), LANES)
+                    out_ref[r * ROWS : end, at] = value
+                else:
+                    per = out_ref.shape[2] // LANES
+                    at = pl.ds(pl.multiple_of(tile % per * LANES, LANES), LANES)
+                    out_ref[tile // per, r * ROWS : end, at] = value
         return carry
 
-    lax.fori_loop(0, cols // width, one, 0)
-
-
-def permute(values, order):
+    lax.fori_loop(0, tiles // halves, one, 0)
+
+
+def permute(values, order, shape):
+    levels, tiles = values.shape[-2], order.shape[1] // LANES
+    rows = -(-levels // ROWS) * ROWS
+    gathered = tiles * 3 // 8
     return pl.pallas_call(
         permute_kernel,
-        out_shape=jax.ShapeDtypeStruct(values.shape, jnp.float32),
+        out_shape=jax.ShapeDtypeStruct(shape, jnp.float32),
         in_specs=[pl.BlockSpec(memory_space=pltpu.VMEM)] * 2,
         out_specs=pl.BlockSpec(memory_space=pltpu.VMEM),
         scratch_shapes=[
-            pltpu.VMEM((values.shape[0] * values.shape[1] // LANES, 2 * LANES), jnp.bfloat16)
+            pltpu.VMEM(((tiles - gathered) * rows, 2 * LANES), jnp.bfloat16),
+            pltpu.VMEM((rows, gathered * LANES), jnp.float32),
         ],
         name="permute",
     )(values, order)
@@ -104,21 +135,39 @@
                                 + (keep * gap[n] + (push - wet))
                             )
                     gap = fresh
-                rain_ref[r0:r1, c0:c1] = scale * (rain[0] + rain[1])
-
-
-def cloud_model(wind, gap, push, anomaly):
-    count, levels, width = anomaly.shape
-    block = LANES if width % LANES == 0 else width
-    flat = pl.BlockSpec((levels, block), lambda i: (0, i))
-    return pl.pallas_call(
+                found = scale * (rain[0] + rain[1])
+                for copy in range(rain_ref.shape[0]):
+                    rain_ref[copy, r0:r1, c0:c1] = found
+
+
+def cloud_model(arrived, anomaly, sections):
+    count, levels, _ = anomaly.shape
+    blocks, _, span = arrived.shape
+    bands = blocks // sections
+    block = LANES if span % LANES == 0 else span
+    steps = span // block
+    if block < LANES:
+        anomaly = anomaly.reshape(count, levels, bands, span).transpose(2, 0, 1, 3)
+        moist = pl.BlockSpec((None, count, levels, span), lambda i: (i, 0, 0, 0))
+    else:
+        moist = pl.BlockSpec((count, levels, block), lambda i: (0, 0, i))
+
+    def of(field):
+        return pl.BlockSpec(
+            (None, levels, block), lambda i: (field * bands + i // steps, 0, i % steps)
+        )
+
+    found = pl.pallas_call(
         cloud_kernel,
-        grid=(width // block,),
-        out_shape=jax.ShapeDtypeStruct((levels, width), jnp.float32),
-        in_specs=[flat, flat, flat, pl.BlockSpec((count, levels, block), lambda i: (0, 0, i))],
-        out_specs=flat,
+        grid=(bands * steps,),
+        out_shape=jax.ShapeDtypeStruct((sections, bands, levels, span), jnp.float32),
+        in_specs=[of(0), of(2), of(3), moist],
+        out_specs=pl.BlockSpec(
+            (sections, None, levels, block), lambda i: (0, i // steps, 0, i % steps)
+        ),
         name="cloud",
-    )(wind, gap, push, anomaly)
+    )(arrived, arrived, arrived, anomaly)
+    return found.reshape(arrived.shape)
 
 
 def march_kernel(grow_ref, retreat_ref, order_ref, zero_ref, cosine_ref, diag_ref, *tables):
@@ -130,21 +179,32 @@
     cosine = [cosine_ref[:, h * LANES : (h + 1) * LANES] for h in range(halves)]
     for h in range(halves):
         tables[h][: 2 * slots, :] = jnp.zeros((2 * slots, LANES), jnp.float32)
-
-    def march(n, carry):
-        index = zero_ref[...] + n
-        grow_n = jnp.take_along_axis(grow, index, axis=1)
-        retreat_n = jnp.take_along_axis(retreat, index, axis=1)
-        first = order == n
-        for h in range(halves):
-            previous = tables[h][pl.ds(pl.multiple_of(n * slots, ROWS), slots), :]
-            current = tables[h][pl.ds(pl.multiple_of((n + 1) * slots, ROWS), slots), :]
-            grown = grow_n * (cosine[h] * current - retreat_n * previous)
-            fresh = jnp.where(first, diag_ref[:, h * LANES : (h + 1) * LANES], grown)
-            tables[h][pl.ds(pl.multiple_of((n + 2) * slots, ROWS), slots), :] = fresh
+    group = 8
+
+    def march(g, carry):
+        begin = g * group
+        held = [
+            [
+                tables[h][pl.ds(pl.multiple_of((begin + j) * slots, ROWS), slots), :]
+                for j in range(2)
+            ]
+            for h in range(halves)
+        ]
+        for j in range(group):
+            n = begin + j
+            index = zero_ref[...] + n
+            grow_n = jnp.take_along_axis(grow, index, axis=1)
+            retreat_n = jnp.take_along_axis(retreat, index, axis=1)
+            first = order == n
+            for h in range(halves):
+                previous, current = held[h]
+                grown = grow_n * (cosine[h] * current - retreat_n * previous)
+                fresh = jnp.where(first, diag_ref[:, h * LANES : (h + 1) * LANES], grown)
+                tables[h][pl.ds(pl.multiple_of((n + 2) * slots, ROWS), slots), :] = fresh
+                held[h] = [current, fresh]
         return carry
 
-    lax.fori_loop(0, MMAX, march, 0)
+    lax.fori_loop(0, MMAX // group, march, 0)
 
 
 def contract_kernel(fourier_ref, *refs):
@@ -259,8 +319,6 @@
     block_cols = band_rows * lon_block
     targets = sections * lat_bands
     per_target = block_cols // targets
-    run_cols = lat_bands * per_target
-    padded = -(-levels // ROWS) * ROWS
     field = lax.axis_index("sec")
     slot_list = cloud_order[0, 0]
     own, force = state[0, 0], forcing[0, 0]
@@ -269,21 +327,21 @@
     part = jnp.where(
         field == 3, (force - mate) / NSUB, jnp.where(field == 2, mate - own, own)
     )
-    flat = jnp.pad(part.reshape(levels, block_cols), ((0, padded - levels), (0, 0)))
-    in_slots = permute(flat, slot_list[None, :])[:levels]
-    outgoing = in_slots.reshape(levels, targets, per_target).transpose(1, 0, 2)
+    flat = part.reshape(levels, block_cols)
+    cut = (targets, levels, per_target)
+    tiled = per_target % LANES == 0
+    if tiled:
+        outgoing = permute(flat, slot_list[None, :], cut)
+    else:
+        in_slots = permute(flat, slot_list[None, :], flat.shape)
+        outgoing = in_slots.reshape(levels, targets, per_target).transpose(1, 0, 2)
     crm_moisture, outgoing = lax.optimization_barrier((crm_moisture, outgoing))
     arrived = lax.all_to_all(outgoing, ("sec", "lat"), split_axis=0, concat_axis=0, tiled=True)
-    arrived = arrived.reshape(sections, lat_bands, levels, per_target).transpose(0, 2, 1, 3)
-    arrived = arrived.reshape(sections, levels, run_cols)
-    rain = cloud_model(arrived[0], arrived[2], arrived[3], crm_moisture[0, :, :, 0, 0, :])
-    homeward = rain.reshape(levels, lat_bands, per_target).transpose(1, 0, 2)
-    homeward = jnp.broadcast_to(homeward[None], (sections, lat_bands, levels, per_target))
-    homeward = homeward.reshape(targets, levels, per_target)
+    homeward = cloud_model(arrived, crm_moisture[0, :, :, 0, 0, :], sections)
     returned = lax.all_to_all(homeward, ("sec", "lat"), split_axis=0, concat_axis=0, tiled=True)
-    returned = returned.transpose(1, 0, 2).reshape(levels, block_cols)
-    returned = jnp.pad(returned, ((0, padded - levels), (0, 0)))
-    rainfall = permute(returned, inverse_order(slot_list)[None, :])[:levels]
+    if not tiled:
+        returned = returned.transpose(1, 0, 2).reshape(levels, block_cols)
+    rainfall = permute(returned, inverse_order(slot_list)[None, :], flat.shape)
     rainfall = rainfall.reshape(levels, band_rows, lon_block)
     share = jnp.where(
         field < 2, own * (-1.0 / NSUB), jnp.where(field == 2, jnp.float32(1), jnp.float32(-1))

time: 221 us -> 195 us (0.88)
  local copies, waits for them, and re-layouts: 48.6 us -> 31.8 us
  Pallas kernels: 88.6 us -> 72.2 us
  waiting for transfers between devices: 31.1 us -> 38.9 us
    pallas_call x3, Pallas kernels: 58 us -> 49.1 us  [the longest x2 33.4 us: permute(): pl.pallas_call(permute_kernel, out_shape=jax.ShapeDtypeStruct(shape, jnp....]
    pallas_call x1, Pallas kernels: 18.7 us -> 11.2 us  [legendre_tables(): pl.pallas_call(march_kernel, out_shape=[table] * (wide // LANES), in_spec...]
    all_to_all x1, waiting for transfers between devices: 6.32 us -> 13.8 us  [shards(): lax.all_to_all(fresh, 'col', split_axis=0, concat_axis=2, tiled=True)]
    reshape x5 -> x1, local copies, waits for them, and re-layouts: 8.35 us -> 3.2 us  [shards(): flat = part.reshape(levels, block_cols)]
    unnamed x21 -> x11, local copies, waits for them, and re-layouts: 5.47 us -> 1.15 us
    pad x2 -> x0, local copies, waits for them, and re-layouts: 3.45 us -> none  [the longest x1 2.36 us: shards(): jnp.pad(part.reshape(levels, block_cols), ((0, padded - levels), (0, 0)))]
    transpose x2 -> x0, local copies, waits for them, and re-layouts: 2.84 us -> none  [the longest x1 1.87 us: shards(): returned = returned.transpose(1, 0, 2).reshape(levels, block_cols)]
  transfers between devices with their start and end apart: 5 -> 5, of which waited for: 4 -> 4; matrix products, arithmetic and copies ran while one was open for 13% -> 14% of each run, Pallas kernels for 8% -> 6%
where the time goes in v3:
time: 195 us; the launch traced here: 194 us
  Pallas kernels  72.2 us (37%)
  waiting for transfers between devices  38.9 us (20%)
  local copies, waits for them, and re-layouts  31.8 us (16%)
  starting transfers between devices  23.1 us (12%)
  other arithmetic  17.9 us (9%)
  matrix products  9.22 us (5%)
    pallas_call x2, Pallas kernels, permute(): pl.pallas_call(permute_kernel, out_shape=jax.ShapeDtypeStruct(shape, jnp....  33.4 us
    pallas_call x1, Pallas kernels, cloud_model(): pl.pallas_call(cloud_kernel, grid=(bands * steps,), out_shape=jax.ShapeDt...  15.7 us
    all_to_all x1, waiting for transfers between devices, shards(): lax.all_to_all(fresh, 'col', split_axis=0, concat_axis=2, tiled=True)  13.8 us
    pallas_call x1, Pallas kernels, contract_tables(): pl.pallas_call(contract_kernel, out_shape=jax.ShapeDtypeStruct((slots, pa...  12 us
    pallas_call x1, Pallas kernels, legendre_tables(): pl.pallas_call(march_kernel, out_shape=[table] * (wide // LANES), in_spec...  11.2 us
    all_to_all x1, waiting for transfers between devices, shards(): lax.all_to_all(outgoing, ('sec', 'lat'), split_axis=0, concat_axis=0, til...  9.34 us
    all_to_all x1, waiting for transfers between devices, shards(): lax.all_to_all(spectra, 'lat', split_axis=0, concat_axis=3, tiled=True)  9.02 us
    all_to_all x1, starting transfers between devices, shards(): lax.all_to_all(outgoing, ('sec', 'lat'), split_axis=0, concat_axis=0, til...  7.69 us
  transfers between devices with their start and end apart: 5, of which 4 were waited for; matrix products, arithmetic and copies ran while one was open for 14% of the time, Pallas kernels for 6%

profile of v3, /device:TPU:0, one launch (start us, length us, event | category | flops | bytes accessed | tf_op | source)
XLA Modules:
  0.0 194.0 jit_solution(4394350886261268898)
XLA Ops:
  0.7 3.1 %bitcast_select_fusion = f32[28,96,96]{2,1,0:T(8,128)} fusion(f32[1,1,28,96,96]{4,3,2,1,0:T(8,128)} %param.5, f32[1,1,28,96,96]{4,3,2,1,0:T(8,128)} %param.6, pred[]{:T(512)S(6)} %eq.44), kind=kLoop, calls=%fused_computation.10 | loop fusion | flops 258048 | bytes 3096577 | tf_op jit(solution)/shard_map/jit(_where)/select_n | solution.py:326
  3.8 1.8 collective-permute-start
  5.6 0.7 add_select_fusion.1
  6.2 0.3 iota_compare_fusion.2
  6.6 0.1 fusion.20
  6.7 2.8 %fusion.2 = f32[28,96,96]{2,1,0:T(8,128)} fusion(f32[28,96,96]{2,1,0:T(8,128)} %collective-permute-done, f32[1,1,28,96,96]{4,3,2,1,0:T(8,128)S(1)} %copy-done, f32[1,1,28,96,96]{4,3,2,1,0:T(8,128)S(1)} %copy-done.1, pred[]{:T(512)S(6)} %eq.44, pred[]{:T(512)S(6)} %eq.45), kind=kLoop, calls=%fused_computation.7 | loop fusion | flops 1290240 | bytes 4128770 | tf_op jit(solution)/shard_map/jit(_where)/select_n | solution.py:327
  9.5 3.2 %reshape.456.x_ref = f32[28,9216]{1,0:T(8,128)} reshape(f32[28,96,96]{2,1,0:T(8,128)} %fusion.2) | data formatting | bytes 2064384 | tf_op jit(solution)/shard_map/reshape | solution.py:330
  12.7 16.7 %permute.2 = f32[8,28,1152]{2,1,0:T(8,128)} custom-call(f32[28,9216]{1,0:T(8,128)} %reshape.456.x_ref, s32[1,9216]{1,0:T(1,128)} %bitcast.58), custom_call_target="tpu_custom_call" | custom-call | tf_op jit(solution)/shard_map/permute/pallas_call | solution.py:91
  29.4 7.7 %all-to-all-start = ((f32[8,28,1152]{2,1,0:T(8,128)}), f32[8,28,1152]{2,1,0:T(8,128)}, u32[]{:S(2)}, u32[]{:S(2)}) async-start(f32[8,28,1152]{2,1,0:T(8,128)} %permute.2), calls=%async_computation | async-start | bytes 2359296 | tf_op jit(solution)/shard_map/all_to_all | solution.py:339
  37.1 0.1 pad_maximum_fusion
  37.2 6.6 %copy.39 = bf16[1,32,28,1,1,2304]{5,2,1,4,3,0:T(8,128)(2,1)} copy(bf16[1,32,28,1,1,2304]{5,1,4,3,2,0:T(8,128)(2,1)} %param.7) | data formatting | bytes 8257536 | tf_op jit(solution)/shard_map/optimization_barrier | solution.py:338
  43.8 9.3 %all-to-all-done.wind_ref.gap_ref.push_ref = f32[8,28,1152]{2,1,0:T(8,128)} async-done(((f32[8,28,1152]{2,1,0:T(8,128)}), f32[8,28,1152]{2,1,0:T(8,128)}, u32[]{:S(2)}, u32[]{:S(2)}) %all-to-all-start) | async-done | bytes 1032224 | tf_op jit(solution)/shard_map/all_to_all | solution.py:339
  53.1 15.7 %cloud.1 = f32[4,2,28,1152]{3,2,1,0:T(8,128)} custom-call(f32[8,28,1152]{2,1,0:T(8,128)} %all-to-all-done.wind_ref.gap_ref.push_ref, f32[8,28,1152]{2,1,0:T(8,128)} %all-to-all-done.wind_ref.gap_ref.push_ref, f32[8,28,1152]{2,1,0:T(8,128)} %all-to-all-done.wind_ref.gap_ref.push_ref, bf16[32,28,2304]{2,1,0:T(8,128)(2,1)} %bitcast.51), custom_call_target="tpu_custom_call" | custom-call | tf_op jit(solution)/shard_map/cloud/pallas_call | solution.py:160
  68.8 4.3 %all-to-all-start.1 = ((f32[8,28,1152]{2,1,0:T(8,128)}), f32[8,28,1152]{2,1,0:T(8,128)}, u32[]{:S(2)}, u32[]{:S(2)}) async-start(f32[8,28,1152]{2,1,0:T(8,128)} %bitcast.53), calls=%async_computation.1 | async-start | bytes 2359296 | tf_op jit(solution)/shard_map/all_to_all | solution.py:341
  73.1 2.0 %broadcast_select_fusion = bf16[2,72,9216]{2,1,0:T(8,128)(2,1)} fusion(pred[72,9216]{1,0:T(8,128)(4,1)S(1)} %iota_compare_fusion.2, bf16[2,9216]{1,0:T(2,128)(2,1)S(1)} %pad_maximum_fusion), kind=kLoop, calls=%fused_computation.4 | loop fusion | flops 1327104 | bytes 3354624 | tf_op jit(solution)/shard_map/jit(_where)/select_n | solution.py:309
  75.0 6.5 %fusion.7 = s32[144,128]{1,0:T(8,128)S(1)} fusion(bf16[144,9216]{1,0:T(8,128)(2,1)} %bitcast.55, s32[9216]{0:T(1024)S(1)} %copy-done.3), kind=kOutput, calls=%fused_computation.19 | convolution fusion | flops 340936704 | bytes 2764800 | tf_op jit(solution)/shard_map/dot_general | solution.py:310
  81.5 0.6 slice_add_fusion
  82.2 6.8 %all-to-all-done.1.x_ref = f32[8,28,1152]{2,1,0:T(8,128)} async-done(((f32[8,28,1152]{2,1,0:T(8,128)}), f32[8,28,1152]{2,1,0:T(8,128)}, u32[]{:S(2)}, u32[]{:S(2)}) %all-to-all-start.1) | async-done | bytes 1032224 | tf_op jit(solution)/shard_map/all_to_all | solution.py:341
  89.0 16.7 %permute.3 = f32[28,9216]{1,0:T(8,128)} custom-call(f32[8,28,1152]{2,1,0:T(8,128)} %all-to-all-done.1.x_ref, s32[1,9216]{1,0:T(1,128)} %bitcast.60), custom_call_target="tpu_custom_call" | custom-call | tf_op jit(solution)/shard_map/permute/pallas_call | solution.py:91
  105.7 2.9 %reshape.459 = f32[28,96,96]{2,1,0:T(8,128)} reshape(f32[28,9216]{1,0:T(8,128)} %permute.3) | data formatting | bytes 2064384 | tf_op jit(solution)/shard_map/reshape | solution.py:345
  108.6 2.8 %bitcast_add_fusion = f32[28,96,96]{2,1,0:T(8,128)} fusion(f32[1,1,28,96,96]{4,3,2,1,0:T(8,128)S(1)} %copy-done, f32[28,96,96]{2,1,0:T(8,128)} %reshape.459, f32[1,1,28,96,96]{4,3,2,1,0:T(8,128)S(1)} %copy-done.1, f32[]{:T(128)S(6)} %select_n.123, pred[]{:T(512)S(6)} %lt.24), kind=kLoop, calls=%fused_computation.9 | loop fusion | flops 1290240 | bytes 4128773 | tf_op jit(solution)/shard_map/add | solution.py:349
  111.4 5.0 %all-to-all-start.2 = ((f32[28,96,96]{2,1,0:T(8,128)}), f32[28,96,96]{2,1,0:T(8,128)}, u32[]{:S(2)}, u32[]{:S(2)}) async-start(f32[28,96,96]{2,1,0:T(8,128)} %bitcast_add_fusion), calls=%async_computation.2 | async-start | bytes 2752512 | tf_op jit(solution)/shard_map/all_to_all | solution.py:351
  116.4 0.1 multiply_cosine_fusion
  116.4 0.6 pad.13.cosine_ref
  117.1 1.5 fusion.18
  118.6 2.9 %reshape.458 = f32[1,1,28,96,96]{4,3,2,1,0:T(8,128)} reshape(f32[28,9216]{1,0:T(8,128)} %permute.3) | data formatting | bytes 2064384 | tf_op jit(solution)/shard_map/reshape | solution.py:345
  121.5 0.1 subtract_multiply_fusion
  121.7 0.1 exponential_multiply_fusion
  121.8 0.6 pad.14.diag_ref
  122.4 0.7 divide_sqrt_fusion
  123.2 0.7 broadcast_in_dim.75.order_ref
  123.9 0.6 broadcast_in_dim.76.zero_ref
  124.5 11.2 %march.1 = (f32[8320,128]{1,0:T(8,128)}, f32[8320,128]{1,0:T(8,128)}) custom-call(f32[64,128]{1,0:T(8,128)} %get-tuple-element.23.grow_ref, f32[64,128]{1,0:T(8,128)} %get-tuple-element.22.retreat_ref, s32[64,128]{1,0:T(8,128)} %broadcast_in_dim.75.order_ref, s32[64,128]{1,0:T(8,128)} %broadcast_in_dim.76.zero_ref, f32[1,256]{1,0:T(1,128)} %pad.13.cosine_ref, ...), custom_call_target="tpu_custom_call" | custom-call | flops 12582912 | bytes 33554432 | tf_op jit(solution)/shard_map/march/pallas_call | solution.py:261
  135.6 13.8 %all-to-all-done.2 = f32[28,96,96]{2,1,0:T(8,128)} async-done(((f32[28,96,96]{2,1,0:T(8,128)}), f32[28,96,96]{2,1,0:T(8,128)}, u32[]{:S(2)}, u32[]{:S(2)}) %all-to-all-start.2) | async-done | bytes 1032224 | tf_op jit(solution)/shard_map/all_to_all | solution.py:351
  149.4 3.3 %copy.40 = f32[4,7,96,96]{3,0,2,1:T(4,128)} copy(f32[4,7,96,96]{3,2,1,0:T(8,128)} %bitcast.10) | data formatting | bytes 2064384 | tf_op jit(solution)/shard_map/all_to_all | solution.py:351
  152.7 2.9 %reshape.463 = f32[7,96,384,1]{2,1,0,3:T(8,128)} reshape(f32[7,96,4,96]{3,2,1,0:T(4,128)} %bitcast.52) | data formatting | bytes 2064384 | tf_op jit(solution)/shard_map/all_to_all | solution.py:351
  155.6 2.7 %convolution_bitcast_fusion = f32[128,7,2,96]{0,3,1,2:T(8,128)S(1)} fusion(f32[7,96,384,1]{2,1,0,3:T(8,128)} %reshape.463, f32[384,1,128]{2,0,1:T(8,128)} %get-tuple-element.25, f32[384,1,128]{2,0,1:T(8,128)} %get-tuple-element.24), kind=kOutput, calls=%fused_computation.18 | convolution fusion | flops 792920064 | bytes 2113536 | tf_op jit(solution)/shard_map/lay,ycs->slca/dot_general | solution.py:353
  158.3 1.4 copy.28
  159.7 4.4 %all-to-all-start.3 = ((f32[128,7,2,96]{3,2,1,0:T(2,128)}), f32[128,7,2,96]{3,2,1,0:T(2,128)}, u32[]{:S(2)}, u32[]{:S(2)}) async-start(f32[128,7,2,96]{3,2,1,0:T(2,128)} %copy.28), calls=%async_computation.3 | async-start | bytes 1835008 | tf_op jit(solution)/shard_map/all_to_all | solution.py:359
  164.1 2.8 %add_add_fusion = f32[1,1,28,96,96]{4,3,2,1,0:T(8,128)} fusion(f32[1,1,28,96,96]{4,3,2,1,0:T(8,128)S(1)} %copy-done, f32[1,1,28,96,96]{4,3,2,1,0:T(8,128)S(1)} %copy-done.1, f32[1,1,28,96,96]{4,3,2,1,0:T(8,128)} %reshape.458, f32[]{:T(128)S(6)} %select_n.123, pred[]{:T(512)S(6)} %lt.24), kind=kLoop, calls=%fused_computation.17 | loop fusion | flops 1290240 | bytes 4128773 | tf_op jit(solution)/shard_map/add | solution.py:349
  166.9 9.0 %all-to-all-done.3 = f32[128,7,2,96]{3,2,1,0:T(2,128)} async-done(((f32[128,7,2,96]{3,2,1,0:T(2,128)}), f32[128,7,2,96]{3,2,1,0:T(2,128)}, u32[]{:S(2)}, u32[]{:S(2)}) %all-to-all-start.3) | async-done | bytes 688160 | tf_op jit(solution)/shard_map/all_to_all | solution.py:359
  176.0 1.3 copy.29
  177.2 0.7 copy.35
  178.0 0.6 reshape.465
  178.5 1.2 pad.12.fourier_ref
  179.7 12.0 %contract.1 = f32[64,16,128]{2,1,0:T(8,128)} custom-call(f32[64,16,256]{2,1,0:T(8,128)} %pad.12.fourier_ref, f32[8320,128]{1,0:T(8,128)} %get-tuple-element.10.refs_0_, f32[8320,128]{1,0:T(8,128)} %get-tuple-element.11.refs_1_), custom_call_target="tpu_custom_call" | custom-call | tf_op jit(solution)/shard_map/contract/pallas_call | solution.py:285
  191.7 1.2 copy.32
  192.9 1.1 copy.33
  (17 shorter events, 0.1 us)
Async XLA Ops:
  0.6 4.9 %copy-start.2 = (s32[1,1,9216]{2,1,0:T(1,128)S(1)}, s32[1,1,9216]{2,1,0:T(1,128)}, u32[]{:S(2)}) copy-start(s32[1,1,9216]{2,1,0:T(1,128)} %param.8) | copy-start | bytes 110596
  0.6 6.0 %copy-start = (f32[1,1,28,96,96]{4,3,2,1,0:T(8,128)S(1)}, f32[1,1,28,96,96]{4,3,2,1,0:T(8,128)}, u32[]{:S(2)}) copy-start(f32[1,1,28,96,96]{4,3,2,1,0:T(8,128)} %param.5) | copy-start | bytes 3096580
  0.7 6.0 %copy-start.1 = (f32[1,1,28,96,96]{4,3,2,1,0:T(8,128)S(1)}, f32[1,1,28,96,96]{4,3,2,1,0:T(8,128)}, u32[]{:S(2)}) copy-start(f32[1,1,28,96,96]{4,3,2,1,0:T(8,128)} %param.6) | copy-start | bytes 3096580
  3.8 2.9 %collective-permute-start = (f32[28,96,96]{2,1,0:T(8,128)}, f32[28,96,96]{2,1,0:T(8,128)}, u32[]{:S(2)}, u32[]{:S(2)}) collective-permute-start(f32[28,96,96]{2,1,0:T(8,128)} %bitcast_select_fusion), channel_id=1, source_target_pairs={{16,24},{24,16},{17,25},{25,17},{18,26},{26,18},{19,27},{27,19},{2... | collective-permute-start | bytes 3096584 | tf_op jit(solution)/shard_map/ppermute | solution.py:326
  29.4 23.7 %all-to-all-start = ((f32[8,28,1152]{2,1,0:T(8,128)}), f32[8,28,1152]{2,1,0:T(8,128)}, u32[]{:S(2)}, u32[]{:S(2)}) async-start(f32[8,28,1152]{2,1,0:T(8,128)} %permute.2), calls=%async_computation | async-start | bytes 2359296 | tf_op jit(solution)/shard_map/all_to_all | solution.py:339
  68.8 20.2 %all-to-all-start.1 = ((f32[8,28,1152]{2,1,0:T(8,128)}), f32[8,28,1152]{2,1,0:T(8,128)}, u32[]{:S(2)}, u32[]{:S(2)}) async-start(f32[8,28,1152]{2,1,0:T(8,128)} %bitcast.53), calls=%async_computation.1 | async-start | bytes 2359296 | tf_op jit(solution)/shard_map/all_to_all | solution.py:341
  73.0 2.0 %copy-start.3 = (s32[9216]{0:T(1024)S(1)}, s32[9216]{0:T(1024)}, u32[]{:S(2)}) copy-start(s32[9216]{0:T(1024)} %get-tuple-element.20) | copy-start | bytes 110596
  111.4 5.7 %copy-start.4 = (s32[128]{0:T(128)S(1)}, s32[128]{0:T(128)}, u32[]{:S(2)}) copy-start(s32[128]{0:T(128)} %param.9) | copy-start | bytes 1540
  111.4 38.0 %all-to-all-start.2 = ((f32[28,96,96]{2,1,0:T(8,128)}), f32[28,96,96]{2,1,0:T(8,128)}, u32[]{:S(2)}, u32[]{:S(2)}) async-start(f32[28,96,96]{2,1,0:T(8,128)} %bitcast_add_fusion), calls=%async_computation.2 | async-start | bytes 2752512 | tf_op jit(solution)/shard_map/all_to_all | solution.py:351
  159.7 16.3 %all-to-all-start.3 = ((f32[128,7,2,96]{3,2,1,0:T(2,128)}), f32[128,7,2,96]{3,2,1,0:T(2,128)}, u32[]{:S(2)}, u32[]{:S(2)}) async-start(f32[128,7,2,96]{3,2,1,0:T(2,128)} %copy.28), calls=%async_computation.3 | async-start | bytes 1835008 | tf_op jit(solution)/shard_map/all_to_all | solution.py:359

commit v4 on v3

--- a/solution.py
+++ b/solution.py
@@ -170,7 +170,14 @@
     return found.reshape(arrived.shape)
 
 
-def march_kernel(grow_ref, retreat_ref, order_ref, zero_ref, cosine_ref, diag_ref, *tables):
+def halve(values):
+    coarse = values.astype(jnp.bfloat16)
+    return coarse, (values - coarse.astype(jnp.float32)).astype(jnp.bfloat16)
+
+
+def march_kernel(
+    grow_ref, retreat_ref, order_ref, zero_ref, cosine_ref, diag_ref, coarse_ref, fine_ref, *tables
+):
     slots = order_ref.shape[0]
     halves = len(tables)
     order = order_ref[...]
@@ -206,15 +213,23 @@
 
     lax.fori_loop(0, MMAX // group, march, 0)
 
-
-def contract_kernel(fourier_ref, *refs):
-    *tables, out_ref = refs
-    slots, terms, _ = fourier_ref.shape
-    group = 4 if slots % 4 == 0 else 1
-
-    def split(values):
-        coarse = values.astype(jnp.bfloat16)
-        return coarse, (values - coarse.astype(jnp.float32)).astype(jnp.bfloat16)
+    def sort(g, carry):
+        for j in range(4):
+            s = g * 4 + j
+            for h in range(halves):
+                rows = tables[h][pl.ds(2 * slots + s, MMAX, stride=slots), :]
+                mine = slice(h * LANES, (h + 1) * LANES)
+                coarse_ref[s, :, mine], fine_ref[s, :, mine] = halve(rows)
+        return carry
+
+    lax.fori_loop(0, slots // 4, sort, 0)
+
+
+def contract_kernel(fourier_ref, coarse_ref, fine_ref, out_ref):
+    levels, slots, _, _ = out_ref.shape
+    bands = fourier_ref.shape[0]
+    terms = 2 * levels
+    rows = -(-terms // 16) * 16
 
     def product(left, right):
         return lax.dot_general(
@@ -222,23 +237,79 @@
         )
 
     def contract(g, carry):
-        for j in range(group):
-            s = g * group + j
-            weighted = jnp.concatenate(
-                [table[pl.ds(2 * slots + s, MMAX, stride=slots), :] for table in tables], axis=1
-            )
-            coarse, fine = split(weighted)
-            head, rest = split(fourier_ref[s])
-            main = product(jnp.concatenate([head, rest], axis=0), coarse)
-            out_ref[s] = main[:terms] + main[terms:] + product(head, fine)
+        for j in range(4):
+            s = g * 4 + j
+            found = [fourier_ref[b, pl.ds(s, terms, stride=slots), :] for b in range(bands)]
+            found = jnp.concatenate(found, axis=1)
+            if rows > terms:
+                fill = jnp.zeros((rows - terms, found.shape[1]), jnp.float32)
+                found = jnp.concatenate([found, fill], axis=0)
+            head, rest = halve(found)
+            main = product(jnp.concatenate([head, rest], axis=0), coarse_ref[s])
+            total = main[:rows] + main[rows:] + product(head, fine_ref[s])
+            for l in range(levels):
+                out_ref[l, s] = total[2 * l : 2 * l + 2]
         return carry
 
-    lax.fori_loop(0, slots // group, contract, 0)
-
-
-def legendre_tables(orders, lats):
+    lax.fori_loop(0, slots // 4, contract, 0)
+
+
+def dft_kernel(x_ref, trig_ref, out_ref):
+    blocks, levels, lats, _ = x_ref.shape
+    parts, _, _, slots, lanes = out_ref.shape
+    count = trig_ref.shape[1]
+    waves = [jnp.concatenate(halve(trig_ref[j]), axis=0) for j in range(blocks)]
+
+    def product(left, right):
+        return lax.dot_general(
+            left, right, (((1,), (1,)), ((), ())), preferred_element_type=jnp.float32
+        )
+
+    for first in range(0, levels, 2):
+        last = min(first + 2, levels)
+        total = None
+        for j in range(blocks):
+            grid = []
+            for l in range(first, last):
+                grid.append(x_ref[j, l])
+                if lanes > lats:
+                    grid.append(jnp.zeros((lanes - lats, x_ref.shape[3]), jnp.float32))
+            coarse, fine = halve(jnp.concatenate(grid, axis=0))
+            main = product(waves[j], coarse)
+            term = main[:count] + main[count:] + product(waves[j][:count], fine)
+            total = term if total is None else total + term
+        for l in range(first, last):
+            mine = total[:, (l - first) * lanes : (l - first + 1) * lanes]
+            for p in range(parts):
+                for c in range(2):
+                    begin = (p * 2 + c) * slots
+                    out_ref[p, l, c] = mine[begin : begin + slots]
+
+
+def dft(regrouped, wave_table, blocks, parts):
+    _, lats, lons = regrouped.shape
+    levels = regrouped.shape[0] // blocks
+    slots = wave_table.shape[0] // parts
+    pad = -lats % ROWS
+    lanes = -(-lats // LANES) * LANES
+    grid = jnp.pad(regrouped, ((0, 0), (0, pad), (0, 0)))
+    trig = trig_table(jnp.arange(NLON, dtype=jnp.int32), wave_table)
+    trig = trig.reshape(blocks, lons, 2, parts, slots).transpose(0, 3, 2, 4, 1)
+    return pl.pallas_call(
+        dft_kernel,
+        out_shape=jax.ShapeDtypeStruct((parts, levels, 2, slots, lanes), jnp.float32),
+        in_specs=[pl.BlockSpec(memory_space=pltpu.VMEM)] * 2,
+        out_specs=pl.BlockSpec(memory_space=pltpu.VMEM),
+        name="dft",
+    )(
+        grid.reshape(blocks, levels, lats + pad, lons),
+        trig.reshape(blocks, 2 * parts * slots, lons),
+    )
+
+
+def legendre_tables(orders, lats, bands):
     slots = orders.shape[0]
-    wide = -(-lats // LANES) * LANES
+    wide = bands * (-(-(lats // bands) // LANES) * LANES)
     colatitude = (jnp.arange(lats, dtype=jnp.int32).astype(jnp.float32) + 0.5) * (math.pi / lats)
     sine_lat = jnp.sin(colatitude)
     order_col = orders.astype(jnp.float32)[:, None]
@@ -256,13 +327,19 @@
         jnp.maximum(lower * lower - order_col * order_col, 0.0) / (4.0 * lower * lower - 1.0)
     )
     grow = jnp.sqrt(numerator / bottom)
-    pad = ((0, 0), (0, wide - lats))
-    table = jax.ShapeDtypeStruct(((MMAX + 2) * slots, LANES), jnp.float32)
+
+    def spread(values):
+        cut = values.reshape(values.shape[0], bands, lats // bands)
+        cut = jnp.pad(cut, ((0, 0), (0, 0), (0, wide // bands - lats // bands)))
+        return cut.reshape(values.shape[0], wide)
+
+    table = jax.ShapeDtypeStruct((slots, MMAX, wide), jnp.bfloat16)
     return pl.pallas_call(
         march_kernel,
-        out_shape=[table] * (wide // LANES),
+        out_shape=[table] * 2,
         in_specs=[pl.BlockSpec(memory_space=pltpu.VMEM)] * 6,
-        out_specs=[pl.BlockSpec(memory_space=pltpu.VMEM)] * (wide // LANES),
+        out_specs=[pl.BlockSpec(memory_space=pltpu.VMEM)] * 2,
+        scratch_shapes=[pltpu.VMEM(((MMAX + 2) * slots, LANES), jnp.float32)] * (wide // LANES),
         cost_estimate=pl.CostEstimate(
             flops=6 * MMAX * slots * wide, bytes_accessed=16 * MMAX * slots * wide, transcendentals=0
         ),
@@ -272,24 +349,20 @@
         retreat,
         jnp.broadcast_to(orders[:, None], (slots, LANES)),
         jnp.zeros((slots, LANES), jnp.int32),
-        jnp.pad(jnp.cos(colatitude)[None, :], pad),
-        jnp.pad(diagonal, pad),
+        spread(jnp.cos(colatitude)[None, :]),
+        spread(diagonal),
     )
 
 
 def contract_tables(fourier, tables):
-    slots, terms, lats = fourier.shape
-    wide = len(tables) * LANES
-    padded = -(-terms // 16) * 16
-    fourier = jnp.pad(fourier, ((0, 0), (0, padded - terms), (0, wide - lats)))
-    found = pl.pallas_call(
+    bands, levels, _, slots, lanes = fourier.shape
+    return pl.pallas_call(
         contract_kernel,
-        out_shape=jax.ShapeDtypeStruct((slots, padded, MMAX), jnp.float32),
-        in_specs=[pl.BlockSpec(memory_space=pltpu.VMEM)] * (1 + len(tables)),
+        out_shape=jax.ShapeDtypeStruct((levels, slots, 2, MMAX), jnp.float32),
+        in_specs=[pl.BlockSpec(memory_space=pltpu.VMEM)] * 3,
         out_specs=pl.BlockSpec(memory_space=pltpu.VMEM),
         name="contract",
-    )(fourier, *tables)
-    return found[:, :terms]
+    )(fourier.reshape(bands, levels * 2 * slots, lanes), *tables)
 
 
 def trig_table(longitudes, wave_numbers):
@@ -348,20 +421,15 @@
     )
     fresh = own + (share * rainfall + force)
 
-    regrouped = lax.all_to_all(fresh, "col", split_axis=0, concat_axis=2, tiled=True)
-    trig_rows = trig_table(jnp.arange(NLON, dtype=jnp.int32), wave_table)
-    spectra = jnp.einsum("lay,ycs->slca", regrouped, trig_rows, precision=lax.Precision.HIGHEST)
+    regrouped = lax.all_to_all(fresh, "col", split_axis=0, concat_axis=0, tiled=True)
+    spectra = dft(regrouped, wave_table, lax.axis_size("col"), lat_bands)
     owner_count = MMAX // lat_bands
     wave_table, _ = lax.optimization_barrier((wave_table, rainfall))
     owned_waves = lax.dynamic_slice_in_dim(
         wave_table, lax.axis_index("lat") * owner_count, owner_count
     )
-    gathered = lax.all_to_all(spectra, "lat", split_axis=0, concat_axis=3, tiled=True)
-    own_levels = gathered.shape[1]
-    coeffs = contract_tables(
-        gathered.reshape(owner_count, own_levels * 2, NLAT), legendre_tables(owned_waves, NLAT)
-    )
-    coeffs = coeffs.reshape(owner_count, own_levels, 2, MMAX).transpose(1, 0, 2, 3)
+    gathered = lax.all_to_all(spectra, "lat", split_axis=0, concat_axis=0, tiled=True)
+    coeffs = contract_tables(gathered, legendre_tables(owned_waves, NLAT, lat_bands))
     return (fresh[None, None], coeffs[None, None])
 
 

time: 195 us -> 195 us (level)
  local copies, waits for them, and re-layouts: 31.8 us -> 18.2 us
  Pallas kernels: 72.2 us -> 81.3 us
  waiting for transfers between devices: 38.9 us -> 45.5 us
  matrix products: 9.22 us -> 6.52 us
    pallas_call x2 -> x3, Pallas kernels: 23.2 us -> 32.3 us  [the longest x1 19.3 us: legendre_tables(): pl.pallas_call(march_kernel, out_shape=[table] * 2, in_specs=[pl.BlockSpe...]
    all_to_all x3 -> x0, local copies, waits for them, and re-layouts: 7.47 us -> none  [the longest x2 6.21 us: shards(): lax.all_to_all(fresh, 'col', split_axis=0, concat_axis=2, tiled=True)]
    all_to_all x2, waiting for transfers between devices: 22.8 us -> 29.5 us  [the longest x1 29.5 us: shards(): lax.all_to_all(fresh, 'col', split_axis=0, concat_axis=0, tiled=True)]
    dot_general x1 -> x0, matrix products: 2.7 us -> none  [shards(): jnp.einsum('lay,ycs->slca', regrouped, trig_rows, precision=lax.Precision...]
  transfers between devices with their start and end apart: 5 -> 5, of which waited for: 4 -> 3; matrix products, arithmetic and copies ran while one was open for 14% -> 15% of each run, Pallas kernels for 6% -> 10%
where the time goes in v4:
time: 195 us; the launch traced here: 194 us
  Pallas kernels  81.3 us (42%)
  waiting for transfers between devices  45.5 us (23%)
  starting transfers between devices  22.9 us (12%)
  other arithmetic  18.5 us (9%)
  local copies, waits for them, and re-layouts  18.2 us (9%)
  matrix products  6.52 us (3%)
    pallas_call x2, Pallas kernels, permute(): pl.pallas_call(permute_kernel, out_shape=jax.ShapeDtypeStruct(shape, jnp....  33.4 us
    all_to_all x1, waiting for transfers between devices, shards(): lax.all_to_all(fresh, 'col', split_axis=0, concat_axis=0, tiled=True)  29.5 us
    pallas_call x1, Pallas kernels, legendre_tables(): pl.pallas_call(march_kernel, out_shape=[table] * 2, in_specs=[pl.BlockSpe...  19.3 us
    pallas_call x1, Pallas kernels, cloud_model(): pl.pallas_call(cloud_kernel, grid=(bands * steps,), out_shape=jax.ShapeDt...  15.7 us
    all_to_all x1, waiting for transfers between devices, shards(): lax.all_to_all(outgoing, ('sec', 'lat'), split_axis=0, concat_axis=0, til...  9.34 us
    pallas_call x1, Pallas kernels, contract_tables(): pl.pallas_call(contract_kernel, out_shape=jax.ShapeDtypeStruct((levels, s...  8.82 us
    all_to_all x1, starting transfers between devices, shards(): lax.all_to_all(outgoing, ('sec', 'lat'), split_axis=0, concat_axis=0, til...  7.68 us
    all_to_all x1, waiting for transfers between devices, shards(): lax.all_to_all(homeward, ('sec', 'lat'), split_axis=0, concat_axis=0, til...  6.7 us
  transfers between devices with their start and end apart: 5, of which 3 were waited for; matrix products, arithmetic and copies ran while one was open for 15% of the time, Pallas kernels for 10%

profile of v4, /device:TPU:0, one launch (start us, length us, event | category | flops | bytes accessed | tf_op | source)
XLA Modules:
  0.0 193.8 jit_solution(7195528164861450824)
XLA Ops:
  0.6 0.0 copy-start.2
  0.6 0.0 copy-start
  0.7 0.0 copy-start.1
  0.7 3.1 %bitcast_select_fusion = f32[28,96,96]{2,1,0:T(8,128)} fusion(f32[1,1,28,96,96]{4,3,2,1,0:T(8,128)} %param.5, f32[1,1,28,96,96]{4,3,2,1,0:T(8,128)} %param.6, pred[]{:T(512)S(6)} %eq.44), kind=kLoop, calls=%fused_computation.10 | loop fusion | flops 258048 | bytes 3096577 | tf_op jit(solution)/shard_map/jit(_where)/select_n | solution.py:399
  3.8 1.8 collective-permute-start
  5.6 0.0 copy-done.2
  5.6 0.7 add_select_fusion.1
  6.2 0.3 iota_compare_fusion.2
  6.6 0.1 fusion.15
  6.7 0.0 collective-permute-done
  6.7 2.8 %fusion.2 = f32[28,96,96]{2,1,0:T(8,128)} fusion(f32[28,96,96]{2,1,0:T(8,128)} %collective-permute-done, f32[1,1,28,96,96]{4,3,2,1,0:T(8,128)S(1)} %copy-done, f32[1,1,28,96,96]{4,3,2,1,0:T(8,128)S(1)} %copy-done.1, pred[]{:T(512)S(6)} %eq.44, pred[]{:T(512)S(6)} %eq.45), kind=kLoop, calls=%fused_computation.7 | loop fusion | flops 1290240 | bytes 4128770 | tf_op jit(solution)/shard_map/jit(_where)/select_n | solution.py:400
  9.5 3.2 %reshape.490.x_ref = f32[28,9216]{1,0:T(8,128)} reshape(f32[28,96,96]{2,1,0:T(8,128)} %fusion.2) | data formatting | bytes 2064384 | tf_op jit(solution)/shard_map/reshape | solution.py:403
  12.7 16.7 %permute.2 = f32[8,28,1152]{2,1,0:T(8,128)} custom-call(f32[28,9216]{1,0:T(8,128)} %reshape.490.x_ref, s32[1,9216]{1,0:T(1,128)} %bitcast.48), custom_call_target="tpu_custom_call" | custom-call | tf_op jit(solution)/shard_map/permute/pallas_call | solution.py:91
  29.4 7.7 %all-to-all-start = ((f32[8,28,1152]{2,1,0:T(8,128)}), f32[8,28,1152]{2,1,0:T(8,128)}, u32[]{:S(2)}, u32[]{:S(2)}) async-start(f32[8,28,1152]{2,1,0:T(8,128)} %permute.2), calls=%async_computation | async-start | bytes 2359296 | tf_op jit(solution)/shard_map/all_to_all | solution.py:412
  37.1 0.1 pad_maximum_fusion
  37.2 6.6 %copy.11 = bf16[1,32,28,1,1,2304]{5,2,1,4,3,0:T(8,128)(2,1)} copy(bf16[1,32,28,1,1,2304]{5,1,4,3,2,0:T(8,128)(2,1)} %param.7) | data formatting | bytes 8257536 | tf_op jit(solution)/shard_map/optimization_barrier | solution.py:411
  43.8 9.3 %all-to-all-done.wind_ref.gap_ref.push_ref = f32[8,28,1152]{2,1,0:T(8,128)} async-done(((f32[8,28,1152]{2,1,0:T(8,128)}), f32[8,28,1152]{2,1,0:T(8,128)}, u32[]{:S(2)}, u32[]{:S(2)}) %all-to-all-start) | async-done | bytes 1032224 | tf_op jit(solution)/shard_map/all_to_all | solution.py:412
  53.1 15.7 %cloud.1 = f32[4,2,28,1152]{3,2,1,0:T(8,128)} custom-call(f32[8,28,1152]{2,1,0:T(8,128)} %all-to-all-done.wind_ref.gap_ref.push_ref, f32[8,28,1152]{2,1,0:T(8,128)} %all-to-all-done.wind_ref.gap_ref.push_ref, f32[8,28,1152]{2,1,0:T(8,128)} %all-to-all-done.wind_ref.gap_ref.push_ref, bf16[32,28,2304]{2,1,0:T(8,128)(2,1)} %bitcast.41), custom_call_target="tpu_custom_call" | custom-call | tf_op jit(solution)/shard_map/cloud/pallas_call | solution.py:160
  68.8 4.3 %all-to-all-start.1 = ((f32[8,28,1152]{2,1,0:T(8,128)}), f32[8,28,1152]{2,1,0:T(8,128)}, u32[]{:S(2)}, u32[]{:S(2)}) async-start(f32[8,28,1152]{2,1,0:T(8,128)} %bitcast.42), calls=%async_computation.1 | async-start | bytes 2359296 | tf_op jit(solution)/shard_map/all_to_all | solution.py:414
  73.0 0.0 copy-start.4
  73.0 0.0 copy-start.3
  73.1 2.0 %broadcast_select_fusion = bf16[2,72,9216]{2,1,0:T(8,128)(2,1)} fusion(pred[72,9216]{1,0:T(8,128)(4,1)S(1)} %iota_compare_fusion.2, bf16[2,9216]{1,0:T(2,128)(2,1)S(1)} %pad_maximum_fusion), kind=kLoop, calls=%fused_computation.4 | loop fusion | flops 1327104 | bytes 3354624 | tf_op jit(solution)/shard_map/jit(_where)/select_n | solution.py:382
  75.0 0.1 mul.202
  75.1 6.5 %fusion.7 = s32[144,128]{1,0:T(8,128)S(1)} fusion(bf16[144,9216]{1,0:T(8,128)(2,1)} %bitcast.43, s32[9216]{0:T(1024)S(1)} %copy-done.3), kind=kOutput, calls=%fused_computation.17 | convolution fusion | flops 340936704 | bytes 2764800 | tf_op jit(solution)/shard_map/dot_general | solution.py:383
  81.6 0.6 slice_add_fusion
  82.3 6.7 %all-to-all-done.1.x_ref = f32[8,28,1152]{2,1,0:T(8,128)} async-done(((f32[8,28,1152]{2,1,0:T(8,128)}), f32[8,28,1152]{2,1,0:T(8,128)}, u32[]{:S(2)}, u32[]{:S(2)}) %all-to-all-start.1) | async-done | bytes 1032224 | tf_op jit(solution)/shard_map/all_to_all | solution.py:414
  89.0 16.7 %permute.3 = f32[28,9216]{1,0:T(8,128)} custom-call(f32[8,28,1152]{2,1,0:T(8,128)} %all-to-all-done.1.x_ref, s32[1,9216]{1,0:T(1,128)} %bitcast.50), custom_call_target="tpu_custom_call" | custom-call | tf_op jit(solution)/shard_map/permute/pallas_call | solution.py:91
  105.7 2.9 %reshape.493 = f32[28,96,96]{2,1,0:T(8,128)} reshape(f32[28,9216]{1,0:T(8,128)} %permute.3) | data formatting | bytes 2064384 | tf_op jit(solution)/shard_map/reshape | solution.py:418
  108.6 2.8 %bitcast_add_fusion = f32[28,96,96]{2,1,0:T(8,128)} fusion(f32[1,1,28,96,96]{4,3,2,1,0:T(8,128)S(1)} %copy-done, f32[28,96,96]{2,1,0:T(8,128)} %reshape.493, f32[1,1,28,96,96]{4,3,2,1,0:T(8,128)S(1)} %copy-done.1, f32[]{:T(128)S(6)} %select_n.125, pred[]{:T(512)S(6)} %lt.24), kind=kLoop, calls=%fused_computation.9 | loop fusion | flops 1290240 | bytes 4128773 | tf_op jit(solution)/shard_map/add | solution.py:422
  111.4 4.9 %all-to-all-start.2 = ((f32[28,96,96]{2,1,0:T(8,128)}), f32[28,96,96]{2,1,0:T(8,128)}, u32[]{:S(2)}, u32[]{:S(2)}) async-start(f32[28,96,96]{2,1,0:T(8,128)} %bitcast_add_fusion), calls=%async_computation.2 | async-start | bytes 2752512 | tf_op jit(solution)/shard_map/all_to_all | solution.py:424
  116.3 0.5 pad.8
  116.9 0.1 broadcast_multiply_fusion
  116.9 1.1 fusion.13
  118.1 0.9 maximum_multiply_fusion
  118.9 0.1 subtract_multiply_fusion
  119.1 0.7 divide_sqrt_fusion
  119.8 29.5 %all-to-all-done.2 = f32[28,96,96]{2,1,0:T(8,128)} async-done(((f32[28,96,96]{2,1,0:T(8,128)}), f32[28,96,96]{2,1,0:T(8,128)}, u32[]{:S(2)}, u32[]{:S(2)}) %all-to-all-start.2) | async-done | bytes 1032224 | tf_op jit(solution)/shard_map/all_to_all | solution.py:424
  149.3 4.1 %dft.1 = f32[2,7,2,64,128]{4,3,2,1,0:T(8,128)} custom-call(f32[4,7,96,96]{3,2,1,0:T(8,128)} %bitcast.8.x_ref, f32[4,256,96]{2,1,0:T(8,128)} %bitcast.44), custom_call_target="tpu_custom_call" | custom-call | tf_op jit(solution)/shard_map/dft/pallas_call | solution.py:298
  153.4 4.4 %all-to-all-start.3 = ((f32[2,7,2,64,128]{4,3,2,1,0:T(8,128)}), f32[2,7,2,64,128]{4,3,2,1,0:T(8,128)}, u32[]{:S(2)}, u32[]{:S(2)}) async-start(f32[2,7,2,64,128]{4,3,2,1,0:T(8,128)} %dft.1), calls=%async_computation.3 | async-start | bytes 1835008 | tf_op jit(solution)/shard_map/all_to_all | solution.py:431
  157.7 0.2 exponential_multiply_fusion
  158.0 2.9 %reshape.492 = f32[1,1,28,96,96]{4,3,2,1,0:T(8,128)} reshape(f32[28,9216]{1,0:T(8,128)} %permute.3) | data formatting | bytes 2064384 | tf_op jit(solution)/shard_map/reshape | solution.py:418
  160.9 0.6 copy.12
  161.5 0.7 broadcast_in_dim.74.order_ref
  162.2 0.6 broadcast_in_dim.75.zero_ref
  162.8 19.3 %march.1 = (bf16[64,128,256]{2,1,0:T(8,128)(2,1)}, bf16[64,128,256]{2,1,0:T(8,128)(2,1)}) custom-call(f32[64,128]{1,0:T(8,128)} %get-tuple-element.19.grow_ref, f32[64,128]{1,0:T(8,128)} %get-tuple-element.18.retreat_ref, s32[64,128]{1,0:T(8,128)} %broadcast_in_dim.74.order_ref, s32[64,128]{1,0:T(8,128)} %broadcast_in_dim.75.zero_ref, f32[1,256]{1,0:T(1,128)} %bitcast.51, ...), custom_call_target="tpu_custom_call" | custom-call | flops 12582912 | bytes 33554432 | tf_op jit(solution)/shard_map/march/pallas_call | solution.py:337
  182.2 2.8 %add_add_fusion = f32[1,1,28,96,96]{4,3,2,1,0:T(8,128)} fusion(f32[1,1,28,96,96]{4,3,2,1,0:T(8,128)S(1)} %copy-done, f32[1,1,28,96,96]{4,3,2,1,0:T(8,128)S(1)} %copy-done.1, f32[1,1,28,96,96]{4,3,2,1,0:T(8,128)} %reshape.492, f32[]{:T(128)S(6)} %select_n.125, pred[]{:T(512)S(6)} %lt.24), kind=kLoop, calls=%fused_computation.16 | loop fusion | flops 1290240 | bytes 4128773 | tf_op jit(solution)/shard_map/add | solution.py:422
  185.0 0.0 all-to-all-done.3
  185.0 8.8 %contract.1 = f32[7,64,2,128]{3,2,1,0:T(2,128)} custom-call(f32[2,896,128]{2,1,0:T(8,128)} %bitcast.11.fourier_ref, bf16[64,128,256]{2,1,0:T(8,128)(2,1)} %get-tuple-element.10.coarse_ref, bf16[64,128,256]{2,1,0:T(8,128)(2,1)} %get-tuple-element.11.fine_ref), custom_call_target="tpu_custom_call" | custom-call | tf_op jit(solution)/shard_map/contract/pallas_call | solution.py:359
  (12 shorter events, 0.1 us)
Async XLA Ops:
  0.6 4.9 %copy-start.2 = (s32[1,1,9216]{2,1,0:T(1,128)S(1)}, s32[1,1,9216]{2,1,0:T(1,128)}, u32[]{:S(2)}) copy-start(s32[1,1,9216]{2,1,0:T(1,128)} %param.8) | copy-start | bytes 110596
  0.6 6.0 %copy-start = (f32[1,1,28,96,96]{4,3,2,1,0:T(8,128)S(1)}, f32[1,1,28,96,96]{4,3,2,1,0:T(8,128)}, u32[]{:S(2)}) copy-start(f32[1,1,28,96,96]{4,3,2,1,0:T(8,128)} %param.5) | copy-start | bytes 3096580
  0.7 6.0 %copy-start.1 = (f32[1,1,28,96,96]{4,3,2,1,0:T(8,128)S(1)}, f32[1,1,28,96,96]{4,3,2,1,0:T(8,128)}, u32[]{:S(2)}) copy-start(f32[1,1,28,96,96]{4,3,2,1,0:T(8,128)} %param.6) | copy-start | bytes 3096580
  3.8 2.9 %collective-permute-start = (f32[28,96,96]{2,1,0:T(8,128)}, f32[28,96,96]{2,1,0:T(8,128)}, u32[]{:S(2)}, u32[]{:S(2)}) collective-permute-start(f32[28,96,96]{2,1,0:T(8,128)} %bitcast_select_fusion), channel_id=1, source_target_pairs={{16,24},{24,16},{17,25},{25,17},{18,26},{26,18},{19,27},{27,19},{2... | collective-permute-start | bytes 3096584 | tf_op jit(solution)/shard_map/ppermute | solution.py:399
  29.4 23.7 %all-to-all-start = ((f32[8,28,1152]{2,1,0:T(8,128)}), f32[8,28,1152]{2,1,0:T(8,128)}, u32[]{:S(2)}, u32[]{:S(2)}) async-start(f32[8,28,1152]{2,1,0:T(8,128)} %permute.2), calls=%async_computation | async-start | bytes 2359296 | tf_op jit(solution)/shard_map/all_to_all | solution.py:412
  68.8 20.2 %all-to-all-start.1 = ((f32[8,28,1152]{2,1,0:T(8,128)}), f32[8,28,1152]{2,1,0:T(8,128)}, u32[]{:S(2)}, u32[]{:S(2)}) async-start(f32[8,28,1152]{2,1,0:T(8,128)} %bitcast.42), calls=%async_computation.1 | async-start | bytes 2359296 | tf_op jit(solution)/shard_map/all_to_all | solution.py:414
  73.0 2.0 %copy-start.4 = (s32[128]{0:T(128)S(1)}, s32[128]{0:T(128)}, u32[]{:S(2)}) copy-start(s32[128]{0:T(128)} %param.9) | copy-start | bytes 1540
  73.0 2.1 %copy-start.3 = (s32[9216]{0:T(1024)S(1)}, s32[9216]{0:T(1024)}, u32[]{:S(2)}) copy-start(s32[9216]{0:T(1024)} %get-tuple-element.14) | copy-start | bytes 110596
  111.4 37.9 %all-to-all-start.2 = ((f32[28,96,96]{2,1,0:T(8,128)}), f32[28,96,96]{2,1,0:T(8,128)}, u32[]{:S(2)}, u32[]{:S(2)}) async-start(f32[28,96,96]{2,1,0:T(8,128)} %bitcast_add_fusion), calls=%async_computation.2 | async-start | bytes 2752512 | tf_op jit(solution)/shard_map/all_to_all | solution.py:424
  153.4 31.6 %all-to-all-start.3 = ((f32[2,7,2,64,128]{4,3,2,1,0:T(8,128)}), f32[2,7,2,64,128]{4,3,2,1,0:T(8,128)}, u32[]{:S(2)}, u32[]{:S(2)}) async-start(f32[2,7,2,64,128]{4,3,2,1,0:T(8,128)} %dft.1), calls=%async_computation.3 | async-start | bytes 1835008 | tf_op jit(solution)/shard_map/all_to_all | solution.py:431

commit v5 on v4

--- a/solution.py
+++ b/solution.py
@@ -422,14 +422,16 @@
     fresh = own + (share * rainfall + force)
 
     regrouped = lax.all_to_all(fresh, "col", split_axis=0, concat_axis=0, tiled=True)
-    spectra = dft(regrouped, wave_table, lax.axis_size("col"), lat_bands)
     owner_count = MMAX // lat_bands
     wave_table, _ = lax.optimization_barrier((wave_table, rainfall))
     owned_waves = lax.dynamic_slice_in_dim(
         wave_table, lax.axis_index("lat") * owner_count, owner_count
     )
+    tables = legendre_tables(owned_waves, NLAT, lat_bands)
+    regrouped, tables = lax.optimization_barrier((regrouped, tables))
+    spectra = dft(regrouped, wave_table, lax.axis_size("col"), lat_bands)
     gathered = lax.all_to_all(spectra, "lat", split_axis=0, concat_axis=0, tiled=True)
-    coeffs = contract_tables(gathered, legendre_tables(owned_waves, NLAT, lat_bands))
+    coeffs = contract_tables(gathered, tables)
     return (fresh[None, None], coeffs[None, None])
 
 

time: 195 us -> 180 us (0.923)
  waiting for transfers between devices: 45.5 us -> 30.1 us
    all_to_all x1, waiting for transfers between devices: 29.5 us -> 8.44 us  [shards(): lax.all_to_all(fresh, 'col', split_axis=0, concat_axis=0, tiled=True)]
    all_to_all x1, waiting for transfers between devices: 0.01 us -> 6.13 us  [shards(): lax.all_to_all(spectra, 'lat', split_axis=0, concat_axis=0, tiled=True)]
  transfers between devices with their start and end apart: 5 -> 5, of which waited for: 3 -> 4; matrix products, arithmetic and copies ran while one was open for 15% -> 16% of each run, Pallas kernels for 10% -> 11%
where the time goes in v5:
time: 180 us; the launch traced here: 178 us
  Pallas kernels  81.2 us (45%)
  waiting for transfers between devices  30.1 us (17%)
  starting transfers between devices  23.1 us (13%)
  other arithmetic  18.5 us (10%)
  local copies, waits for them, and re-layouts  18.3 us (10%)
  matrix products  6.52 us (4%)
    pallas_call x2, Pallas kernels, permute(): pl.pallas_call(permute_kernel, out_shape=jax.ShapeDtypeStruct(shape, jnp....  33.4 us
    pallas_call x1, Pallas kernels, legendre_tables(): pl.pallas_call(march_kernel, out_shape=[table] * 2, in_specs=[pl.BlockSpe...  19.3 us
    pallas_call x1, Pallas kernels, cloud_model(): pl.pallas_call(cloud_kernel, grid=(bands * steps,), out_shape=jax.ShapeDt...  15.7 us
    all_to_all x1, waiting for transfers between devices, shards(): lax.all_to_all(outgoing, ('sec', 'lat'), split_axis=0, concat_axis=0, til...  9.34 us
    pallas_call x1, Pallas kernels, contract_tables(): pl.pallas_call(contract_kernel, out_shape=jax.ShapeDtypeStruct((levels, s...  8.82 us
    all_to_all x1, waiting for transfers between devices, shards(): lax.all_to_all(fresh, 'col', split_axis=0, concat_axis=0, tiled=True)  8.44 us
    all_to_all x1, starting transfers between devices, shards(): lax.all_to_all(outgoing, ('sec', 'lat'), split_axis=0, concat_axis=0, til...  7.69 us
    optimization_barrier x1, local copies, waits for them, and re-layouts, shards(): crm_moisture, outgoing = lax.optimization_barrier((crm_moisture, outgoing))  6.6 us
  transfers between devices with their start and end apart: 5, of which 4 were waited for; matrix products, arithmetic and copies ran while one was open for 16% of the time, Pallas kernels for 11%

profile of v5, /device:TPU:0, one launch (start us, length us, event | category | flops | bytes accessed | tf_op | source)
XLA Modules:
  0.0 178.4 jit_solution(9728323830269053248)
XLA Ops:
  0.6 0.0 copy-start.2
  0.6 0.0 copy-start
  0.7 0.0 copy-start.1
  0.7 3.1 %bitcast_select_fusion = f32[28,96,96]{2,1,0:T(8,128)} fusion(f32[1,1,28,96,96]{4,3,2,1,0:T(8,128)} %param.5, f32[1,1,28,96,96]{4,3,2,1,0:T(8,128)} %param.6, pred[]{:T(512)S(6)} %eq.44), kind=kLoop, calls=%fused_computation.10 | loop fusion | flops 258048 | bytes 3096577 | tf_op jit(solution)/shard_map/jit(_where)/select_n | solution.py:399
  3.8 1.8 collective-permute-start
  5.6 0.7 add_select_fusion.1
  6.2 0.3 iota_compare_fusion.2
  6.6 0.1 fusion.15
  6.7 0.0 collective-permute-done
  6.7 0.0 copy-done
  6.7 0.0 copy-done.1
  6.7 2.8 %fusion.2 = f32[28,96,96]{2,1,0:T(8,128)} fusion(f32[28,96,96]{2,1,0:T(8,128)} %collective-permute-done, f32[1,1,28,96,96]{4,3,2,1,0:T(8,128)S(1)} %copy-done, f32[1,1,28,96,96]{4,3,2,1,0:T(8,128)S(1)} %copy-done.1, pred[]{:T(512)S(6)} %eq.44, pred[]{:T(512)S(6)} %eq.45), kind=kLoop, calls=%fused_computation.7 | loop fusion | flops 1290240 | bytes 4128770 | tf_op jit(solution)/shard_map/jit(_where)/select_n | solution.py:400
  9.5 3.2 %reshape.490.x_ref = f32[28,9216]{1,0:T(8,128)} reshape(f32[28,96,96]{2,1,0:T(8,128)} %fusion.2) | data formatting | bytes 2064384 | tf_op jit(solution)/shard_map/reshape | solution.py:403
  12.7 16.7 %permute.2 = f32[8,28,1152]{2,1,0:T(8,128)} custom-call(f32[28,9216]{1,0:T(8,128)} %reshape.490.x_ref, s32[1,9216]{1,0:T(1,128)} %bitcast.48), custom_call_target="tpu_custom_call" | custom-call | tf_op jit(solution)/shard_map/permute/pallas_call | solution.py:91
  29.4 7.7 %all-to-all-start = ((f32[8,28,1152]{2,1,0:T(8,128)}), f32[8,28,1152]{2,1,0:T(8,128)}, u32[]{:S(2)}, u32[]{:S(2)}) async-start(f32[8,28,1152]{2,1,0:T(8,128)} %permute.2), calls=%async_computation | async-start | bytes 2359296 | tf_op jit(solution)/shard_map/all_to_all | solution.py:412
  37.1 0.1 pad_maximum_fusion
  37.2 6.6 %copy.11 = bf16[1,32,28,1,1,2304]{5,2,1,4,3,0:T(8,128)(2,1)} copy(bf16[1,32,28,1,1,2304]{5,1,4,3,2,0:T(8,128)(2,1)} %param.7) | data formatting | bytes 8257536 | tf_op jit(solution)/shard_map/optimization_barrier | solution.py:411
  43.8 9.3 %all-to-all-done.wind_ref.gap_ref.push_ref = f32[8,28,1152]{2,1,0:T(8,128)} async-done(((f32[8,28,1152]{2,1,0:T(8,128)}), f32[8,28,1152]{2,1,0:T(8,128)}, u32[]{:S(2)}, u32[]{:S(2)}) %all-to-all-start) | async-done | bytes 1032224 | tf_op jit(solution)/shard_map/all_to_all | solution.py:412
  53.1 15.7 %cloud.1 = f32[4,2,28,1152]{3,2,1,0:T(8,128)} custom-call(f32[8,28,1152]{2,1,0:T(8,128)} %all-to-all-done.wind_ref.gap_ref.push_ref, f32[8,28,1152]{2,1,0:T(8,128)} %all-to-all-done.wind_ref.gap_ref.push_ref, f32[8,28,1152]{2,1,0:T(8,128)} %all-to-all-done.wind_ref.gap_ref.push_ref, bf16[32,28,2304]{2,1,0:T(8,128)(2,1)} %bitcast.41), custom_call_target="tpu_custom_call" | custom-call | tf_op jit(solution)/shard_map/cloud/pallas_call | solution.py:160
  68.8 4.3 %all-to-all-start.1 = ((f32[8,28,1152]{2,1,0:T(8,128)}), f32[8,28,1152]{2,1,0:T(8,128)}, u32[]{:S(2)}, u32[]{:S(2)}) async-start(f32[8,28,1152]{2,1,0:T(8,128)} %bitcast.42), calls=%async_computation.1 | async-start | bytes 2359296 | tf_op jit(solution)/shard_map/all_to_all | solution.py:414
  73.0 0.0 copy-start.3
  73.1 2.0 %broadcast_select_fusion = bf16[2,72,9216]{2,1,0:T(8,128)(2,1)} fusion(pred[72,9216]{1,0:T(8,128)(4,1)S(1)} %iota_compare_fusion.2, bf16[2,9216]{1,0:T(2,128)(2,1)S(1)} %pad_maximum_fusion), kind=kLoop, calls=%fused_computation.4 | loop fusion | flops 1327104 | bytes 3354624 | tf_op jit(solution)/shard_map/jit(_where)/select_n | solution.py:382
  75.1 0.6 pad.8
  75.7 6.5 %fusion.7 = s32[144,128]{1,0:T(8,128)S(1)} fusion(bf16[144,9216]{1,0:T(8,128)(2,1)} %bitcast.43, s32[9216]{0:T(1024)S(1)} %copy-done.3), kind=kOutput, calls=%fused_computation.17 | convolution fusion | flops 340936704 | bytes 2764800 | tf_op jit(solution)/shard_map/dot_general | solution.py:383
  82.2 0.6 slice_add_fusion
  82.8 6.2 %all-to-all-done.1.x_ref = f32[8,28,1152]{2,1,0:T(8,128)} async-done(((f32[8,28,1152]{2,1,0:T(8,128)}), f32[8,28,1152]{2,1,0:T(8,128)}, u32[]{:S(2)}, u32[]{:S(2)}) %all-to-all-start.1) | async-done | bytes 1032224 | tf_op jit(solution)/shard_map/all_to_all | solution.py:414
  89.0 16.7 %permute.3 = f32[28,9216]{1,0:T(8,128)} custom-call(f32[8,28,1152]{2,1,0:T(8,128)} %all-to-all-done.1.x_ref, s32[1,9216]{1,0:T(1,128)} %bitcast.50), custom_call_target="tpu_custom_call" | custom-call | tf_op jit(solution)/shard_map/permute/pallas_call | solution.py:91
  105.7 2.9 %reshape.493 = f32[28,96,96]{2,1,0:T(8,128)} reshape(f32[28,9216]{1,0:T(8,128)} %permute.3) | data formatting | bytes 2064384 | tf_op jit(solution)/shard_map/reshape | solution.py:418
  108.6 2.8 %bitcast_add_fusion = f32[28,96,96]{2,1,0:T(8,128)} fusion(f32[1,1,28,96,96]{4,3,2,1,0:T(8,128)S(1)} %copy-done, f32[28,96,96]{2,1,0:T(8,128)} %reshape.493, f32[1,1,28,96,96]{4,3,2,1,0:T(8,128)S(1)} %copy-done.1, f32[]{:T(128)S(6)} %select_n.125, pred[]{:T(512)S(6)} %lt.24), kind=kLoop, calls=%fused_computation.9 | loop fusion | flops 1290240 | bytes 4128773 | tf_op jit(solution)/shard_map/add | solution.py:422
  111.4 5.0 %all-to-all-start.2 = ((f32[28,96,96]{2,1,0:T(8,128)}), f32[28,96,96]{2,1,0:T(8,128)}, u32[]{:S(2)}, u32[]{:S(2)}) async-start(f32[28,96,96]{2,1,0:T(8,128)} %bitcast_add_fusion), calls=%async_computation.2 | async-start | bytes 2752512 | tf_op jit(solution)/shard_map/all_to_all | solution.py:424
  116.4 0.0 copy-done.4
  116.5 0.1 mul.220
  116.5 0.1 subtract_multiply_fusion
  116.7 0.2 exponential_multiply_fusion
  116.9 0.6 copy.12
  117.6 0.7 divide_sqrt_fusion
  118.3 0.7 broadcast_in_dim.74.order_ref
  119.0 0.6 broadcast_in_dim.75.zero_ref
  119.6 19.3 %march.1 = (bf16[64,128,256]{2,1,0:T(8,128)(2,1)}, bf16[64,128,256]{2,1,0:T(8,128)(2,1)}) custom-call(f32[64,128]{1,0:T(8,128)} %get-tuple-element.25.grow_ref, f32[64,128]{1,0:T(8,128)} %get-tuple-element.24.retreat_ref, s32[64,128]{1,0:T(8,128)} %broadcast_in_dim.74.order_ref, s32[64,128]{1,0:T(8,128)} %broadcast_in_dim.75.zero_ref, f32[1,256]{1,0:T(1,128)} %bitcast.51, ...), custom_call_target="tpu_custom_call" | custom-call | flops 12582912 | bytes 33554432 | tf_op jit(solution)/shard_map/march/pallas_call | solution.py:337
  138.9 1.1 fusion.13
  140.1 0.9 maximum_multiply_fusion
  141.0 8.4 %all-to-all-done.2 = f32[28,96,96]{2,1,0:T(8,128)} async-done(((f32[28,96,96]{2,1,0:T(8,128)}), f32[28,96,96]{2,1,0:T(8,128)}, u32[]{:S(2)}, u32[]{:S(2)}) %all-to-all-start.2) | async-done | bytes 1032224 | tf_op jit(solution)/shard_map/all_to_all | solution.py:424
  149.4 4.0 %dft.1 = f32[2,7,2,64,128]{4,3,2,1,0:T(8,128)} custom-call(f32[4,7,96,96]{3,2,1,0:T(8,128)} %bitcast.9.x_ref, f32[4,256,96]{2,1,0:T(8,128)} %bitcast.44), custom_call_target="tpu_custom_call" | custom-call | tf_op jit(solution)/shard_map/dft/pallas_call | solution.py:298
  153.4 4.4 %all-to-all-start.3 = ((f32[2,7,2,64,128]{4,3,2,1,0:T(8,128)}), f32[2,7,2,64,128]{4,3,2,1,0:T(8,128)}, u32[]{:S(2)}, u32[]{:S(2)}) async-start(f32[2,7,2,64,128]{4,3,2,1,0:T(8,128)} %dft.1), calls=%async_computation.3 | async-start | bytes 1835008 | tf_op jit(solution)/shard_map/all_to_all | solution.py:433
  157.8 2.9 %reshape.492 = f32[1,1,28,96,96]{4,3,2,1,0:T(8,128)} reshape(f32[28,9216]{1,0:T(8,128)} %permute.3) | data formatting | bytes 2064384 | tf_op jit(solution)/shard_map/reshape | solution.py:418
  160.7 2.8 %add_add_fusion = f32[1,1,28,96,96]{4,3,2,1,0:T(8,128)} fusion(f32[1,1,28,96,96]{4,3,2,1,0:T(8,128)S(1)} %copy-done, f32[1,1,28,96,96]{4,3,2,1,0:T(8,128)S(1)} %copy-done.1, f32[1,1,28,96,96]{4,3,2,1,0:T(8,128)} %reshape.492, f32[]{:T(128)S(6)} %select_n.125, pred[]{:T(512)S(6)} %lt.24), kind=kLoop, calls=%fused_computation.16 | loop fusion | flops 1290240 | bytes 4128773 | tf_op jit(solution)/shard_map/add | solution.py:422
  163.5 6.1 %all-to-all-done.3 = f32[2,7,2,64,128]{4,3,2,1,0:T(8,128)} async-done(((f32[2,7,2,64,128]{4,3,2,1,0:T(8,128)}), f32[2,7,2,64,128]{4,3,2,1,0:T(8,128)}, u32[]{:S(2)}, u32[]{:S(2)}) %all-to-all-start.3) | async-done | bytes 917536 | tf_op jit(solution)/shard_map/all_to_all | solution.py:433
  169.6 8.8 %contract.1 = f32[7,64,2,128]{3,2,1,0:T(2,128)} custom-call(f32[2,896,128]{2,1,0:T(8,128)} %bitcast.12.fourier_ref, bf16[64,128,256]{2,1,0:T(8,128)(2,1)} %get-tuple-element.16.coarse_ref, bf16[64,128,256]{2,1,0:T(8,128)(2,1)} %get-tuple-element.17.fine_ref), custom_call_target="tpu_custom_call" | custom-call | tf_op jit(solution)/shard_map/contract/pallas_call | solution.py:359
  (12 shorter events, 0.2 us)
Async XLA Ops:
  0.6 4.9 %copy-start.2 = (s32[1,1,9216]{2,1,0:T(1,128)S(1)}, s32[1,1,9216]{2,1,0:T(1,128)}, u32[]{:S(2)}) copy-start(s32[1,1,9216]{2,1,0:T(1,128)} %param.8) | copy-start | bytes 110596
  0.6 6.0 %copy-start = (f32[1,1,28,96,96]{4,3,2,1,0:T(8,128)S(1)}, f32[1,1,28,96,96]{4,3,2,1,0:T(8,128)}, u32[]{:S(2)}) copy-start(f32[1,1,28,96,96]{4,3,2,1,0:T(8,128)} %param.5) | copy-start | bytes 3096580
  0.7 6.0 %copy-start.1 = (f32[1,1,28,96,96]{4,3,2,1,0:T(8,128)S(1)}, f32[1,1,28,96,96]{4,3,2,1,0:T(8,128)}, u32[]{:S(2)}) copy-start(f32[1,1,28,96,96]{4,3,2,1,0:T(8,128)} %param.6) | copy-start | bytes 3096580
  3.8 2.9 %collective-permute-start = (f32[28,96,96]{2,1,0:T(8,128)}, f32[28,96,96]{2,1,0:T(8,128)}, u32[]{:S(2)}, u32[]{:S(2)}) collective-permute-start(f32[28,96,96]{2,1,0:T(8,128)} %bitcast_select_fusion), channel_id=1, source_target_pairs={{16,24},{24,16},{17,25},{25,17},{18,26},{26,18},{19,27},{27,19},{2... | collective-permute-start | bytes 3096584 | tf_op jit(solution)/shard_map/ppermute | solution.py:399
  29.4 23.7 %all-to-all-start = ((f32[8,28,1152]{2,1,0:T(8,128)}), f32[8,28,1152]{2,1,0:T(8,128)}, u32[]{:S(2)}, u32[]{:S(2)}) async-start(f32[8,28,1152]{2,1,0:T(8,128)} %permute.2), calls=%async_computation | async-start | bytes 2359296 | tf_op jit(solution)/shard_map/all_to_all | solution.py:412
  68.8 20.2 %all-to-all-start.1 = ((f32[8,28,1152]{2,1,0:T(8,128)}), f32[8,28,1152]{2,1,0:T(8,128)}, u32[]{:S(2)}, u32[]{:S(2)}) async-start(f32[8,28,1152]{2,1,0:T(8,128)} %bitcast.42), calls=%async_computation.1 | async-start | bytes 2359296 | tf_op jit(solution)/shard_map/all_to_all | solution.py:414
  73.0 2.6 %copy-start.3 = (s32[9216]{0:T(1024)S(1)}, s32[9216]{0:T(1024)}, u32[]{:S(2)}) copy-start(s32[9216]{0:T(1024)} %get-tuple-element.20) | copy-start | bytes 110596
  111.4 5.1 %copy-start.4 = (s32[128]{0:T(128)S(1)}, s32[128]{0:T(128)}, u32[]{:S(2)}) copy-start(s32[128]{0:T(128)} %param.9) | copy-start | bytes 1540
  111.4 38.0 %all-to-all-start.2 = ((f32[28,96,96]{2,1,0:T(8,128)}), f32[28,96,96]{2,1,0:T(8,128)}, u32[]{:S(2)}, u32[]{:S(2)}) async-start(f32[28,96,96]{2,1,0:T(8,128)} %bitcast_add_fusion), calls=%async_computation.2 | async-start | bytes 2752512 | tf_op jit(solution)/shard_map/all_to_all | solution.py:424
  153.4 16.2 %all-to-all-start.3 = ((f32[2,7,2,64,128]{4,3,2,1,0:T(8,128)}), f32[2,7,2,64,128]{4,3,2,1,0:T(8,128)}, u32[]{:S(2)}, u32[]{:S(2)}) async-start(f32[2,7,2,64,128]{4,3,2,1,0:T(8,128)} %dft.1), calls=%async_computation.3 | async-start | bytes 1835008 | tf_op jit(solution)/shard_map/all_to_all | solution.py:433

commit v6 on v5

--- a/solution.py
+++ b/solution.py
@@ -18,7 +18,8 @@
 CONDENSE = 0.5
 
 
-def permute_kernel(x_ref, order_ref, out_ref, parts, held):
+def permute_kernel(x_ref, order_ref, *refs):
+    *updates, out_ref, parts, held = refs
     levels = x_ref.shape[-2]
     rows = held.shape[0]
     cols = order_ref.shape[1]
@@ -74,6 +75,9 @@
                 value = total[r][: end - r * ROWS]
                 if out_ref.ndim == 2:
                     at = pl.ds(pl.multiple_of(tile * LANES, LANES), LANES)
+                    if updates:
+                        share_ref, base_ref = updates
+                        value = base_ref[r * ROWS : end, at] + share_ref[r * ROWS : end, at] * value
                     out_ref[r * ROWS : end, at] = value
                 else:
                     per = out_ref.shape[2] // LANES
@@ -84,21 +88,21 @@
     lax.fori_loop(0, tiles // halves, one, 0)
 
 
-def permute(values, order, shape):
+def permute(values, order, shape, updates=()):
     levels, tiles = values.shape[-2], order.shape[1] // LANES
     rows = -(-levels // ROWS) * ROWS
     gathered = tiles * 3 // 8
     return pl.pallas_call(
         permute_kernel,
         out_shape=jax.ShapeDtypeStruct(shape, jnp.float32),
-        in_specs=[pl.BlockSpec(memory_space=pltpu.VMEM)] * 2,
+        in_specs=[pl.BlockSpec(memory_space=pltpu.VMEM)] * (2 + len(updates)),
         out_specs=pl.BlockSpec(memory_space=pltpu.VMEM),
         scratch_shapes=[
             pltpu.VMEM(((tiles - gathered) * rows, 2 * LANES), jnp.bfloat16),
             pltpu.VMEM((rows, gathered * LANES), jnp.float32),
         ],
         name="permute",
-    )(values, order)
+    )(values, order, *updates)
 
 
 def cloud_kernel(wind_ref, gap_ref, push_ref, anomaly_ref, rain_ref):
@@ -226,9 +230,11 @@
 
 
 def contract_kernel(fourier_ref, coarse_ref, fine_ref, out_ref):
-    levels, slots, _, _ = out_ref.shape
+    levels, share, _, _ = out_ref.shape
     bands = fourier_ref.shape[0]
     terms = 2 * levels
+    slots = fourier_ref.shape[1] // terms
+    begin = pl.program_id(0) * share
     rows = -(-terms // 16) * 16
 
     def product(left, right):
@@ -239,7 +245,7 @@
     def contract(g, carry):
         for j in range(4):
             s = g * 4 + j
-            found = [fourier_ref[b, pl.ds(s, terms, stride=slots), :] for b in range(bands)]
+            found = [fourier_ref[b, pl.ds(begin + s, terms, stride=slots), :] for b in range(bands)]
             found = jnp.concatenate(found, axis=1)
             if rows > terms:
                 fill = jnp.zeros((rows - terms, found.shape[1]), jnp.float32)
@@ -251,7 +257,7 @@
                 out_ref[l, s] = total[2 * l : 2 * l + 2]
         return carry
 
-    lax.fori_loop(0, slots // 4, contract, 0)
+    lax.fori_loop(0, share // 4, contract, 0)
 
 
 def dft_kernel(x_ref, trig_ref, out_ref):
@@ -356,11 +362,15 @@
 
 def contract_tables(fourier, tables):
     bands, levels, _, slots, lanes = fourier.shape
+    step = 8
+    rows = levels * 2 * slots
+    table = pl.BlockSpec((step, MMAX, bands * lanes), lambda i: (i, 0, 0))
     return pl.pallas_call(
         contract_kernel,
+        grid=(slots // step,),
         out_shape=jax.ShapeDtypeStruct((levels, slots, 2, MMAX), jnp.float32),
-        in_specs=[pl.BlockSpec(memory_space=pltpu.VMEM)] * 3,
-        out_specs=pl.BlockSpec(memory_space=pltpu.VMEM),
+        in_specs=[pl.BlockSpec((bands, rows, lanes), lambda i: (0, 0, 0)), table, table],
+        out_specs=pl.BlockSpec((levels, step, 2, MMAX), lambda i: (0, i, 0, 0)),
         name="contract",
     )(fourier.reshape(bands, levels * 2 * slots, lanes), *tables)
 
@@ -408,22 +418,24 @@
     else:
         in_slots = permute(flat, slot_list[None, :], flat.shape)
         outgoing = in_slots.reshape(levels, targets, per_target).transpose(1, 0, 2)
-    crm_moisture, outgoing = lax.optimization_barrier((crm_moisture, outgoing))
+    crm_moisture, outgoing, own, force = lax.optimization_barrier(
+        (crm_moisture, outgoing, own, force)
+    )
+    share = jnp.where(
+        field < 2, own * (-1.0 / NSUB), jnp.where(field == 2, jnp.float32(1), jnp.float32(-1))
+    ).reshape(flat.shape)
+    base = (own + force).reshape(flat.shape)
     arrived = lax.all_to_all(outgoing, ("sec", "lat"), split_axis=0, concat_axis=0, tiled=True)
     homeward = cloud_model(arrived, crm_moisture[0, :, :, 0, 0, :], sections)
     returned = lax.all_to_all(homeward, ("sec", "lat"), split_axis=0, concat_axis=0, tiled=True)
     if not tiled:
         returned = returned.transpose(1, 0, 2).reshape(levels, block_cols)
-    rainfall = permute(returned, inverse_order(slot_list)[None, :], flat.shape)
-    rainfall = rainfall.reshape(levels, band_rows, lon_block)
-    share = jnp.where(
-        field < 2, own * (-1.0 / NSUB), jnp.where(field == 2, jnp.float32(1), jnp.float32(-1))
-    )
-    fresh = own + (share * rainfall + force)
+    fresh = permute(returned, inverse_order(slot_list)[None, :], flat.shape, (share, base))
+    fresh = fresh.reshape(levels, band_rows, lon_block)
 
     regrouped = lax.all_to_all(fresh, "col", split_axis=0, concat_axis=0, tiled=True)
     owner_count = MMAX // lat_bands
-    wave_table, _ = lax.optimization_barrier((wave_table, rainfall))
+    wave_table, _ = lax.optimization_barrier((wave_table, fresh))
     owned_waves = lax.dynamic_slice_in_dim(
         wave_table, lax.axis_index("lat") * owner_count, owner_count
     )

time: 180 us -> 180 us (level)
  local copies, waits for them, and re-layouts: 18.3 us -> 25.2 us
  other arithmetic: 18.5 us -> 14.2 us
  waiting for transfers between devices: 30.1 us -> 27.4 us
    all_to_all x1, waiting for transfers between devices: 6.16 us -> 1.69 us  [shards(): lax.all_to_all(homeward, ('sec', 'lat'), split_axis=0, concat_axis=0, til...]
    add x2 -> x1, other arithmetic: 5.62 us -> 1.33 us  [shards(): base = (own + force).reshape(flat.shape)]
    all_to_all x1, waiting for transfers between devices: 6.13 us -> 10.1 us  [shards(): lax.all_to_all(spectra, 'lat', split_axis=0, concat_axis=0, tiled=True)]
    unnamed x11 -> x21, local copies, waits for them, and re-layouts: 0.66 us -> 3.79 us
    reshape x2 -> x3, local copies, waits for them, and re-layouts: 5.8 us -> 7.94 us  [the longest x1 3.19 us: shards(): base = (own + force).reshape(flat.shape)]
    all_to_all x1, waiting for transfers between devices: 9.34 us -> 7.3 us  [shards(): lax.all_to_all(outgoing, ('sec', 'lat'), split_axis=0, concat_axis=0, til...]
  transfers between devices with their start and end apart: 5 -> 5, of which waited for: 4 -> 4; matrix products, arithmetic and copies ran while one was open for 16% -> 17% of each run, Pallas kernels for 11% -> 11%
where the time goes in v6:
time: 180 us; the launch traced here: 179 us
  Pallas kernels  82.3 us (46%)
  waiting for transfers between devices  27.4 us (15%)
  local copies, waits for them, and re-layouts  25.2 us (14%)
  starting transfers between devices  22.4 us (12%)
  other arithmetic  14.2 us (8%)
  matrix products  6.63 us (4%)
    pallas_call x2, Pallas kernels, permute(): pl.pallas_call(permute_kernel, out_shape=jax.ShapeDtypeStruct(shape, jnp....  34.4 us
    pallas_call x1, Pallas kernels, legendre_tables(): pl.pallas_call(march_kernel, out_shape=[table] * 2, in_specs=[pl.BlockSpe...  19.4 us
    pallas_call x1, Pallas kernels, cloud_model(): pl.pallas_call(cloud_kernel, grid=(bands * steps,), out_shape=jax.ShapeDt...  15.7 us
    all_to_all x1, waiting for transfers between devices, shards(): lax.all_to_all(spectra, 'lat', split_axis=0, concat_axis=0, tiled=True)  10.1 us
    pallas_call x1, Pallas kernels, contract_tables(): pl.pallas_call(contract_kernel, grid=(slots // step,), out_shape=jax.Shap...  8.78 us
    all_to_all x1, waiting for transfers between devices, shards(): lax.all_to_all(fresh, 'col', split_axis=0, concat_axis=0, tiled=True)  8.31 us
    all_to_all x1, starting transfers between devices, shards(): lax.all_to_all(outgoing, ('sec', 'lat'), split_axis=0, concat_axis=0, til...  7.56 us
    all_to_all x1, waiting for transfers between devices, shards(): lax.all_to_all(outgoing, ('sec', 'lat'), split_axis=0, concat_axis=0, til...  7.3 us
  transfers between devices with their start and end apart: 5, of which 4 were waited for; matrix products, arithmetic and copies ran while one was open for 17% of the time, Pallas kernels for 11%

profile of v6, /device:TPU:0, one launch (start us, length us, event | category | flops | bytes accessed | tf_op | source)
XLA Modules:
  0.0 178.9 jit_solution(16668763028662456915)
XLA Ops:
  0.6 0.0 copy-start.7
  0.7 0.0 copy-start.2
  0.7 3.1 %broadcast_select_fusion.1 = f32[28,96,96]{2,1,0:T(8,128)} fusion(pred[]{:T(512)S(6)} %eq.45, f32[1,1,28,96,96]{4,3,2,1,0:T(8,128)} %param.5, f32[1,1,28,96,96]{4,3,2,1,0:T(8,128)} %param.6), kind=kLoop, calls=%fused_computation.10 | loop fusion | flops 258048 | bytes 3096577 | tf_op jit(solution)/shard_map/jit(_where)/select_n | solution.py:409
  3.8 1.8 collective-permute-start
  5.6 0.7 add_select_fusion.1
  6.2 0.3 iota_compare_fusion.2
  6.6 0.1 fusion.11
  6.7 0.1 pad_maximum_fusion
  6.8 0.0 collective-permute-done
  6.8 2.8 %fusion.2 = f32[28,96,96]{2,1,0:T(8,128)} fusion(f32[28,96,96]{2,1,0:T(8,128)} %collective-permute-done, pred[]{:T(512)S(6)} %eq.45, pred[]{:T(512)S(6)} %eq.44, f32[1,1,28,96,96]{4,3,2,1,0:T(8,128)S(1)} %copy-done.1, f32[1,1,28,96,96]{4,3,2,1,0:T(8,128)S(1)} %copy-done.2), kind=kLoop, calls=%fused_computation.7 | loop fusion | flops 1290240 | bytes 4128770 | tf_op jit(solution)/shard_map/jit(_where)/select_n | solution.py:410
  9.6 3.2 %reshape.493.x_ref = f32[28,9216]{1,0:T(8,128)} reshape(f32[28,96,96]{2,1,0:T(8,128)} %fusion.2) | data formatting | bytes 2064384 | tf_op jit(solution)/shard_map/reshape | solution.py:413
  12.8 16.7 %permute.2 = f32[8,28,1152]{2,1,0:T(8,128)} custom-call(f32[28,9216]{1,0:T(8,128)} %reshape.493.x_ref, s32[1,9216]{1,0:T(1,128)} %bitcast.37), custom_call_target="tpu_custom_call" | custom-call | tf_op jit(solution)/shard_map/permute/pallas_call | solution.py:95
  29.5 7.6 %all-to-all-start = ((f32[8,28,1152]{2,1,0:T(8,128)}), f32[8,28,1152]{2,1,0:T(8,128)S(1)}, u32[]{:S(2)}, u32[]{:S(2)}) async-start(f32[8,28,1152]{2,1,0:T(8,128)} %permute.2), calls=%async_computation | async-start | bytes 2359296 | tf_op jit(solution)/shard_map/all_to_all | solution.py:428
  37.1 2.0 %broadcast_select_fusion = bf16[2,72,9216]{2,1,0:T(8,128)(2,1)} fusion(pred[72,9216]{1,0:T(8,128)(4,1)S(1)} %iota_compare_fusion.2, bf16[2,9216]{1,0:T(2,128)(2,1)S(1)} %pad_maximum_fusion), kind=kLoop, calls=%fused_computation.4 | loop fusion | flops 1327104 | bytes 3354624 | tf_op jit(solution)/shard_map/jit(_where)/select_n | solution.py:392
  39.1 6.6 %copy.11 = bf16[1,32,28,1,1,2304]{5,2,1,4,3,0:T(8,128)(2,1)} copy(bf16[1,32,28,1,1,2304]{5,1,4,3,2,0:T(8,128)(2,1)} %param.7) | data formatting | bytes 8257536 | tf_op jit(solution)/shard_map/optimization_barrier | solution.py:421
  45.7 7.3 %all-to-all-done.wind_ref.gap_ref.push_ref = f32[8,28,1152]{2,1,0:T(8,128)S(1)} async-done(((f32[8,28,1152]{2,1,0:T(8,128)}), f32[8,28,1152]{2,1,0:T(8,128)S(1)}, u32[]{:S(2)}, u32[]{:S(2)}) %all-to-all-start) | async-done | bytes 1032224 | tf_op jit(solution)/shard_map/all_to_all | solution.py:428
  53.0 1.0 copy-done
  54.0 15.7 %cloud.1 = f32[4,2,28,1152]{3,2,1,0:T(8,128)} custom-call(f32[8,28,1152]{2,1,0:T(8,128)} %copy-done, f32[8,28,1152]{2,1,0:T(8,128)} %copy-done, f32[8,28,1152]{2,1,0:T(8,128)} %copy-done, bf16[32,28,2304]{2,1,0:T(8,128)(2,1)} %bitcast.26), custom_call_target="tpu_custom_call" | custom-call | tf_op jit(solution)/shard_map/cloud/pallas_call | solution.py:164
  69.7 4.4 %all-to-all-start.1 = ((f32[8,28,1152]{2,1,0:T(8,128)}), f32[8,28,1152]{2,1,0:T(8,128)}, u32[]{:S(2)}, u32[]{:S(2)}) async-start(f32[8,28,1152]{2,1,0:T(8,128)} %bitcast.30), calls=%async_computation.1 | async-start | bytes 2359296 | tf_op jit(solution)/shard_map/all_to_all | solution.py:430
  74.1 0.6 pad.8
  74.7 6.6 %fusion.3 = s32[144,128]{1,0:T(8,128)S(1)} fusion(bf16[144,9216]{1,0:T(8,128)(2,1)} %bitcast.32, s32[9216]{0:T(1024)S(1)} %copy-done.8), kind=kOutput, calls=%fused_computation.9 | convolution fusion | flops 340936704 | bytes 2764800 | tf_op jit(solution)/shard_map/dot_general | solution.py:393
  81.4 0.6 slice_add_fusion
  82.0 1.3 fusion.27
  83.3 3.2 %reshape.496.refs_1_ = f32[28,9216]{1,0:T(8,128)} reshape(f32[28,96,96]{2,1,0:T(8,128)} %get-tuple-element.24) | data formatting | bytes 2064384 | tf_op jit(solution)/shard_map/reshape | solution.py:427
  86.5 1.8 %reshape.495.refs_0_ = f32[28,9216]{1,0:T(8,128)} reshape(f32[28,96,96]{2,1,0:T(8,128)S(1)} %get-tuple-element.25) | data formatting | bytes 2064384 | tf_op jit(solution)/shard_map/reshape | solution.py:426
  88.4 1.7 all-to-all-done.1.x_ref
  90.0 17.7 %permute.3 = f32[28,9216]{1,0:T(8,128)} custom-call(f32[8,28,1152]{2,1,0:T(8,128)} %all-to-all-done.1.x_ref, s32[1,9216]{1,0:T(1,128)} %bitcast.39, f32[28,9216]{1,0:T(8,128)} %reshape.495.refs_0_, f32[28,9216]{1,0:T(8,128)} %reshape.496.refs_1_), custom_call_target="tpu_custom_call" | custom-call | tf_op jit(solution)/shard_map/permute/pallas_call | solution.py:95
  107.8 2.9 %reshape.497 = f32[28,96,96]{2,1,0:T(8,128)} reshape(f32[28,9216]{1,0:T(8,128)} %permute.3) | data formatting | bytes 2064384 | tf_op jit(solution)/shard_map/reshape | solution.py:434
  110.7 5.0 %all-to-all-start.2 = ((f32[28,96,96]{2,1,0:T(8,128)}), f32[28,96,96]{2,1,0:T(8,128)S(1)}, u32[]{:S(2)}, u32[]{:S(2)}) async-start(f32[28,96,96]{2,1,0:T(8,128)} %reshape.497), calls=%async_computation.2 | async-start | bytes 2752512 | tf_op jit(solution)/shard_map/all_to_all | solution.py:436
  115.7 0.1 broadcast_multiply_fusion
  115.8 0.1 mul.205
  115.8 0.1 subtract_multiply_fusion
  116.0 0.2 exponential_multiply_fusion
  116.3 0.6 copy.12
  116.9 0.7 divide_sqrt_fusion
  117.6 0.7 broadcast_in_dim.70.order_ref
  118.3 0.6 broadcast_in_dim.71.zero_ref
  118.9 19.4 %march.1 = (bf16[64,128,256]{2,1,0:T(8,128)(2,1)}, bf16[64,128,256]{2,1,0:T(8,128)(2,1)}) custom-call(f32[64,128]{1,0:T(8,128)} %get-tuple-element.31.grow_ref, f32[64,128]{1,0:T(8,128)} %get-tuple-element.30.retreat_ref, s32[64,128]{1,0:T(8,128)} %broadcast_in_dim.70.order_ref, s32[64,128]{1,0:T(8,128)} %broadcast_in_dim.71.zero_ref, f32[1,256]{1,0:T(1,128)} %bitcast.40, ...), custom_call_target="tpu_custom_call" | custom-call | flops 12582912 | bytes 33554432 | tf_op jit(solution)/shard_map/march/pallas_call | solution.py:343
  138.3 1.1 fusion.9
  139.4 0.9 maximum_multiply_fusion
  140.3 8.3 %all-to-all-done.2 = f32[28,96,96]{2,1,0:T(8,128)S(1)} async-done(((f32[28,96,96]{2,1,0:T(8,128)}), f32[28,96,96]{2,1,0:T(8,128)S(1)}, u32[]{:S(2)}, u32[]{:S(2)}) %all-to-all-start.2) | async-done | bytes 1032224 | tf_op jit(solution)/shard_map/all_to_all | solution.py:436
  148.6 1.1 copy-done.5
  149.7 4.0 %dft.1 = f32[2,7,2,64,128]{4,3,2,1,0:T(8,128)} custom-call(f32[4,7,96,96]{3,2,1,0:T(8,128)} %bitcast.29, f32[4,256,96]{2,1,0:T(8,128)} %bitcast.33), custom_call_target="tpu_custom_call" | custom-call | tf_op jit(solution)/shard_map/dft/pallas_call | solution.py:304
  153.7 3.7 %all-to-all-start.3 = ((f32[2,7,2,64,128]{4,3,2,1,0:T(8,128)}), f32[2,7,2,64,128]{4,3,2,1,0:T(8,128)S(1)}, u32[]{:S(2)}, u32[]{:S(2)}) async-start(f32[2,7,2,64,128]{4,3,2,1,0:T(8,128)} %dft.1), calls=%async_computation.3 | async-start | bytes 1835008 | tf_op jit(solution)/shard_map/all_to_all | solution.py:445
  157.4 1.6 broadcast_in_dim_reshape.3
  159.0 10.1 %all-to-all-done.3 = f32[2,7,2,64,128]{4,3,2,1,0:T(8,128)S(1)} async-done(((f32[2,7,2,64,128]{4,3,2,1,0:T(8,128)}), f32[2,7,2,64,128]{4,3,2,1,0:T(8,128)S(1)}, u32[]{:S(2)}, u32[]{:S(2)}) %all-to-all-start.3) | async-done | bytes 917536 | tf_op jit(solution)/shard_map/all_to_all | solution.py:445
  169.1 1.0 copy-done.6
  170.2 8.8 %contract.1 = f32[7,64,2,128]{3,2,1,0:T(2,128)} custom-call(f32[2,896,128]{2,1,0:T(8,128)} %bitcast.31, bf16[64,128,256]{2,1,0:T(8,128)(2,1)} %get-tuple-element.20.coarse_ref, bf16[64,128,256]{2,1,0:T(8,128)(2,1)} %get-tuple-element.21.fine_ref), custom_call_target="tpu_custom_call" | custom-call | tf_op jit(solution)/shard_map/contract/pallas_call | solution.py:368
  (23 shorter events, 0.1 us)
Async XLA Ops:
  0.6 5.0 %copy-start.7 = (s32[1,1,9216]{2,1,0:T(1,128)S(1)}, s32[1,1,9216]{2,1,0:T(1,128)}, u32[]{:S(2)}) copy-start(s32[1,1,9216]{2,1,0:T(1,128)} %param.8) | copy-start | bytes 110596
  0.6 6.1 %copy-start.1 = (f32[1,1,28,96,96]{4,3,2,1,0:T(8,128)S(1)}, f32[1,1,28,96,96]{4,3,2,1,0:T(8,128)}, u32[]{:S(2)}) copy-start(f32[1,1,28,96,96]{4,3,2,1,0:T(8,128)} %param.5) | copy-start | bytes 3096580
  0.7 6.1 %copy-start.2 = (f32[1,1,28,96,96]{4,3,2,1,0:T(8,128)S(1)}, f32[1,1,28,96,96]{4,3,2,1,0:T(8,128)}, u32[]{:S(2)}) copy-start(f32[1,1,28,96,96]{4,3,2,1,0:T(8,128)} %param.6) | copy-start | bytes 3096580
  3.8 3.0 %collective-permute-start = (f32[28,96,96]{2,1,0:T(8,128)}, f32[28,96,96]{2,1,0:T(8,128)}, u32[]{:S(2)}, u32[]{:S(2)}) collective-permute-start(f32[28,96,96]{2,1,0:T(8,128)} %broadcast_select_fusion.1), channel_id=1, source_target_pairs={{16,24},{24,16},{17,25},{25,17},{18,26},{26,18},{19,27},{27,19},{2... | collective-permute-start | bytes 3096584 | tf_op jit(solution)/shard_map/ppermute | solution.py:409
  29.5 23.5 %all-to-all-start = ((f32[8,28,1152]{2,1,0:T(8,128)}), f32[8,28,1152]{2,1,0:T(8,128)S(1)}, u32[]{:S(2)}, u32[]{:S(2)}) async-start(f32[8,28,1152]{2,1,0:T(8,128)} %permute.2), calls=%async_computation | async-start | bytes 2359296 | tf_op jit(solution)/shard_map/all_to_all | solution.py:428
  53.0 1.0 copy-start
  69.7 5.0 %copy-start.8 = (s32[9216]{0:T(1024)S(1)}, s32[9216]{0:T(1024)}, u32[]{:S(2)}) copy-start(s32[9216]{0:T(1024)} %get-tuple-element.26) | copy-start | bytes 110596
  69.7 20.3 %all-to-all-start.1 = ((f32[8,28,1152]{2,1,0:T(8,128)}), f32[8,28,1152]{2,1,0:T(8,128)}, u32[]{:S(2)}, u32[]{:S(2)}) async-start(f32[8,28,1152]{2,1,0:T(8,128)} %bitcast.30), calls=%async_computation.1 | async-start | bytes 2359296 | tf_op jit(solution)/shard_map/all_to_all | solution.py:430
  74.7 7.3 %copy-start.3 = (f32[1,1,28,96,96]{4,3,2,1,0:T(8,128)S(1)}, f32[1,1,28,96,96]{4,3,2,1,0:T(8,128)}, u32[]{:S(2)}) copy-start(f32[1,1,28,96,96]{4,3,2,1,0:T(8,128)} %param.6) | copy-start | bytes 3096580
  110.7 5.1 %copy-start.9 = (s32[128]{0:T(128)S(1)}, s32[128]{0:T(128)}, u32[]{:S(2)}) copy-start(s32[128]{0:T(128)} %param.9) | copy-start | bytes 1540
  110.7 37.9 %all-to-all-start.2 = ((f32[28,96,96]{2,1,0:T(8,128)}), f32[28,96,96]{2,1,0:T(8,128)S(1)}, u32[]{:S(2)}, u32[]{:S(2)}) async-start(f32[28,96,96]{2,1,0:T(8,128)} %reshape.497), calls=%async_computation.2 | async-start | bytes 2752512 | tf_op jit(solution)/shard_map/all_to_all | solution.py:436
  148.6 1.1 copy-start.5
  153.7 3.7 %copy-start.4 = (f32[28,9216]{1,0:T(8,128)S(1)}, f32[28,9216]{1,0:T(8,128)}, u32[]{:S(2)}) copy-start(f32[28,9216]{1,0:T(8,128)} %permute.3) | copy-start | bytes 3096580
  153.7 15.4 %all-to-all-start.3 = ((f32[2,7,2,64,128]{4,3,2,1,0:T(8,128)}), f32[2,7,2,64,128]{4,3,2,1,0:T(8,128)S(1)}, u32[]{:S(2)}, u32[]{:S(2)}) async-start(f32[2,7,2,64,128]{4,3,2,1,0:T(8,128)} %dft.1), calls=%async_computation.3 | async-start | bytes 1835008 | tf_op jit(solution)/shard_map/all_to_all | solution.py:445
  169.1 1.0 copy-start.6

commit v7 on v5

--- a/solution.py
+++ b/solution.py
@@ -87,7 +87,7 @@
 def permute(values, order, shape):
     levels, tiles = values.shape[-2], order.shape[1] // LANES
     rows = -(-levels // ROWS) * ROWS
-    gathered = tiles * 3 // 8
+    gathered = tiles * 7 // 16
     return pl.pallas_call(
         permute_kernel,
         out_shape=jax.ShapeDtypeStruct(shape, jnp.float32),

time: 180 us -> 180 us (level)
  no operation moved by 1% of the time
where the time goes in v7:
time: 180 us; the launch traced here: 179 us
  Pallas kernels  81.4 us (45%)
  waiting for transfers between devices  30.1 us (17%)
  starting transfers between devices  23.1 us (13%)
  other arithmetic  18.5 us (10%)
  local copies, waits for them, and re-layouts  18.3 us (10%)
  matrix products  6.52 us (4%)
    pallas_call x2, Pallas kernels, permute(): pl.pallas_call(permute_kernel, out_shape=jax.ShapeDtypeStruct(shape, jnp....  33.6 us
    pallas_call x1, Pallas kernels, legendre_tables(): pl.pallas_call(march_kernel, out_shape=[table] * 2, in_specs=[pl.BlockSpe...  19.3 us
    pallas_call x1, Pallas kernels, cloud_model(): pl.pallas_call(cloud_kernel, grid=(bands * steps,), out_shape=jax.ShapeDt...  15.7 us
    all_to_all x1, waiting for transfers between devices, shards(): lax.all_to_all(outgoing, ('sec', 'lat'), split_axis=0, concat_axis=0, til...  9.34 us
    pallas_call x1, Pallas kernels, contract_tables(): pl.pallas_call(contract_kernel, out_shape=jax.ShapeDtypeStruct((levels, s...  8.82 us
    all_to_all x1, waiting for transfers between devices, shards(): lax.all_to_all(fresh, 'col', split_axis=0, concat_axis=0, tiled=True)  8.44 us
    all_to_all x1, starting transfers between devices, shards(): lax.all_to_all(outgoing, ('sec', 'lat'), split_axis=0, concat_axis=0, til...  7.71 us
    optimization_barrier x1, local copies, waits for them, and re-layouts, shards(): crm_moisture, outgoing = lax.optimization_barrier((crm_moisture, outgoing))  6.6 us
  transfers between devices with their start and end apart: 5, of which 4 were waited for; matrix products, arithmetic and copies ran while one was open for 16% of the time, Pallas kernels for 11%

profile of v7, /device:TPU:0, one launch (start us, length us, event | category | flops | bytes accessed | tf_op | source)
XLA Modules:
  0.0 178.6 jit_solution(169072222602159466)
XLA Ops:
  0.6 0.0 copy-start.2
  0.6 0.0 copy-start
  0.7 0.0 copy-start.1
  0.7 3.1 %bitcast_select_fusion = f32[28,96,96]{2,1,0:T(8,128)} fusion(f32[1,1,28,96,96]{4,3,2,1,0:T(8,128)} %param.5, f32[1,1,28,96,96]{4,3,2,1,0:T(8,128)} %param.6, pred[]{:T(512)S(6)} %eq.44), kind=kLoop, calls=%fused_computation.10 | loop fusion | flops 258048 | bytes 3096577 | tf_op jit(solution)/shard_map/jit(_where)/select_n | solution.py:399
  3.8 1.8 collective-permute-start
  5.6 0.0 copy-done.2
  5.6 0.7 add_select_fusion.1
  6.2 0.3 iota_compare_fusion.2
  6.6 0.1 fusion.15
  6.7 0.0 collective-permute-done
  6.7 0.0 copy-done
  6.7 0.0 copy-done.1
  6.7 2.8 %fusion.2 = f32[28,96,96]{2,1,0:T(8,128)} fusion(f32[28,96,96]{2,1,0:T(8,128)} %collective-permute-done, f32[1,1,28,96,96]{4,3,2,1,0:T(8,128)S(1)} %copy-done, f32[1,1,28,96,96]{4,3,2,1,0:T(8,128)S(1)} %copy-done.1, pred[]{:T(512)S(6)} %eq.44, pred[]{:T(512)S(6)} %eq.45), kind=kLoop, calls=%fused_computation.7 | loop fusion | flops 1290240 | bytes 4128770 | tf_op jit(solution)/shard_map/jit(_where)/select_n | solution.py:400
  9.5 3.2 %reshape.490.x_ref = f32[28,9216]{1,0:T(8,128)} reshape(f32[28,96,96]{2,1,0:T(8,128)} %fusion.2) | data formatting | bytes 2064384 | tf_op jit(solution)/shard_map/reshape | solution.py:403
  12.7 16.9 %permute.2 = f32[8,28,1152]{2,1,0:T(8,128)} custom-call(f32[28,9216]{1,0:T(8,128)} %reshape.490.x_ref, s32[1,9216]{1,0:T(1,128)} %bitcast.48), custom_call_target="tpu_custom_call" | custom-call | tf_op jit(solution)/shard_map/permute/pallas_call | solution.py:91
  29.6 7.7 %all-to-all-start = ((f32[8,28,1152]{2,1,0:T(8,128)}), f32[8,28,1152]{2,1,0:T(8,128)}, u32[]{:S(2)}, u32[]{:S(2)}) async-start(f32[8,28,1152]{2,1,0:T(8,128)} %permute.2), calls=%async_computation | async-start | bytes 2359296 | tf_op jit(solution)/shard_map/all_to_all | solution.py:412
  37.3 0.1 pad_maximum_fusion
  37.4 6.6 %copy.11 = bf16[1,32,28,1,1,2304]{5,2,1,4,3,0:T(8,128)(2,1)} copy(bf16[1,32,28,1,1,2304]{5,1,4,3,2,0:T(8,128)(2,1)} %param.7) | data formatting | bytes 8257536 | tf_op jit(solution)/shard_map/optimization_barrier | solution.py:411
  44.0 9.3 %all-to-all-done.wind_ref.gap_ref.push_ref = f32[8,28,1152]{2,1,0:T(8,128)} async-done(((f32[8,28,1152]{2,1,0:T(8,128)}), f32[8,28,1152]{2,1,0:T(8,128)}, u32[]{:S(2)}, u32[]{:S(2)}) %all-to-all-start) | async-done | bytes 1032224 | tf_op jit(solution)/shard_map/all_to_all | solution.py:412
  53.3 15.7 %cloud.1 = f32[4,2,28,1152]{3,2,1,0:T(8,128)} custom-call(f32[8,28,1152]{2,1,0:T(8,128)} %all-to-all-done.wind_ref.gap_ref.push_ref, f32[8,28,1152]{2,1,0:T(8,128)} %all-to-all-done.wind_ref.gap_ref.push_ref, f32[8,28,1152]{2,1,0:T(8,128)} %all-to-all-done.wind_ref.gap_ref.push_ref, bf16[32,28,2304]{2,1,0:T(8,128)(2,1)} %bitcast.41), custom_call_target="tpu_custom_call" | custom-call | tf_op jit(solution)/shard_map/cloud/pallas_call | solution.py:160
  69.0 4.3 %all-to-all-start.1 = ((f32[8,28,1152]{2,1,0:T(8,128)}), f32[8,28,1152]{2,1,0:T(8,128)}, u32[]{:S(2)}, u32[]{:S(2)}) async-start(f32[8,28,1152]{2,1,0:T(8,128)} %bitcast.42), calls=%async_computation.1 | async-start | bytes 2359296 | tf_op jit(solution)/shard_map/all_to_all | solution.py:414
  73.2 0.0 copy-start.3
  73.3 2.0 %broadcast_select_fusion = bf16[2,72,9216]{2,1,0:T(8,128)(2,1)} fusion(pred[72,9216]{1,0:T(8,128)(4,1)S(1)} %iota_compare_fusion.2, bf16[2,9216]{1,0:T(2,128)(2,1)S(1)} %pad_maximum_fusion), kind=kLoop, calls=%fused_computation.4 | loop fusion | flops 1327104 | bytes 3354624 | tf_op jit(solution)/shard_map/jit(_where)/select_n | solution.py:382
  75.3 0.6 pad.8
  75.9 6.5 %fusion.7 = s32[144,128]{1,0:T(8,128)S(1)} fusion(bf16[144,9216]{1,0:T(8,128)(2,1)} %bitcast.43, s32[9216]{0:T(1024)S(1)} %copy-done.3), kind=kOutput, calls=%fused_computation.17 | convolution fusion | flops 340936704 | bytes 2764800 | tf_op jit(solution)/shard_map/dot_general | solution.py:383
  82.4 0.6 slice_add_fusion
  83.0 6.2 %all-to-all-done.1.x_ref = f32[8,28,1152]{2,1,0:T(8,128)} async-done(((f32[8,28,1152]{2,1,0:T(8,128)}), f32[8,28,1152]{2,1,0:T(8,128)}, u32[]{:S(2)}, u32[]{:S(2)}) %all-to-all-start.1) | async-done | bytes 1032224 | tf_op jit(solution)/shard_map/all_to_all | solution.py:414
  89.2 16.7 %permute.3 = f32[28,9216]{1,0:T(8,128)} custom-call(f32[8,28,1152]{2,1,0:T(8,128)} %all-to-all-done.1.x_ref, s32[1,9216]{1,0:T(1,128)} %bitcast.50), custom_call_target="tpu_custom_call" | custom-call | tf_op jit(solution)/shard_map/permute/pallas_call | solution.py:91
  105.9 2.9 %reshape.493 = f32[28,96,96]{2,1,0:T(8,128)} reshape(f32[28,9216]{1,0:T(8,128)} %permute.3) | data formatting | bytes 2064384 | tf_op jit(solution)/shard_map/reshape | solution.py:418
  108.8 2.8 %bitcast_add_fusion = f32[28,96,96]{2,1,0:T(8,128)} fusion(f32[1,1,28,96,96]{4,3,2,1,0:T(8,128)S(1)} %copy-done, f32[28,96,96]{2,1,0:T(8,128)} %reshape.493, f32[1,1,28,96,96]{4,3,2,1,0:T(8,128)S(1)} %copy-done.1, f32[]{:T(128)S(6)} %select_n.125, pred[]{:T(512)S(6)} %lt.24), kind=kLoop, calls=%fused_computation.9 | loop fusion | flops 1290240 | bytes 4128773 | tf_op jit(solution)/shard_map/add | solution.py:422
  111.6 4.9 %all-to-all-start.2 = ((f32[28,96,96]{2,1,0:T(8,128)}), f32[28,96,96]{2,1,0:T(8,128)}, u32[]{:S(2)}, u32[]{:S(2)}) async-start(f32[28,96,96]{2,1,0:T(8,128)} %bitcast_add_fusion), calls=%async_computation.2 | async-start | bytes 2752512 | tf_op jit(solution)/shard_map/all_to_all | solution.py:424
  116.6 0.1 mul.220
  116.7 0.1 subtract_multiply_fusion
  116.8 0.2 exponential_multiply_fusion
  117.1 0.6 copy.12
  117.7 0.7 divide_sqrt_fusion
  118.5 0.7 broadcast_in_dim.74.order_ref
  119.1 0.6 broadcast_in_dim.75.zero_ref
  119.7 19.3 %march.1 = (bf16[64,128,256]{2,1,0:T(8,128)(2,1)}, bf16[64,128,256]{2,1,0:T(8,128)(2,1)}) custom-call(f32[64,128]{1,0:T(8,128)} %get-tuple-element.25.grow_ref, f32[64,128]{1,0:T(8,128)} %get-tuple-element.24.retreat_ref, s32[64,128]{1,0:T(8,128)} %broadcast_in_dim.74.order_ref, s32[64,128]{1,0:T(8,128)} %broadcast_in_dim.75.zero_ref, f32[1,256]{1,0:T(1,128)} %bitcast.51, ...), custom_call_target="tpu_custom_call" | custom-call | flops 12582912 | bytes 33554432 | tf_op jit(solution)/shard_map/march/pallas_call | solution.py:337
  139.1 1.1 fusion.13
  140.2 0.9 maximum_multiply_fusion
  141.1 8.4 %all-to-all-done.2 = f32[28,96,96]{2,1,0:T(8,128)} async-done(((f32[28,96,96]{2,1,0:T(8,128)}), f32[28,96,96]{2,1,0:T(8,128)}, u32[]{:S(2)}, u32[]{:S(2)}) %all-to-all-start.2) | async-done | bytes 1032224 | tf_op jit(solution)/shard_map/all_to_all | solution.py:424
  149.5 4.0 %dft.1 = f32[2,7,2,64,128]{4,3,2,1,0:T(8,128)} custom-call(f32[4,7,96,96]{3,2,1,0:T(8,128)} %bitcast.9.x_ref, f32[4,256,96]{2,1,0:T(8,128)} %bitcast.44), custom_call_target="tpu_custom_call" | custom-call | tf_op jit(solution)/shard_map/dft/pallas_call | solution.py:298
  153.5 4.4 %all-to-all-start.3 = ((f32[2,7,2,64,128]{4,3,2,1,0:T(8,128)}), f32[2,7,2,64,128]{4,3,2,1,0:T(8,128)}, u32[]{:S(2)}, u32[]{:S(2)}) async-start(f32[2,7,2,64,128]{4,3,2,1,0:T(8,128)} %dft.1), calls=%async_computation.3 | async-start | bytes 1835008 | tf_op jit(solution)/shard_map/all_to_all | solution.py:433
  157.9 2.9 %reshape.492 = f32[1,1,28,96,96]{4,3,2,1,0:T(8,128)} reshape(f32[28,9216]{1,0:T(8,128)} %permute.3) | data formatting | bytes 2064384 | tf_op jit(solution)/shard_map/reshape | solution.py:418
  160.8 2.8 %add_add_fusion = f32[1,1,28,96,96]{4,3,2,1,0:T(8,128)} fusion(f32[1,1,28,96,96]{4,3,2,1,0:T(8,128)S(1)} %copy-done, f32[1,1,28,96,96]{4,3,2,1,0:T(8,128)S(1)} %copy-done.1, f32[1,1,28,96,96]{4,3,2,1,0:T(8,128)} %reshape.492, f32[]{:T(128)S(6)} %select_n.125, pred[]{:T(512)S(6)} %lt.24), kind=kLoop, calls=%fused_computation.16 | loop fusion | flops 1290240 | bytes 4128773 | tf_op jit(solution)/shard_map/add | solution.py:422
  163.6 6.1 %all-to-all-done.3 = f32[2,7,2,64,128]{4,3,2,1,0:T(8,128)} async-done(((f32[2,7,2,64,128]{4,3,2,1,0:T(8,128)}), f32[2,7,2,64,128]{4,3,2,1,0:T(8,128)}, u32[]{:S(2)}, u32[]{:S(2)}) %all-to-all-start.3) | async-done | bytes 917536 | tf_op jit(solution)/shard_map/all_to_all | solution.py:433
  169.8 8.8 %contract.1 = f32[7,64,2,128]{3,2,1,0:T(2,128)} custom-call(f32[2,896,128]{2,1,0:T(8,128)} %bitcast.12.fourier_ref, bf16[64,128,256]{2,1,0:T(8,128)(2,1)} %get-tuple-element.16.coarse_ref, bf16[64,128,256]{2,1,0:T(8,128)(2,1)} %get-tuple-element.17.fine_ref), custom_call_target="tpu_custom_call" | custom-call | tf_op jit(solution)/shard_map/contract/pallas_call | solution.py:359
  (12 shorter events, 0.2 us)
Async XLA Ops:
  0.6 4.9 %copy-start.2 = (s32[1,1,9216]{2,1,0:T(1,128)S(1)}, s32[1,1,9216]{2,1,0:T(1,128)}, u32[]{:S(2)}) copy-start(s32[1,1,9216]{2,1,0:T(1,128)} %param.8) | copy-start | bytes 110596
  0.6 6.0 %copy-start = (f32[1,1,28,96,96]{4,3,2,1,0:T(8,128)S(1)}, f32[1,1,28,96,96]{4,3,2,1,0:T(8,128)}, u32[]{:S(2)}) copy-start(f32[1,1,28,96,96]{4,3,2,1,0:T(8,128)} %param.5) | copy-start | bytes 3096580
  0.7 6.0 %copy-start.1 = (f32[1,1,28,96,96]{4,3,2,1,0:T(8,128)S(1)}, f32[1,1,28,96,96]{4,3,2,1,0:T(8,128)}, u32[]{:S(2)}) copy-start(f32[1,1,28,96,96]{4,3,2,1,0:T(8,128)} %param.6) | copy-start | bytes 3096580
  3.8 2.9 %collective-permute-start = (f32[28,96,96]{2,1,0:T(8,128)}, f32[28,96,96]{2,1,0:T(8,128)}, u32[]{:S(2)}, u32[]{:S(2)}) collective-permute-start(f32[28,96,96]{2,1,0:T(8,128)} %bitcast_select_fusion), channel_id=1, source_target_pairs={{16,24},{24,16},{17,25},{25,17},{18,26},{26,18},{19,27},{27,19},{2... | collective-permute-start | bytes 3096584 | tf_op jit(solution)/shard_map/ppermute | solution.py:399
  29.6 23.7 %all-to-all-start = ((f32[8,28,1152]{2,1,0:T(8,128)}), f32[8,28,1152]{2,1,0:T(8,128)}, u32[]{:S(2)}, u32[]{:S(2)}) async-start(f32[8,28,1152]{2,1,0:T(8,128)} %permute.2), calls=%async_computation | async-start | bytes 2359296 | tf_op jit(solution)/shard_map/all_to_all | solution.py:412
  69.0 20.2 %all-to-all-start.1 = ((f32[8,28,1152]{2,1,0:T(8,128)}), f32[8,28,1152]{2,1,0:T(8,128)}, u32[]{:S(2)}, u32[]{:S(2)}) async-start(f32[8,28,1152]{2,1,0:T(8,128)} %bitcast.42), calls=%async_computation.1 | async-start | bytes 2359296 | tf_op jit(solution)/shard_map/all_to_all | solution.py:414
  73.2 2.6 %copy-start.3 = (s32[9216]{0:T(1024)S(1)}, s32[9216]{0:T(1024)}, u32[]{:S(2)}) copy-start(s32[9216]{0:T(1024)} %get-tuple-element.20) | copy-start | bytes 110596
  111.6 5.0 %copy-start.4 = (s32[128]{0:T(128)S(1)}, s32[128]{0:T(128)}, u32[]{:S(2)}) copy-start(s32[128]{0:T(128)} %param.9) | copy-start | bytes 1540
  111.6 38.0 %all-to-all-start.2 = ((f32[28,96,96]{2,1,0:T(8,128)}), f32[28,96,96]{2,1,0:T(8,128)}, u32[]{:S(2)}, u32[]{:S(2)}) async-start(f32[28,96,96]{2,1,0:T(8,128)} %bitcast_add_fusion), calls=%async_computation.2 | async-start | bytes 2752512 | tf_op jit(solution)/shard_map/all_to_all | solution.py:424
  153.5 16.2 %all-to-all-start.3 = ((f32[2,7,2,64,128]{4,3,2,1,0:T(8,128)}), f32[2,7,2,64,128]{4,3,2,1,0:T(8,128)}, u32[]{:S(2)}, u32[]{:S(2)}) async-start(f32[2,7,2,64,128]{4,3,2,1,0:T(8,128)} %dft.1), calls=%async_computation.3 | async-start | bytes 1835008 | tf_op jit(solution)/shard_map/all_to_all | solution.py:433
